TPU v7x, 512 devices: a whole 4x4x16 slice. The times are simulated.
512 devices in a mesh: dp: 32 (over y, x, core), mp: 16 (over z).
Axes of the slice: x: 4, y: 4, z: 16, core: 2. Of those that a mesh axis runs over, the one named last changes fastest.
Arguments:
- tokens: bfloat16 [32768, 8192], P('dp', 'mp'), may hold values from -6 to 6
- value_weight: bfloat16 [8192, 1024], P('mp'), may hold values from -0.0625 to 0.0625
- down_panels: bfloat16 [256, 8192, 64], P('dp', 'mp'), may hold values from -0.0625 to 0.0625
- up_panels: bfloat16 [256, 64, 1024], P('dp'), may hold values from -0.75 to 0.75
- cotangent: bfloat16 [32768, 1024], P(('dp', 'mp')), may hold values from -6 to 6
- block_adapter: int32 [256], replicated, may hold values from 0 to 255, as said below
- adapter_slot: int32 [256], replicated, may hold values from 0 to 255, as said below
Outputs:
- projected: bfloat16 [32768, 1024], P(('dp', 'mp'))
- grad_tokens: bfloat16 [32768, 8192], P('dp', 'mp')
- grad_down: bfloat16 [256, 8192, 64], P('dp', 'mp')
- grad_up: bfloat16 [256, 64, 1024], P('dp')
Inputs may be any that keep to these rules, and one draw needn't show every extreme that they name: `block_adapter`: the 8 blocks of one index of dp name adapters stored on 8 different owners, the owner of slot s being s // 8. `adapter_slot`: A permutation of the adapters.
All inputs are finite; a program needn't handle non-finite values.
Results may differ from a plain program's by a relative error of at most 0.005.
Values may be sent and summed in bfloat16 or wider, within the bound.
A program may use at most 128 MiB of HBM per device.

v0:
```python
import jax
import jax.numpy as jnp
from jax import lax
from jax.sharding import PartitionSpec as P

RANK = 64
BLOCK_ROWS = 128


def per_device(
    tokens, value_weight, down_panels, up_panels, cotangent, block_adapter, adapter_slot
):
    n_owners = lax.axis_size("dp")
    myself = lax.axis_index("dp")
    n_split = lax.axis_size("mp")
    my_part = lax.axis_index("mp")
    rows, width_dev = tokens.shape
    own_rows, kv_full = cotangent.shape
    kv_part = kv_full // n_split
    stored = down_panels.shape[0]
    blocks = rows // BLOCK_ROWS
    group = min(own_rows, BLOCK_ROWS)
    groups = own_rows // group
    highest = lax.Precision.HIGHEST
    hits = block_adapter[:, None] == jnp.arange(adapter_slot.shape[0], dtype=jnp.int32)[None, :]
    slots_all = jnp.sum(jnp.where(hits, adapter_slot[None, :], 0), axis=1)
    owner_all = (slots_all // stored).reshape(n_owners, blocks)
    local_all = (slots_all % stored).reshape(n_owners, blocks)
    mine = owner_all == myself
    wanted = jnp.sum(jnp.where(mine, local_all, 0), axis=1)
    served = jnp.any(mine, axis=1)
    pick_mask = (wanted[:, None] == jnp.arange(stored, dtype=jnp.int32)[None, :]) & served[:, None]
    pick_bf = pick_mask.astype(jnp.bfloat16)
    my_owner = lax.dynamic_index_in_dim(owner_all, myself, 0, keepdims=False)
    select_mask = my_owner[:, None] == jnp.arange(n_owners, dtype=jnp.int32)[None, :]
    select_bf = select_mask.astype(jnp.bfloat16)
    select_f32 = select_mask.astype(jnp.float32)
    send_a = jnp.einsum(
        "ra,adk->rdk", pick_bf, down_panels, preferred_element_type=jnp.float32
    ).astype(jnp.bfloat16)
    send_b = jnp.einsum(
        "ra,akc->rkc", pick_bf, up_panels, preferred_element_type=jnp.float32
    ).astype(jnp.bfloat16)
    got_a, got_b = (
        lax.all_to_all(send_a, "dp", split_axis=0, concat_axis=0, tiled=True),
        lax.all_to_all(send_b, "dp", split_axis=0, concat_axis=0, tiled=True),
    )
    panel_a = jnp.einsum(
        "bo,odk->bdk", select_bf, got_a, preferred_element_type=jnp.float32
    ).astype(jnp.bfloat16)
    panel_b = jnp.einsum(
        "bo,okc->bkc", select_bf, got_b, preferred_element_type=jnp.float32
    ).astype(jnp.bfloat16)
    token_blocks = tokens.reshape(blocks, BLOCK_ROWS, width_dev)
    partial_value = jnp.dot(tokens, value_weight, preferred_element_type=jnp.float32)
    base = lax.psum_scatter(partial_value, "mp", scatter_dimension=0, tiled=True)
    down_part = jnp.einsum(
        "bnd,bdk->bnk", token_blocks, panel_a, preferred_element_type=jnp.float32
    )
    down = lax.psum(down_part, "mp").astype(jnp.bfloat16)
    first_row = my_part * own_rows
    my_down = lax.dynamic_slice_in_dim(down.reshape(rows, RANK), first_row, own_rows, 0).reshape(
        groups, group, RANK
    )
    group_blocks = (first_row + jnp.arange(groups, dtype=jnp.int32) * group) // BLOCK_ROWS
    my_up = jnp.take(panel_b, group_blocks, axis=0)
    lifted = jnp.einsum("gnk,gkc->gnc", my_down, my_up, preferred_element_type=jnp.float32)
    projected = (base + lifted.reshape(own_rows, kv_full)).astype(jnp.bfloat16)
    cot_all = lax.all_gather(cotangent, "mp", axis=0, tiled=True)
    grad_base = jnp.einsum("nc,dc->nd", cot_all, value_weight, preferred_element_type=jnp.float32)
    cot_blocks = cot_all.reshape(blocks, BLOCK_ROWS, kv_full)
    back = jnp.einsum(
        "bnc,bkc->bnk", cot_blocks, panel_b, preferred_element_type=jnp.float32
    ).astype(jnp.bfloat16)
    through = jnp.einsum("bnk,bdk->bnd", back, panel_a, preferred_element_type=jnp.float32)
    grad_tokens = (grad_base + through.reshape(rows, width_dev)).astype(jnp.bfloat16)
    block_grad_a = jnp.einsum(
        "bnd,bnk->bdk", token_blocks, back, preferred_element_type=jnp.float32
    )
    cot_share = lax.dynamic_slice_in_dim(cot_blocks, my_part * kv_part, kv_part, 2)
    block_grad_b = jnp.einsum("bnk,bnc->bkc", down, cot_share, preferred_element_type=jnp.float32)
    send_ga = jnp.einsum("bo,bdk->odk", select_f32, block_grad_a, precision=highest)
    send_gb = jnp.einsum("bo,bkc->okc", select_f32, block_grad_b, precision=highest)
    recv_ga, recv_gb = (
        lax.all_to_all(send_ga, "dp", split_axis=0, concat_axis=0, tiled=True),
        lax.all_to_all(send_gb, "dp", split_axis=0, concat_axis=0, tiled=True),
    )
    pick_f32 = pick_mask.astype(jnp.float32)
    grad_down = jnp.einsum("ra,rdk->adk", pick_f32, recv_ga, precision=highest).astype(jnp.bfloat16)
    grad_share = jnp.einsum("ra,rkc->akc", pick_f32, recv_gb, precision=highest).astype(
        jnp.bfloat16
    )
    grad_up = lax.all_gather(grad_share, "mp", axis=2, tiled=True)
    return (projected, grad_tokens, grad_down, grad_up)


def solution(mesh):
    placed = (
        P("dp", "mp"),
        P("mp", None),
        P("dp", "mp", None),
        P("dp", None, None),
        P(("dp", "mp"), None),
        P(),
        P(),
    )
    return jax.shard_map(
        per_device,
        mesh=mesh,
        in_specs=placed,
        out_specs=(P(("dp", "mp"), None), P("dp", "mp"), P("dp", "mp", None), P("dp", None, None)),
        check_vma=False,
    )
```

profile of v0, /device:TPU:24, one launch (start us, length us, event | category | flops | bytes accessed | tf_op | source)
XLA Modules:
  0.0 293.9 jit_solution(1035140061272832880)
XLA Ops:
  7.2 0.0 all-gather.3.cloned.1.call-start
  7.2 0.7 all-gather.3.cloned.1.call-update
  7.9 0.9 select_reduce_fusion
  8.8 0.1 reduce_sum.21
  8.9 0.1 fusion.56
  9.0 0.1 fusion.34
  9.1 1.8 convolution_convert_fusion.1
  10.9 2.5 copy.43
  13.5 9.4 %all-to-all-start = ((bf16[32,512,64]{1,2,0:T(8,128)(2,1)}), bf16[32,512,64]{1,2,0:T(8,128)(2,1)S(1)}, u32[]{:S(2)}, u32[]{:S(2)}) async-start(bf16[32,512,64]{1,2,0:T(8,128)(2,1)} %copy.43), calls=%async_computation.1 | async-start | bytes 4194304 | tf_op jit(solution)/shard_map/all_to_all | solution.py:45
  22.9 0.0 all-gather.5.cloned.1.call-start
  23.0 27.1 %all-to-all-done = bf16[32,512,64]{1,2,0:T(8,128)(2,1)S(1)} async-done(((bf16[32,512,64]{1,2,0:T(8,128)(2,1)}), bf16[32,512,64]{1,2,0:T(8,128)(2,1)S(1)}, u32[]{:S(2)}, u32[]{:S(2)}) %all-to-all-start) | async-done | bytes 2097184 | tf_op jit(solution)/shard_map/all_to_all | solution.py:45
  50.1 1.2 fusion.10
  51.3 0.8 copy-done.1
  52.1 0.5 convolution_bitcast_fusion.1
  52.6 62.9 %all-reduce.1 = bf16[8,128,64]{1,2,0:T(8,128)(2,1)S(1)} all-reduce(f32[8,128,64]{1,2,0:T(8,128)S(1)} %convolution_bitcast_fusion.1), channel_id=1, replica_groups=mesh['dp'=32,'mp'=16] {'mp'}, use_global_device_ids=true, to_apply=%region_4.5 | all-reduce | flops 65536 | bytes 393216 | tf_op jit(solution)/shard_map/psum | solution.py:60
  115.5 1.2 fusion.28
  116.8 0.7 fusion.26
  117.5 0.6 copy.57
  118.1 0.7 reshape.88
  118.8 14.9 %all_to_all.20 = f32[32,1,4096]{2,1,0:T(1,128)S(1)} all-to-all(f32[32,1,4096]{2,1,0:T(1,128)S(1)} %reshape.88), channel_id=1, replica_groups=mesh['dp'=32,'mp'=16] {'dp'}, dimensions={0} | all-to-all | bytes 1048576 | tf_op jit(solution)/shard_map/all_to_all | solution.py:86
  133.7 0.5 broadcast.68
  134.2 1.9 reduce
  136.1 0.4 reshape.89
  136.5 1.0 convolution_convert_fusion.2
  137.5 0.8 copy.59
  138.4 1.3 convolution_convert_fusion
  139.7 4.3 %copy.48 = bf16[32,64,1024]{2,1,0:T(8,128)(2,1)} copy(bf16[32,64,1024]{2,0,1:T(8,128)(2,1)S(1)} %convolution_convert_fusion) | data formatting | bytes 8388608 | tf_op jit(solution)/shard_map/convert_element_type | solution.py:43
  144.0 7.2 %all-to-all-start.1 = ((bf16[32,64,1024]{2,1,0:T(8,128)(2,1)}), bf16[32,64,1024]{2,1,0:T(8,128)(2,1)}, u32[]{:S(2)}, u32[]{:S(2)}) async-start(bf16[32,64,1024]{2,1,0:T(8,128)(2,1)} %copy.48), calls=%async_computation.2 | async-start | bytes 8388608 | tf_op jit(solution)/shard_map/all_to_all | solution.py:46
  151.2 0.3 reduce-scatter.2.cloned.1.call-start
  151.5 3.2 %fusion.57 = f32[1024,1024]{1,0:T(8,128)} fusion(bf16[1024,512]{1,0:T(8,128)(2,1)S(1)} %copy-done.4, bf16[512,1024]{1,0:T(8,128)(2,1)S(1)} %copy-done.7), kind=kOutput, calls=%fused_computation.66 | convolution fusion | flops 1073741824 | bytes 6291456 | tf_op jit(solution)/shard_map/dot_general | solution.py:55
  154.7 46.9 %all-to-all-done.1 = bf16[32,64,1024]{2,1,0:T(8,128)(2,1)} async-done(((bf16[32,64,1024]{2,1,0:T(8,128)(2,1)}), bf16[32,64,1024]{2,1,0:T(8,128)(2,1)}, u32[]{:S(2)}, u32[]{:S(2)}) %all-to-all-start.1) | async-done | bytes 4194336 | tf_op jit(solution)/shard_map/all_to_all | solution.py:46
  201.6 6.9 %fusion.7 = bf16[8,64,1024]{2,0,1:T(8,128)(2,1)S(1)} fusion(bf16[32,64,1024]{2,1,0:T(8,128)(2,1)} %all-to-all-done.1, s32[8]{0:T(128)S(1)} %fusion.51), kind=kOutput, calls=%fused_computation.10 | convolution fusion | flops 34078976 | bytes 5242912 | tf_op jit(solution)/shard_map/bo,okc->bkc/dot_general | solution.py:51
  208.5 0.9 convolution_convert_fusion.3
  209.4 0.3 convolution_bitcast_fusion
  209.7 2.1 fusion.18
  211.8 4.4 %copy.53 = f32[32,512,64]{1,2,0:T(8,128)} copy(f32[32,512,64]{1,0,2:T(8,128)S(1)} %fusion.18) | data formatting | bytes 8388608 | tf_op jit(solution)/shard_map/bo,bdk->odk/dot_general | solution.py:82
  216.2 8.1 %all-to-all-start.2 = ((f32[32,512,64]{1,2,0:T(8,128)}), f32[32,512,64]{1,2,0:T(8,128)}, u32[]{:S(2)}, u32[]{:S(2)}) async-start(f32[32,512,64]{1,2,0:T(8,128)} %copy.53), calls=%async_computation.3 | async-start | bytes 8388608 | tf_op jit(solution)/shard_map/all_to_all | solution.py:85
  224.3 0.3 broadcast_select_fusion
  224.7 0.5 fusion.23
  225.2 0.7 copy-done.6
  225.9 0.3 copy-done.8
  226.1 2.3 fusion.4
  228.4 3.3 %copy.61 = bf16[8,64,1024]{2,1,0:T(8,128)(2,1)} copy(bf16[8,64,1024]{1,0,2:T(8,128)(2,1)} %all-gather.5.cloned.1.call-done) | data formatting | bytes 2097152
  231.7 43.0 %all-to-all-done.2 = f32[32,512,64]{1,2,0:T(8,128)} async-done(((f32[32,512,64]{1,2,0:T(8,128)}), f32[32,512,64]{1,2,0:T(8,128)}, u32[]{:S(2)}, u32[]{:S(2)}) %all-to-all-start.2) | async-done | bytes 4194336 | tf_op jit(solution)/shard_map/all_to_all | solution.py:85
  274.7 5.8 %fusion.13 = bf16[8,512,64]{1,0,2:T(8,128)(2,1)S(1)} fusion(f32[32,512,64]{1,2,0:T(8,128)} %all-to-all-done.2, s32[32]{0:T(128)S(1)} %fusion.34, pred[32]{0:T(512)(128)(4,1)S(1)} %get-tuple-element.31), kind=kOutput, calls=%fused_computation.13 | convolution fusion | flops 100925952 | bytes 4718752 | tf_op jit(solution)/shard_map/ra,rdk->adk/dot_general | solution.py:89
  280.5 0.9 copy.60
  281.4 4.0 %reduce-scatter.2.cloned.1.call-done = f32[64,1024]{1,0:T(8,128)} async-done(((f32[1024,1024]{1,0:T(8,128)}), f32[64,1024]{1,0:T(8,128)}) %reduce-scatter.2.cloned.1.call-update) | async-done | bytes 262160 | tf_op jit(solution)/shard_map/reduce_scatter | solution.py:56
  285.4 1.9 fusion.16
  (21 shorter events, 0.1 us)
Async XLA Ops:
  7.2 131.2 %copy-start = (bf16[8,64,1024]{2,1,0:T(8,128)(2,1)S(1)}, bf16[8,64,1024]{2,1,0:T(8,128)(2,1)}, u32[]{:S(2)}) copy-start(bf16[8,64,1024]{2,1,0:T(8,128)(2,1)} %param.10) | copy-start | bytes 3145732
  7.2 108.4 %all-gather.3.cloned.1.call-start = ((), (), s32[]{:S(2)}) async-start(), calls=%async_computation.6 | async-start | bytes 2228224 | tf_op jit(solution)/shard_map/all_gather | solution.py:69
  13.5 36.6 %all-to-all-start = ((bf16[32,512,64]{1,2,0:T(8,128)(2,1)}), bf16[32,512,64]{1,2,0:T(8,128)(2,1)S(1)}, u32[]{:S(2)}, u32[]{:S(2)}) async-start(bf16[32,512,64]{1,2,0:T(8,128)(2,1)} %copy.43), calls=%async_computation.1 | async-start | bytes 4194304 | tf_op jit(solution)/shard_map/all_to_all | solution.py:45
  22.9 205.5 %all-gather.5.cloned.1.call-start = ((), (), s32[]{:S(2)}) async-start(), calls=%async_computation.7 | async-start | bytes 2228224 | tf_op jit(solution)/shard_map/all_gather | solution.py:93
  50.1 2.0 copy-start.3
  51.3 0.8 copy-start.1
  144.0 7.5 %copy-start.4 = (bf16[1024,512]{1,0:T(8,128)(2,1)S(1)}, bf16[1024,512]{1,0:T(8,128)(2,1)}, u32[]{:S(2)}) copy-start(bf16[1024,512]{1,0:T(8,128)(2,1)} %param.7) | copy-start | bytes 3145732
  144.0 7.5 %copy-start.7 = (bf16[512,1024]{1,0:T(8,128)(2,1)S(1)}, bf16[512,1024]{1,0:T(8,128)(2,1)}, u32[]{:S(2)}) copy-start(bf16[512,1024]{1,0:T(8,128)(2,1)} %param.8) | copy-start | bytes 3145732
  144.0 57.6 %all-to-all-start.1 = ((bf16[32,64,1024]{2,1,0:T(8,128)(2,1)}), bf16[32,64,1024]{2,1,0:T(8,128)(2,1)}, u32[]{:S(2)}, u32[]{:S(2)}) async-start(bf16[32,64,1024]{2,1,0:T(8,128)(2,1)} %copy.48), calls=%async_computation.2 | async-start | bytes 8388608 | tf_op jit(solution)/shard_map/all_to_all | solution.py:46
  151.2 134.2 %reduce-scatter.2.cloned.1.call-start = ((), (), s32[]{:S(2)}) async-start(), calls=%async_computation.5 | async-start | bytes 4456448 | tf_op jit(solution)/shard_map/reduce_scatter | solution.py:56
  201.6 6.9 %copy-start.5 = (bf16[1024,1024]{1,0:T(8,128)(2,1)S(1)}, bf16[1024,1024]{1,0:T(8,128)(2,1)}, u32[]{:S(2)}) copy-start(bf16[1024,1024]{1,0:T(8,128)(2,1)} %all-gather.3.cloned.1.call-done) | copy-start | bytes 6291460
  216.2 8.5 %copy-start.2 = (bf16[8,512,64]{1,0,2:T(8,128)(2,1)S(1)}, bf16[8,512,64]{1,0,2:T(8,128)(2,1)}, u32[]{:S(2)}) copy-start(bf16[8,512,64]{1,0,2:T(8,128)(2,1)} %copy-done.1) | copy-start | bytes 1572868
  216.2 58.4 %all-to-all-start.2 = ((f32[32,512,64]{1,2,0:T(8,128)}), f32[32,512,64]{1,2,0:T(8,128)}, u32[]{:S(2)}, u32[]{:S(2)}) async-start(f32[32,512,64]{1,2,0:T(8,128)} %copy.53), calls=%async_computation.3 | async-start | bytes 8388608 | tf_op jit(solution)/shard_map/all_to_all | solution.py:85
  224.3 1.6 copy-start.6
  224.3 1.8 copy-start.8
Sparse Core Ops, SparseCore 0:
  10.1 78.2 all-gather.2
  138.5 67.9 all-gather.4
  209.4 76.0 reduce-scatter.1
where the time goes:
time: 295 us; the launch traced here: 294 us
  waiting for transfers between devices  122 us (41%)
  blocking collectives  77.8 us (26%)
  matrix products  31.6 us (11%)
  starting transfers between devices  25 us (8%)
  local copies, waits for them, and re-layouts  20.3 us (7%)
  between operations  14 us (5%)
  other arithmetic  3.37 us (1%)
    psum x1, blocking collectives, per_device(): down = lax.psum(down_part, 'mp').astype(jnp.bfloat16)  62.9 us
    all_to_all x1, waiting for transfers between devices, per_device(): lax.all_to_all(send_b, 'dp', split_axis=0, concat_axis=0, tiled=True)  46.9 us
    all_to_all x1, waiting for transfers between devices, per_device(): lax.all_to_all(send_ga, 'dp', split_axis=0, concat_axis=0, tiled=True)  43 us
    all_to_all x1, waiting for transfers between devices, per_device(): lax.all_to_all(send_a, 'dp', split_axis=0, concat_axis=0, tiled=True)  27.1 us
    all_to_all x1, blocking collectives, per_device(): lax.all_to_all(send_gb, 'dp', split_axis=0, concat_axis=0, tiled=True)  14.9 us
    all_to_all x1, starting transfers between devices, per_device(): lax.all_to_all(send_a, 'dp', split_axis=0, concat_axis=0, tiled=True)  9.43 us
    all_to_all x1, starting transfers between devices, per_device(): lax.all_to_all(send_ga, 'dp', split_axis=0, concat_axis=0, tiled=True)  8.05 us
    all_to_all x1, starting transfers between devices, per_device(): lax.all_to_all(send_b, 'dp', split_axis=0, concat_axis=0, tiled=True)  7.2 us
  transfers between devices with their start and end apart: 6, of which 4 were waited for; matrix products, arithmetic and copies ran while one was open for 15% of the time, Pallas kernels for 0%

commit v1 on v0

v1 whole, which is shorter than its diff:
```python
import jax
import jax.numpy as jnp
from jax import lax
from jax.sharding import PartitionSpec as P

RANK = 64
BLOCK_ROWS = 128


def per_device(
    tokens, value_weight, down_panels, up_panels, cotangent, block_adapter, adapter_slot
):
    n_owners = lax.axis_size("dp")
    myself = lax.axis_index("dp")
    n_split = lax.axis_size("mp")
    my_part = lax.axis_index("mp")
    rows, width_dev = tokens.shape
    own_rows, kv_full = cotangent.shape
    kv_part = kv_full // n_split
    stored = down_panels.shape[0]
    blocks = rows // BLOCK_ROWS
    highest = lax.Precision.HIGHEST
    hits = block_adapter[:, None] == jnp.arange(adapter_slot.shape[0], dtype=jnp.int32)[None, :]
    slots_all = jnp.sum(jnp.where(hits, adapter_slot[None, :], 0), axis=1)
    owner_all = (slots_all // stored).reshape(n_owners, blocks)
    local_all = (slots_all % stored).reshape(n_owners, blocks)
    mine = owner_all == myself
    wanted = jnp.sum(jnp.where(mine, local_all, 0), axis=1)
    served = jnp.any(mine, axis=1)
    pick_mask = (wanted[:, None] == jnp.arange(stored, dtype=jnp.int32)[None, :]) & served[:, None]
    my_owner = lax.dynamic_index_in_dim(owner_all, myself, 0, keepdims=False)
    select_mask = my_owner[:, None] == jnp.arange(n_owners, dtype=jnp.int32)[None, :]
    select_f32 = select_mask.astype(jnp.float32)

    send_a = jnp.take(down_panels, wanted, axis=0)
    up_cols = lax.dynamic_slice_in_dim(up_panels, my_part * kv_part, kv_part, 2)
    send_b = jnp.take(up_cols, wanted, axis=0)
    got_a = lax.all_to_all(send_a, "dp", split_axis=0, concat_axis=0, tiled=True)
    got_b = lax.all_to_all(send_b, "dp", split_axis=0, concat_axis=0, tiled=True)
    panel_a = jnp.take(got_a, my_owner, axis=0)
    panel_b_cols = jnp.take(got_b, my_owner, axis=0)

    first_row = my_part * own_rows
    part_block = (jnp.arange(n_split, dtype=jnp.int32) * own_rows) // BLOCK_ROWS
    to_parts = jnp.take(panel_b_cols, part_block, axis=0)
    from_parts = lax.all_to_all(to_parts, "mp", split_axis=0, concat_axis=0, tiled=True)
    my_up = from_parts.transpose(1, 0, 2).reshape(RANK, kv_full)

    token_blocks = tokens.reshape(blocks, BLOCK_ROWS, width_dev)
    partial_value = jnp.dot(tokens, value_weight, preferred_element_type=jnp.float32)
    base = lax.psum_scatter(partial_value, "mp", scatter_dimension=0, tiled=True)
    down_part = jnp.einsum(
        "bnd,bdk->bnk", token_blocks, panel_a, preferred_element_type=jnp.float32
    )
    down = lax.psum(down_part, "mp").astype(jnp.bfloat16)
    my_down = lax.dynamic_slice_in_dim(down.reshape(rows, RANK), first_row, own_rows, 0)
    lifted = jnp.dot(my_down, my_up, preferred_element_type=jnp.float32)
    projected = (base + lifted).astype(jnp.bfloat16)

    my_back = jnp.einsum(
        "nc,kc->nk", cotangent, my_up, preferred_element_type=jnp.float32
    ).astype(jnp.bfloat16)
    back = lax.all_gather(my_back, "mp", axis=0, tiled=True).reshape(blocks, BLOCK_ROWS, RANK)

    cot_all = lax.all_gather(cotangent, "mp", axis=0, tiled=True)
    grad_base = jnp.einsum("nc,dc->nd", cot_all, value_weight, preferred_element_type=jnp.float32)
    through = jnp.einsum("bnk,bdk->bnd", back, panel_a, preferred_element_type=jnp.float32)
    grad_tokens = (grad_base + through.reshape(rows, width_dev)).astype(jnp.bfloat16)

    block_grad_a = jnp.einsum(
        "bnd,bnk->bdk", token_blocks, back, preferred_element_type=jnp.float32
    ).astype(jnp.bfloat16)
    cot_blocks = cot_all.reshape(blocks, BLOCK_ROWS, kv_full)
    cot_share = lax.dynamic_slice_in_dim(cot_blocks, my_part * kv_part, kv_part, 2)
    block_grad_b = jnp.einsum(
        "bnk,bnc->bkc", down.reshape(blocks, BLOCK_ROWS, RANK), cot_share,
        preferred_element_type=jnp.float32,
    )
    send_ga = jnp.einsum(
        "bo,bdk->odk", select_mask.astype(jnp.bfloat16), block_grad_a,
        preferred_element_type=jnp.float32,
    ).astype(jnp.bfloat16)
    send_gb = jnp.einsum("bo,bkc->okc", select_f32, block_grad_b, precision=highest)
    recv_ga = lax.all_to_all(send_ga, "dp", split_axis=0, concat_axis=0, tiled=True)
    recv_gb = lax.all_to_all(send_gb, "dp", split_axis=0, concat_axis=0, tiled=True)
    pick_f32 = pick_mask.astype(jnp.float32)
    grad_down = jnp.einsum(
        "ra,rdk->adk", pick_mask.astype(jnp.bfloat16), recv_ga, preferred_element_type=jnp.float32
    ).astype(jnp.bfloat16)
    grad_share = jnp.einsum("ra,rkc->akc", pick_f32, recv_gb, precision=highest).astype(
        jnp.bfloat16
    )
    grad_up = lax.all_gather(grad_share, "mp", axis=2, tiled=True)
    return (projected, grad_tokens, grad_down, grad_up)


def solution(mesh):
    placed = (
        P("dp", "mp"),
        P("mp", None),
        P("dp", "mp", None),
        P("dp", None, None),
        P(("dp", "mp"), None),
        P(),
        P(),
    )
    return jax.shard_map(
        per_device,
        mesh=mesh,
        in_specs=placed,
        out_specs=(P(("dp", "mp"), None), P("dp", "mp"), P("dp", "mp", None), P("dp", None, None)),
        check_vma=False,
    )
```

time: 295 us -> 298 us (1.010)
  blocking collectives: 77.8 us -> 131 us
  waiting for transfers between devices: 122 us -> 85.1 us
  matrix products: 31.6 us -> 19.1 us
    all_to_all x1, waiting for transfers between devices: 46.9 us -> 6.67 us  [per_device(): lax.all_to_all(send_b, 'dp', split_axis=0, concat_axis=0, tiled=True)]
    all_gather x0 -> x1, blocking collectives: none -> 31.2 us  [per_device(): lax.all_gather(my_back, 'mp', axis=0, tiled=True)]
    reduce_scatter x1, waiting for transfers between devices: 4.04 us -> 27.8 us  [per_device(): lax.psum_scatter(partial_value, 'mp', scatter_dimension=0, tiled=True)]
    all_to_all x0 -> x1, blocking collectives: none -> 21.9 us  [per_device(): lax.all_to_all(to_parts, 'mp', split_axis=0, concat_axis=0, tiled=True)]
    all_to_all x1, waiting for transfers between devices: 43 us -> 22.8 us  [per_device(): lax.all_to_all(send_ga, 'dp', split_axis=0, concat_axis=0, tiled=True)]
    dot_general x9 -> x5, matrix products: 23.1 us -> 5.37 us  [the longest x1 1.91 us: per_device(): lifted = jnp.dot(my_down, my_up, preferred_element_type=jnp.float32)]
    gather x0 -> x5, local copies, waits for them, and re-layouts: none -> 5.72 us  [the longest x1 2.17 us: per_device(): panel_a = jnp.take(got_a, my_owner, axis=0)]
    dot_general x1 -> x0, local copies, waits for them, and re-layouts: 4.39 us -> none  [per_device(): jnp.einsum('bo,bdk->odk', select_f32, block_grad_a, precision=highest)]
  transfers between devices with their start and end apart: 6 -> 6, of which waited for: 4 -> 4; matrix products, arithmetic and copies ran while one was open for 15% -> 12% of each run, Pallas kernels for 0% -> 0%
where the time goes in v1:
time: 298 us; the launch traced here: 297 us
  blocking collectives  131 us (44%)
  waiting for transfers between devices  85.1 us (29%)
  starting transfers between devices  22.2 us (7%)
  local copies, waits for them, and re-layouts  20.6 us (7%)
  matrix products  19.1 us (6%)
  between operations  14.1 us (5%)
  other arithmetic  4.96 us (2%)
    psum x1, blocking collectives, per_device(): down = lax.psum(down_part, 'mp').astype(jnp.bfloat16)  62.6 us
    all_gather x1, blocking collectives, per_device(): lax.all_gather(my_back, 'mp', axis=0, tiled=True)  31.2 us
    reduce_scatter x1, waiting for transfers between devices, per_device(): lax.psum_scatter(partial_value, 'mp', scatter_dimension=0, tiled=True)  27.8 us
    all_to_all x1, waiting for transfers between devices, per_device(): lax.all_to_all(send_a, 'dp', split_axis=0, concat_axis=0, tiled=True)  27.1 us
    all_to_all x1, waiting for transfers between devices, per_device(): lax.all_to_all(send_ga, 'dp', split_axis=0, concat_axis=0, tiled=True)  22.8 us
    all_to_all x1, blocking collectives, per_device(): lax.all_to_all(to_parts, 'mp', split_axis=0, concat_axis=0, tiled=True)  21.9 us
    all_to_all x1, blocking collectives, per_device(): lax.all_to_all(send_gb, 'dp', split_axis=0, concat_axis=0, tiled=True)  15.1 us
    all_to_all x1, starting transfers between devices, per_device(): lax.all_to_all(send_a, 'dp', split_axis=0, concat_axis=0, tiled=True)  10.1 us
  transfers between devices with their start and end apart: 6, of which 4 were waited for; matrix products, arithmetic and copies ran while one was open for 12% of the time, Pallas kernels for 0%

profile of v1, /device:TPU:24, one launch (start us, length us, event | category | flops | bytes accessed | tf_op | source)
XLA Modules:
  0.0 296.9 jit_solution(200860388559841904)
XLA Ops:
  7.2 0.7 all-gather.3.cloned.1.call-update
  7.9 0.9 select_reduce_fusion
  9.2 1.7 gather_fusion
  10.9 1.6 broadcast_select_fusion
  12.5 10.1 %all-to-all-start = ((bf16[32,512,64]{1,2,0:T(8,128)(2,1)}), bf16[32,512,64]{1,2,0:T(8,128)(2,1)}, u32[]{:S(2)}, u32[]{:S(2)}) async-start(bf16[32,512,64]{1,2,0:T(8,128)(2,1)} %broadcast_select_fusion), calls=%async_computation.1 | async-start | bytes 4194304 | tf_op jit(solution)/shard_map/all_to_all | solution.py:38
  22.7 27.1 %all-to-all-done = bf16[32,512,64]{1,2,0:T(8,128)(2,1)} async-done(((bf16[32,512,64]{1,2,0:T(8,128)(2,1)}), bf16[32,512,64]{1,2,0:T(8,128)(2,1)}, u32[]{:S(2)}, u32[]{:S(2)}) %all-to-all-start) | async-done | bytes 2097184 | tf_op jit(solution)/shard_map/all_to_all | solution.py:38
  49.8 2.2 gather_fusion.1
  52.0 0.5 convolution_bitcast_fusion
  52.5 62.6 %all-reduce.1 = bf16[8,128,64]{1,2,0:T(8,128)(2,1)S(1)} all-reduce(f32[8,128,64]{1,2,0:T(8,128)S(1)} %convolution_bitcast_fusion), channel_id=1, replica_groups=mesh['dp'=32,'mp'=16] {'mp'}, use_global_device_ids=true, to_apply=%region_3.4 | all-reduce | flops 65536 | bytes 393216 | tf_op jit(solution)/shard_map/psum | solution.py:55
  115.2 1.2 fusion.13
  116.5 0.7 fusion.11
  117.2 0.6 copy.58
  117.8 0.7 reshape.206
  118.4 15.1 %all_to_all.25 = f32[32,1,4096]{2,1,0:T(1,128)S(1)} all-to-all(f32[32,1,4096]{2,1,0:T(1,128)S(1)} %reshape.206), channel_id=1, replica_groups=mesh['dp'=32,'mp'=16] {'dp'}, dimensions={0} | all-to-all | bytes 1048576 | tf_op jit(solution)/shard_map/all_to_all | solution.py:85
  133.5 0.5 broadcast.234
  134.0 1.9 reduce
  135.9 0.4 reshape.207
  136.4 1.0 convolution_convert_fusion.2
  137.4 0.8 copy.60
  138.3 4.4 %fusion.45 = f32[1024,1024]{1,0:T(8,128)} fusion(bf16[1024,512]{1,0:T(8,128)(2,1)S(1)} %copy-done, bf16[512,1024]{1,0:T(8,128)(2,1)} %param.8), kind=kOutput, calls=%fused_computation.90 | convolution fusion | flops 1073741824 | bytes 6291456 | tf_op jit(solution)/shard_map/dot_general | solution.py:50
  142.7 1.0 constant_dynamic-slice_fusion
  143.8 0.6 gather_fusion.2
  144.5 1.1 reshape.202
  145.6 6.2 %all-to-all-start.1 = ((bf16[32,2,2048]{2,1,0:T(2,128)(2,1)}), bf16[32,2,2048]{2,1,0:T(2,128)(2,1)S(1)}, u32[]{:S(2)}, u32[]{:S(2)}) async-start(bf16[32,2,2048]{2,1,0:T(2,128)(2,1)} %reshape.202), calls=%async_computation.2 | async-start | bytes 524288 | tf_op jit(solution)/shard_map/all_to_all | solution.py:39
  151.9 6.7 %all-to-all-done.1 = bf16[32,2,2048]{2,1,0:T(2,128)(2,1)S(1)} async-done(((bf16[32,2,2048]{2,1,0:T(2,128)(2,1)}), bf16[32,2,2048]{2,1,0:T(2,128)(2,1)S(1)}, u32[]{:S(2)}, u32[]{:S(2)}) %all-to-all-start.1) | async-done | bytes 262176 | tf_op jit(solution)/shard_map/all_to_all | solution.py:39
  158.5 0.4 reshape.203
  158.9 0.6 gather_fusion.3
  159.6 0.6 gather_fusion.4
  160.3 0.2 reshape.204
  160.5 21.9 %all_to_all.26 = bf16[16,2,2048]{2,1,0:T(2,128)(2,1)S(1)} all-to-all(bf16[16,2,2048]{2,1,0:T(2,128)(2,1)S(1)} %reshape.204), channel_id=1, replica_groups=mesh['dp'=32,'mp'=16] {'mp'}, dimensions={0} | all-to-all | bytes 262144 | tf_op jit(solution)/shard_map/all_to_all | solution.py:46
  182.4 0.2 reshape.205
  182.7 0.2 copy.48
  182.8 0.2 reshape.156
  183.1 0.2 fusion.8
  183.3 31.2 %all_gather.10 = bf16[1024,64]{1,0:T(8,128)(2,1)S(1)} all-gather(bf16[64,64]{1,0:T(8,128)(2,1)S(1)} %copy.49), channel_id=1, replica_groups=mesh['dp'=32,'mp'=16] {'mp'}, dimensions={0}, use_global_device_ids=true | all-gather | bytes 139264 | tf_op jit(solution)/shard_map/all_gather | solution.py:63
  214.5 0.3 fusion.6
  214.9 0.8 convolution_convert_fusion
  215.7 2.5 copy.54
  218.2 5.9 %all-to-all-start.3 = ((bf16[32,512,64]{1,2,0:T(8,128)(2,1)}), bf16[32,512,64]{1,2,0:T(8,128)(2,1)S(1)}, u32[]{:S(2)}, u32[]{:S(2)}) async-start(bf16[32,512,64]{1,2,0:T(8,128)(2,1)} %copy.54), calls=%async_computation.4 | async-start | bytes 4194304 | tf_op jit(solution)/shard_map/all_to_all | solution.py:84
  224.1 1.6 copy_bitcast_fusion
  225.7 2.8 fusion.15
  228.5 22.8 %all-to-all-done.3 = bf16[32,512,64]{1,2,0:T(8,128)(2,1)S(1)} async-done(((bf16[32,512,64]{1,2,0:T(8,128)(2,1)}), bf16[32,512,64]{1,2,0:T(8,128)(2,1)S(1)}, u32[]{:S(2)}, u32[]{:S(2)}) %all-to-all-start.3) | async-done | bytes 2097184 | tf_op jit(solution)/shard_map/all_to_all | solution.py:84
  251.3 1.2 fusion.3
  252.5 1.0 copy.61
  253.5 3.9 %fusion = bf16[1024,512]{1,0:T(8,128)(2,1)} fusion(f32[8,128,512]{2,1,0:T(8,128)S(1)} %copy-done.2, bf16[1024,1024]{1,0:T(8,128)(2,1)} %all-gather.3.cloned.1.call-done, bf16[512,1024]{1,0:T(8,128)(2,1)S(1)} %copy-done.5), kind=kOutput, calls=%fused_computation.6 | convolution fusion | flops 1074790400 | bytes 6291456 | tf_op jit(solution)/shard_map/nc,dc->nd/dot_general | solution.py:66
  257.3 3.3 %copy.62 = bf16[8,64,1024]{2,1,0:T(8,128)(2,1)} copy(bf16[8,64,1024]{1,0,2:T(8,128)(2,1)} %all-gather.5.cloned.1.call-done) | data formatting | bytes 2097152
  260.6 27.8 %reduce-scatter.2.cloned.1.call-done = f32[64,1024]{1,0:T(8,128)} async-done(((f32[1024,1024]{1,0:T(8,128)}), f32[64,1024]{1,0:T(8,128)}) %reduce-scatter.2.cloned.1.call-update) | async-done | bytes 262160 | tf_op jit(solution)/shard_map/reduce_scatter | solution.py:51
  288.4 1.9 fusion.7
  (35 shorter events, 1.0 us)
Async XLA Ops:
  7.2 44.8 %copy-start = (bf16[1024,512]{1,0:T(8,128)(2,1)S(1)}, bf16[1024,512]{1,0:T(8,128)(2,1)}, u32[]{:S(2)}) copy-start(bf16[1024,512]{1,0:T(8,128)(2,1)} %param.7) | copy-start | bytes 3145732
  7.2 108.0 %all-gather.3.cloned.1.call-start = ((), (), s32[]{:S(2)}) async-start(), calls=%async_computation.7 | async-start | bytes 2228224 | tf_op jit(solution)/shard_map/all_gather | solution.py:65
  12.5 37.3 %all-to-all-start = ((bf16[32,512,64]{1,2,0:T(8,128)(2,1)}), bf16[32,512,64]{1,2,0:T(8,128)(2,1)}, u32[]{:S(2)}, u32[]{:S(2)}) async-start(bf16[32,512,64]{1,2,0:T(8,128)(2,1)} %broadcast_select_fusion), calls=%async_computation.1 | async-start | bytes 4194304 | tf_op jit(solution)/shard_map/all_to_all | solution.py:38
  22.6 234.8 %all-gather.5.cloned.1.call-start = ((), (), s32[]{:S(2)}) async-start(), calls=%async_computation.8 | async-start | bytes 2228224 | tf_op jit(solution)/shard_map/all_gather | solution.py:93
  52.0 65.2 %copy-start.1 = (bf16[8,512,64]{1,2,0:T(8,128)(2,1)}, bf16[8,512,64]{1,2,0:T(8,128)(2,1)S(1)}, u32[]{:S(2)}) copy-start(bf16[8,512,64]{1,2,0:T(8,128)(2,1)S(1)} %gather_fusion.1) | copy-start | bytes 1572868
  115.2 1.3 copy-start.3
  138.3 150.2 %reduce-scatter.2.cloned.1.call-start = ((), (), s32[]{:S(2)}) async-start(), calls=%async_computation.6 | async-start | bytes 4456448 | tf_op jit(solution)/shard_map/reduce_scatter | solution.py:51
  145.6 12.9 %all-to-all-start.1 = ((bf16[32,2,2048]{2,1,0:T(2,128)(2,1)}), bf16[32,2,2048]{2,1,0:T(2,128)(2,1)S(1)}, u32[]{:S(2)}, u32[]{:S(2)}) async-start(bf16[32,2,2048]{2,1,0:T(2,128)(2,1)} %reshape.202), calls=%async_computation.2 | async-start | bytes 524288 | tf_op jit(solution)/shard_map/all_to_all | solution.py:39
  151.9 31.2 %copy-start.4 = (bf16[64,1024]{1,0:T(8,128)(2,1)S(1)}, bf16[64,1024]{1,0:T(8,128)(2,1)}, u32[]{:S(2)}) copy-start(bf16[64,1024]{1,0:T(8,128)(2,1)} %param.11) | copy-start | bytes 393220
  218.2 33.1 %all-to-all-start.3 = ((bf16[32,512,64]{1,2,0:T(8,128)(2,1)}), bf16[32,512,64]{1,2,0:T(8,128)(2,1)S(1)}, u32[]{:S(2)}, u32[]{:S(2)}) async-start(bf16[32,512,64]{1,2,0:T(8,128)(2,1)} %copy.54), calls=%async_computation.4 | async-start | bytes 4194304 | tf_op jit(solution)/shard_map/all_to_all | solution.py:84
  251.3 2.2 copy-start.2
  251.3 2.2 copy-start.5
Sparse Core Ops, SparseCore 0:
  10.1 77.6 all-gather.2
  138.4 71.5 all-gather.4
  212.8 75.5 reduce-scatter.1

commit v2 on v1

v2 whole, which is shorter than its diff:
```python
import jax
import jax.numpy as jnp
from jax import lax
from jax.sharding import PartitionSpec as P

RANK = 64
BLOCK_ROWS = 128


def per_device(
    tokens, value_weight, down_panels, up_panels, cotangent, block_adapter, adapter_slot
):
    n_owners = lax.axis_size("dp")
    myself = lax.axis_index("dp")
    n_split = lax.axis_size("mp")
    my_part = lax.axis_index("mp")
    rows, width_dev = tokens.shape
    own_rows, kv_full = cotangent.shape
    kv_part = kv_full // n_split
    stored = down_panels.shape[0]
    blocks = rows // BLOCK_ROWS
    hits = block_adapter[:, None] == jnp.arange(adapter_slot.shape[0], dtype=jnp.int32)[None, :]
    slots_all = jnp.sum(jnp.where(hits, adapter_slot[None, :], 0), axis=1)
    owner_all = (slots_all // stored).reshape(n_owners, blocks)
    local_all = (slots_all % stored).reshape(n_owners, blocks)
    mine = owner_all == myself
    wanted = jnp.sum(jnp.where(mine, local_all, 0), axis=1)
    served = jnp.any(mine, axis=1)
    pick_mask = (wanted[:, None] == jnp.arange(stored, dtype=jnp.int32)[None, :]) & served[:, None]
    my_owner = lax.dynamic_index_in_dim(owner_all, myself, 0, keepdims=False)
    select_mask = my_owner[:, None] == jnp.arange(n_owners, dtype=jnp.int32)[None, :]

    up_cols = lax.dynamic_slice_in_dim(up_panels, my_part * kv_part, kv_part, 2)
    both = jnp.concatenate([down_panels, up_cols], axis=1)
    got = lax.all_to_all(jnp.take(both, wanted, axis=0), "dp", split_axis=0, concat_axis=0, tiled=True)
    mine_got = jnp.take(got, my_owner, axis=0)
    panel_a = mine_got[:, :width_dev]
    panel_b_cols = mine_got[:, width_dev:]
    cot_all = lax.all_gather(cotangent, "mp", axis=0, tiled=True)
    panel_b = lax.all_gather(panel_b_cols, "mp", axis=2, tiled=True)

    token_blocks = tokens.reshape(blocks, BLOCK_ROWS, width_dev)
    partial_value = jnp.dot(tokens, value_weight, preferred_element_type=jnp.float32)
    base = lax.psum_scatter(partial_value, "mp", scatter_dimension=0, tiled=True)
    down_part = jnp.einsum(
        "bnd,bdk->bnk", token_blocks, panel_a, preferred_element_type=jnp.float32
    )
    first_row = my_part * own_rows
    my_down = lax.psum_scatter(
        down_part.reshape(rows, RANK), "mp", scatter_dimension=0, tiled=True
    ).astype(jnp.bfloat16)
    down = lax.all_gather(my_down, "mp", axis=0, tiled=True)

    cot_blocks = cot_all.reshape(blocks, BLOCK_ROWS, kv_full)
    back = jnp.einsum(
        "bnc,bkc->bnk", cot_blocks, panel_b, preferred_element_type=jnp.float32
    ).astype(jnp.bfloat16)
    block_grad_a = jnp.einsum(
        "bnd,bnk->bdk", token_blocks, back, preferred_element_type=jnp.float32
    ).astype(jnp.bfloat16)
    cot_share = lax.dynamic_slice_in_dim(cot_blocks, my_part * kv_part, kv_part, 2)
    block_grad_b = jnp.einsum(
        "bnk,bnc->bkc", down.reshape(blocks, BLOCK_ROWS, RANK), cot_share,
        preferred_element_type=jnp.float32,
    ).astype(jnp.bfloat16)
    grads = jnp.concatenate([block_grad_a, block_grad_b], axis=1)
    send_g = jnp.einsum(
        "bo,bdk->odk", select_mask.astype(jnp.bfloat16), grads, preferred_element_type=jnp.float32
    ).astype(jnp.bfloat16)
    recv_g = lax.all_to_all(send_g, "dp", split_axis=0, concat_axis=0, tiled=True)
    grad_both = jnp.einsum(
        "ra,rdk->adk", pick_mask.astype(jnp.bfloat16), recv_g, preferred_element_type=jnp.float32
    ).astype(jnp.bfloat16)
    grad_down = grad_both[:, :width_dev]
    grad_up = lax.all_gather(grad_both[:, width_dev:], "mp", axis=2, tiled=True)

    my_up = lax.dynamic_index_in_dim(panel_b, first_row // BLOCK_ROWS, 0, keepdims=False)
    lifted = jnp.dot(my_down, my_up, preferred_element_type=jnp.float32)
    projected = (base + lifted).astype(jnp.bfloat16)

    grad_base = jnp.einsum("nc,dc->nd", cot_all, value_weight, preferred_element_type=jnp.float32)
    through = jnp.einsum("bnk,bdk->bnd", back, panel_a, preferred_element_type=jnp.float32)
    grad_tokens = (grad_base + through.reshape(rows, width_dev)).astype(jnp.bfloat16)
    return (projected, grad_tokens, grad_down, grad_up)


def solution(mesh):
    placed = (
        P("dp", "mp"),
        P("mp", None),
        P("dp", "mp", None),
        P("dp", None, None),
        P(("dp", "mp"), None),
        P(),
        P(),
    )
    return jax.shard_map(
        per_device,
        mesh=mesh,
        in_specs=placed,
        out_specs=(P(("dp", "mp"), None), P("dp", "mp"), P("dp", "mp", None), P("dp", None, None)),
        check_vma=False,
    )
```

time: 298 us -> 443 us (1.49)
  waiting for transfers between devices: 85.1 us -> 311 us
  blocking collectives: 131 us -> 68.1 us
  starting transfers between devices: 22.2 us -> 10.4 us
  local copies, waits for them, and re-layouts: 20.6 us -> 15.7 us
    all_gather x1 -> x2, waiting for transfers between devices: 0.01 us -> 143 us  [the longest x1 72.1 us: per_device(): grad_up = lax.all_gather(grad_both[:, width_dev:], 'mp', axis=2, tiled=True)]
    unnamed x3 -> x6, waiting for transfers between devices: 0.71 us -> 63.9 us
    psum x1 -> x0, blocking collectives: 62.6 us -> none  [per_device(): down = lax.psum(down_part, 'mp').astype(jnp.bfloat16)]
    all_gather x1, waiting for transfers between devices: 0.02 us -> 43.7 us  [per_device(): cot_all = lax.all_gather(cotangent, 'mp', axis=0, tiled=True)]
    all_to_all x3 -> x1, waiting for transfers between devices: 56.6 us -> 32.9 us  [per_device(): lax.all_to_all(jnp.take(both, wanted, axis=0), 'dp', split_axis=0, concat...]
    all_to_all x3 -> x1, starting transfers between devices: 22.1 us -> 10.2 us  [per_device(): lax.all_to_all(jnp.take(both, wanted, axis=0), 'dp', split_axis=0, concat...]
    all_to_all x2 -> x1, blocking collectives: 37 us -> 39.2 us  [per_device(): lax.all_to_all(send_g, 'dp', split_axis=0, concat_axis=0, tiled=True)]
  transfers between devices with their start and end apart: 6 -> 6, of which waited for: 4 -> 6; matrix products, arithmetic and copies ran while one was open for 12% -> 5% of each run, Pallas kernels for 0% -> 0%
where the time goes in v2:
time: 443 us; the launch traced here: 442 us
  waiting for transfers between devices  311 us (70%)
  blocking collectives  68.1 us (15%)
  matrix products  17 us (4%)
  local copies, waits for them, and re-layouts  15.7 us (4%)
  between operations  14 us (3%)
  starting transfers between devices  10.4 us (2%)
  other arithmetic  6.2 us (1%)
    all_gather x1, waiting for transfers between devices, per_device(): grad_up = lax.all_gather(grad_both[:, width_dev:], 'mp', axis=2, tiled=True)  72.1 us
    all_gather x1, waiting for transfers between devices, per_device(): panel_b = lax.all_gather(panel_b_cols, 'mp', axis=2, tiled=True)  71.2 us
    unnamed x6, waiting for transfers between devices  63.9 us
    all_gather x1, waiting for transfers between devices, per_device(): cot_all = lax.all_gather(cotangent, 'mp', axis=0, tiled=True)  43.7 us
    all_to_all x1, blocking collectives, per_device(): lax.all_to_all(send_g, 'dp', split_axis=0, concat_axis=0, tiled=True)  39.2 us
    all_to_all x1, waiting for transfers between devices, per_device(): lax.all_to_all(jnp.take(both, wanted, axis=0), 'dp', split_axis=0, concat...  32.9 us
    all_gather x1, blocking collectives, per_device(): down = lax.all_gather(my_down, 'mp', axis=0, tiled=True)  28.9 us
    reduce_scatter x1, waiting for transfers between devices, per_device(): lax.psum_scatter(partial_value, 'mp', scatter_dimension=0, tiled=True)  27.3 us
  transfers between devices with their start and end apart: 6, of which 6 were waited for; matrix products, arithmetic and copies ran while one was open for 5% of the time, Pallas kernels for 0%

profile of v2, /device:TPU:24, one launch (start us, length us, event | category | flops | bytes accessed | tf_op | source)
XLA Modules:
  0.0 442.4 jit_solution(5169202900593899612)
XLA Ops:
  7.2 1.0 select_reduce_fusion
  8.1 0.1 reduce_sum.23
  8.2 0.1 fusion.32
  8.4 0.1 fusion.16
  8.5 1.0 constant_dynamic-slice_fusion
  9.5 0.1 copy.42
  9.7 1.1 pad_maximum_fusion
  10.8 2.4 gather_fusion
  13.2 3.6 broadcast_select_fusion
  16.8 10.2 %all-to-all-start = ((bf16[32,576,64]{1,2,0:T(8,128)(2,1)}), bf16[32,576,64]{1,2,0:T(8,128)(2,1)}, u32[]{:S(2)}, u32[]{:S(2)}) async-start(bf16[32,576,64]{1,2,0:T(8,128)(2,1)} %broadcast_select_fusion), calls=%async_computation.1 | async-start | bytes 5242880 | tf_op jit(solution)/shard_map/all_to_all | solution.py:35
  26.9 0.0 reduce-scatter.7.cloned.1.call-start
  27.0 32.9 %all-to-all-done = bf16[32,576,64]{1,2,0:T(8,128)(2,1)} async-done(((bf16[32,576,64]{1,2,0:T(8,128)(2,1)}), bf16[32,576,64]{1,2,0:T(8,128)(2,1)}, u32[]{:S(2)}, u32[]{:S(2)}) %all-to-all-start) | async-done | bytes 2359328 | tf_op jit(solution)/shard_map/all_to_all | solution.py:35
  59.9 2.4 gather_fusion.1
  62.3 0.1 broadcast_select_fusion.1
  62.5 0.5 convolution_bitcast_fusion
  63.0 1.0 copy.60
  64.0 0.0 reduce-scatter.7.cloned.1.call-update
  64.0 0.0 all-gather.6.cloned.1.call-start
  64.0 0.7 all-gather.6.cloned.1.call-update
  64.7 0.0 all-gather.4.cloned.1.call-start
  64.8 0.7 slice.21
  65.5 0.0 reduce-scatter.5.cloned.1.call-start
  65.5 4.4 fusion.34
  70.0 0.0 all-gather.8.cloned.1.call-start
  70.0 63.2 %reduce-scatter.7.cloned.1.call-done = f32[64,64]{1,0:T(8,128)} async-done(((f32[1024,64]{1,0:T(8,128)}), f32[64,64]{1,0:T(8,128)}) %reduce-scatter.7.cloned.1.call-update) | async-done | bytes 16400
  133.2 0.8 copy.59
  134.1 0.1 copy.45
  134.2 28.9 %all_gather.14 = bf16[1024,64]{1,0:T(8,128)(2,1)S(1)} all-gather(bf16[64,64]{1,0:T(8,128)(2,1)S(1)} %copy.45), channel_id=1, replica_groups=mesh['dp'=32,'mp'=16] {'mp'}, dimensions={0}, use_global_device_ids=true | all-gather | bytes 139264 | tf_op jit(solution)/shard_map/all_gather | solution.py:52
  163.0 43.7 %all-gather.6.cloned.1.call-done = bf16[1024,1024]{1,0:T(8,128)(2,1)} async-done(((bf16[64,1024]{1,0:T(8,128)(2,1)}), bf16[1024,1024]{1,0:T(8,128)(2,1)}) %all-gather.6.cloned.1.call-update) | async-done | bytes 2097168 | tf_op jit(solution)/shard_map/all_gather | solution.py:39
  206.7 1.3 convolution_convert_fusion.2
  208.0 71.2 %all-gather.4.cloned.1.call-done = bf16[8,64,1024]{1,2,0:T(8,128)(2,1)} async-done(((bf16[8,64,64]{1,2,0:T(8,128)(2,1)}), bf16[8,64,1024]{1,2,0:T(8,128)(2,1)}) %all-gather.4.cloned.1.call-update) | async-done | bytes 1048592 | tf_op jit(solution)/shard_map/all_gather | solution.py:40
  279.2 3.1 convolution_convert_fusion.3
  282.3 0.3 fusion.6
  282.6 0.1 pad_maximum_fusion.1
  282.7 1.0 convolution_convert_fusion
  283.6 0.9 copy.50
  284.6 39.2 %all_to_all.10 = bf16[32,576,64]{1,2,0:T(8,128)(2,1)S(1)} all-to-all(bf16[32,576,64]{1,2,0:T(8,128)(2,1)S(1)} %copy.50), channel_id=1, replica_groups=mesh['dp'=32,'mp'=16] {'dp'}, dimensions={0} | all-to-all | bytes 4718592 | tf_op jit(solution)/shard_map/all_to_all | solution.py:70
  323.8 1.8 fusion.3
  325.6 0.7 slice.23
  326.3 0.5 fusion.9
  326.8 0.1 copy-done.2
  326.9 1.1 copy-done.1
  328.0 2.3 fusion.2
  330.3 0.9 copy.52
  331.2 27.3 %reduce-scatter.5.cloned.1.call-done = f32[64,1024]{1,0:T(8,128)} async-done(((f32[1024,1024]{1,0:T(8,128)}), f32[64,1024]{1,0:T(8,128)}) %reduce-scatter.5.cloned.1.call-update) | async-done | bytes 262160 | tf_op jit(solution)/shard_map/reduce_scatter | solution.py:44
  358.5 1.9 fusion.7
  360.4 72.1 %all-gather.8.cloned.1.call-done = bf16[8,64,1024]{1,0,2:T(8,128)(2,1)} async-done(((bf16[8,64,64]{1,0,2:T(8,128)(2,1)}), bf16[8,64,1024]{1,0,2:T(8,128)(2,1)}) %all-gather.8.cloned.1.call-update) | async-done | bytes 1048592 | tf_op jit(solution)/shard_map/all_gather | solution.py:75
  432.5 3.3 copy.53
  (14 shorter events, 0.2 us)
Async XLA Ops:
  7.2 55.3 %copy-start = (bf16[1024,512]{1,0:T(8,128)(2,1)S(1)}, bf16[1024,512]{1,0:T(8,128)(2,1)}, u32[]{:S(2)}) copy-start(bf16[1024,512]{1,0:T(8,128)(2,1)} %param.7) | copy-start | bytes 3145732
  16.8 43.1 %all-to-all-start = ((bf16[32,576,64]{1,2,0:T(8,128)(2,1)}), bf16[32,576,64]{1,2,0:T(8,128)(2,1)}, u32[]{:S(2)}, u32[]{:S(2)}) async-start(bf16[32,576,64]{1,2,0:T(8,128)(2,1)} %broadcast_select_fusion), calls=%async_computation.1 | async-start | bytes 5242880 | tf_op jit(solution)/shard_map/all_to_all | solution.py:35
  26.9 106.3 %reduce-scatter.7.cloned.1.call-start = ((), (), s32[]{:S(2)}) async-start(), calls=%async_computation.8 | async-start | bytes 557056
  64.0 142.7 %all-gather.6.cloned.1.call-start = ((), (), s32[]{:S(2)}) async-start(), calls=%async_computation.6 | async-start | bytes 2228224 | tf_op jit(solution)/shard_map/all_gather | solution.py:39
  64.7 214.4 %all-gather.4.cloned.1.call-start = ((), (), s32[]{:S(2)}) async-start(), calls=%async_computation.5 | async-start | bytes 2228224 | tf_op jit(solution)/shard_map/all_gather | solution.py:40
  65.5 293.0 %reduce-scatter.5.cloned.1.call-start = ((), (), s32[]{:S(2)}) async-start(), calls=%async_computation.4 | async-start | bytes 4456448 | tf_op jit(solution)/shard_map/reduce_scatter | solution.py:44
  70.0 362.5 %all-gather.8.cloned.1.call-start = ((), (), s32[]{:S(2)}) async-start(), calls=%async_computation.7 | async-start | bytes 2228224 | tf_op jit(solution)/shard_map/all_gather | solution.py:75
  325.6 1.3 copy-start.2
  326.3 1.7 copy-start.1
Sparse Core Ops, SparseCore 0:
  64.1 69.0 reduce-scatter.6
  135.5 71.1 all-gather.5
  209.5 69.5 all-gather.3
  282.1 76.3 reduce-scatter.4
  361.2 71.2 all-gather.7

commit v3 on v2

--- a/solution.py
+++ b/solution.py
@@ -1,10 +1,81 @@
+import functools
+
 import jax
 import jax.numpy as jnp
 from jax import lax
+from jax.experimental import pallas as pl
+from jax.experimental.pallas import tpu as pltpu
 from jax.sharding import PartitionSpec as P
 
 RANK = 64
 BLOCK_ROWS = 128
+
+
+def _exchange_kernel(n, spread, *refs):
+    k = len(spread)
+    ins, outs = refs[:k], refs[k:2 * k]
+    send_sems, recv_sems, local_sem = refs[2 * k:]
+    me = lax.axis_index("mp")
+    row = lax.axis_index("dp")
+    barrier = pltpu.get_barrier_semaphore()
+    for d in range(1, n):
+        pl.semaphore_signal(
+            barrier, inc=1, device_id=(row, lax.rem(me + d, n)),
+            device_id_type=pl.DeviceIdType.MESH,
+        )
+    pl.semaphore_wait(barrier, n - 1)
+    copies = []
+    for a in range(k):
+        for d in range(1, n):
+            tgt = lax.rem(me + d, n)
+            src = ins[a].at[0] if spread[a] else ins[a].at[tgt]
+            copy = pltpu.make_async_remote_copy(
+                src_ref=src,
+                dst_ref=outs[a].at[me],
+                send_sem=send_sems.at[a, d],
+                recv_sem=recv_sems.at[a, d],
+                device_id=(row, tgt),
+                device_id_type=pl.DeviceIdType.MESH,
+            )
+            copy.start()
+            copies.append((a, d, copy))
+    for a in range(k):
+        src = ins[a].at[0] if spread[a] else ins[a].at[me]
+        local = pltpu.make_async_copy(src, outs[a].at[me], local_sem.at[a])
+        local.start()
+        local.wait()
+    for a, d, copy in copies:
+        copy.wait_send()
+        origin = lax.rem(me + n - d, n)
+        pltpu.make_async_remote_copy(
+            src_ref=outs[a].at[origin],
+            dst_ref=outs[a].at[origin],
+            send_sem=send_sems.at[a, d],
+            recv_sem=recv_sems.at[a, d],
+            device_id=(row, origin),
+            device_id_type=pl.DeviceIdType.MESH,
+        ).wait_recv()
+
+
+def mp_exchange(arrays, spread, n, tag):
+    outs = tuple(
+        jax.ShapeDtypeStruct((n,) + x.shape[1:], x.dtype) for x in arrays
+    )
+    moved = sum(x.size * x.dtype.itemsize for x in outs)
+    vmem = pl.BlockSpec(memory_space=pltpu.VMEM)
+    return pl.pallas_call(
+        functools.partial(_exchange_kernel, n, tuple(spread)),
+        out_shape=outs,
+        in_specs=[vmem] * len(arrays),
+        out_specs=tuple([vmem] * len(arrays)),
+        scratch_shapes=[
+            pltpu.SemaphoreType.DMA((len(arrays), n)),
+            pltpu.SemaphoreType.DMA((len(arrays), n)),
+            pltpu.SemaphoreType.DMA((len(arrays),)),
+        ],
+        compiler_params=pltpu.CompilerParams(collective_id=tag, has_side_effects=True),
+        cost_estimate=pl.CostEstimate(flops=0, transcendentals=0, bytes_accessed=2 * moved),
+    )(*arrays)
 
 
 def per_device(
@@ -37,7 +108,6 @@
     panel_a = mine_got[:, :width_dev]
     panel_b_cols = mine_got[:, width_dev:]
     cot_all = lax.all_gather(cotangent, "mp", axis=0, tiled=True)
-    panel_b = lax.all_gather(panel_b_cols, "mp", axis=2, tiled=True)
 
     token_blocks = tokens.reshape(blocks, BLOCK_ROWS, width_dev)
     partial_value = jnp.dot(tokens, value_weight, preferred_element_type=jnp.float32)
@@ -45,16 +115,23 @@
     down_part = jnp.einsum(
         "bnd,bdk->bnk", token_blocks, panel_a, preferred_element_type=jnp.float32
     )
-    first_row = my_part * own_rows
-    my_down = lax.psum_scatter(
-        down_part.reshape(rows, RANK), "mp", scatter_dimension=0, tiled=True
+    part_block = (jnp.arange(n_split, dtype=jnp.int32) * own_rows) // BLOCK_ROWS
+    to_parts = jnp.take(panel_b_cols, part_block, axis=0)
+    down_parts, up_parts = mp_exchange(
+        [down_part.reshape(n_split, own_rows, RANK), to_parts], [False, False], n_split, 0
+    )
+    my_down = jnp.sum(down_parts, axis=0).astype(jnp.bfloat16)
+    my_up = up_parts.transpose(1, 0, 2).reshape(RANK, kv_full)
+    my_back = jnp.einsum(
+        "nc,kc->nk", cotangent, my_up, preferred_element_type=jnp.float32
     ).astype(jnp.bfloat16)
-    down = lax.all_gather(my_down, "mp", axis=0, tiled=True)
+    down, back = mp_exchange([my_down[None], my_back[None]], [True, True], n_split, 1)
+    down = down.reshape(rows, RANK).astype(jnp.bfloat16)
+    back = back.reshape(blocks, BLOCK_ROWS, RANK)
+    lifted = jnp.dot(my_down, my_up, preferred_element_type=jnp.float32)
+    projected = (base + lifted).astype(jnp.bfloat16)
 
     cot_blocks = cot_all.reshape(blocks, BLOCK_ROWS, kv_full)
-    back = jnp.einsum(
-        "bnc,bkc->bnk", cot_blocks, panel_b, preferred_element_type=jnp.float32
-    ).astype(jnp.bfloat16)
     block_grad_a = jnp.einsum(
         "bnd,bnk->bdk", token_blocks, back, preferred_element_type=jnp.float32
     ).astype(jnp.bfloat16)
@@ -73,10 +150,6 @@
     ).astype(jnp.bfloat16)
     grad_down = grad_both[:, :width_dev]
     grad_up = lax.all_gather(grad_both[:, width_dev:], "mp", axis=2, tiled=True)
-
-    my_up = lax.dynamic_index_in_dim(panel_b, first_row // BLOCK_ROWS, 0, keepdims=False)
-    lifted = jnp.dot(my_down, my_up, preferred_element_type=jnp.float32)
-    projected = (base + lifted).astype(jnp.bfloat16)
 
     grad_base = jnp.einsum("nc,dc->nd", cot_all, value_weight, preferred_element_type=jnp.float32)
     through = jnp.einsum("bnk,bdk->bnd", back, panel_a, preferred_element_type=jnp.float32)

time: 443 us -> 360 us (0.81)
  waiting for transfers between devices: 311 us -> 169 us
  Pallas kernels: 0 us -> 83.8 us
  blocking collectives: 68.1 us -> 40.2 us
    pallas_call x0 -> x2, Pallas kernels: none -> 83.8 us  [mp_exchange(): pl.pallas_call(functools.partial(_exchange_kernel, n, tuple(spread)), out...]
    all_gather x1 -> x0, waiting for transfers between devices: 71.2 us -> none  [per_device(): panel_b = lax.all_gather(panel_b_cols, 'mp', axis=2, tiled=True)]
    unnamed x6 -> x3, waiting for transfers between devices: 63.9 us -> 0.71 us
    reduce_scatter x1, waiting for transfers between devices: 27.3 us -> 75.6 us  [per_device(): lax.psum_scatter(partial_value, 'mp', scatter_dimension=0, tiled=True)]
    all_gather x1, waiting for transfers between devices: 43.7 us -> 0.02 us  [per_device(): cot_all = lax.all_gather(cotangent, 'mp', axis=0, tiled=True)]
    all_gather x1 -> x0, blocking collectives: 28.9 us -> none  [per_device(): down = lax.all_gather(my_down, 'mp', axis=0, tiled=True)]
    all_gather x1, waiting for transfers between devices: 72.1 us -> 59.8 us  [per_device(): grad_up = lax.all_gather(grad_both[:, width_dev:], 'mp', axis=2, tiled=True)]
  transfers between devices with their start and end apart: 6 -> 4, of which waited for: 6 -> 3; matrix products, arithmetic and copies ran while one was open for 5% -> 9% of each run, Pallas kernels for 0% -> 23%
where the time goes in v3:
time: 360 us; the launch traced here: 359 us
  waiting for transfers between devices  169 us (47%)
  Pallas kernels  83.8 us (23%)
  blocking collectives  40.2 us (11%)
  local copies, waits for them, and re-layouts  17 us (5%)
  matrix products  15.6 us (4%)
  between operations  14 us (4%)
  starting transfers between devices  10.4 us (3%)
  other arithmetic  8.62 us (2%)
    pallas_call x2, Pallas kernels, mp_exchange(): pl.pallas_call(functools.partial(_exchange_kernel, n, tuple(spread)), out...  83.8 us
    reduce_scatter x1, waiting for transfers between devices, per_device(): lax.psum_scatter(partial_value, 'mp', scatter_dimension=0, tiled=True)  75.6 us
    all_gather x1, waiting for transfers between devices, per_device(): grad_up = lax.all_gather(grad_both[:, width_dev:], 'mp', axis=2, tiled=True)  59.8 us
    all_to_all x1, blocking collectives, per_device(): lax.all_to_all(send_g, 'dp', split_axis=0, concat_axis=0, tiled=True)  40.2 us
    all_to_all x1, waiting for transfers between devices, per_device(): lax.all_to_all(jnp.take(both, wanted, axis=0), 'dp', split_axis=0, concat...  32.8 us
    all_to_all x1, starting transfers between devices, per_device(): lax.all_to_all(jnp.take(both, wanted, axis=0), 'dp', split_axis=0, concat...  10.1 us
  transfers between devices with their start and end apart: 4, of which 3 were waited for; matrix products, arithmetic and copies ran while one was open for 9% of the time, Pallas kernels for 23%

profile of v3, /device:TPU:24, one launch (start us, length us, event | category | flops | bytes accessed | tf_op | source)
XLA Modules:
  0.0 358.7 jit_solution(12992193348275186767)
XLA Ops:
  7.2 0.0 all-gather.3.cloned.1.call-start
  7.2 0.7 all-gather.3.cloned.1.call-update
  7.9 1.0 constant_dynamic-slice_fusion
  8.9 0.1 copy.52
  9.1 0.9 select_reduce_fusion
  10.0 0.1 reduce_sum.32
  10.0 0.1 fusion.32
  10.2 0.1 fusion.15
  10.3 1.1 pad_maximum_fusion
  11.4 2.4 gather_fusion
  13.8 3.6 broadcast_select_fusion
  17.4 10.1 %all-to-all-start = ((bf16[32,576,64]{1,2,0:T(8,128)(2,1)}), bf16[32,576,64]{1,2,0:T(8,128)(2,1)}, u32[]{:S(2)}, u32[]{:S(2)}) async-start(bf16[32,576,64]{1,2,0:T(8,128)(2,1)} %broadcast_select_fusion), calls=%async_computation.1 | async-start | bytes 5242880 | tf_op jit(solution)/shard_map/all_to_all | solution.py:106
  27.5 0.0 all-gather.5.cloned.1.call-start
  27.7 32.8 %all-to-all-done = bf16[32,576,64]{1,2,0:T(8,128)(2,1)} async-done(((bf16[32,576,64]{1,2,0:T(8,128)(2,1)}), bf16[32,576,64]{1,2,0:T(8,128)(2,1)}, u32[]{:S(2)}, u32[]{:S(2)}) %all-to-all-start) | async-done | bytes 2359328 | tf_op jit(solution)/shard_map/all_to_all | solution.py:106
  60.5 2.4 gather_fusion.1
  62.9 0.1 broadcast_select_fusion.1
  63.1 0.5 convolution_bitcast_fusion
  63.6 1.0 copy.53
  64.6 0.1 copy.54
  64.7 0.6 gather_fusion.2
  65.3 0.8 broadcast_select_fusion.2.refs_1_
  66.1 50.4 %shard_map.102 = (f32[16,64,64]{2,1,0:T(8,128)}, bf16[16,64,64]{2,1,0:T(8,128)(2,1)}) custom-call(f32[16,64,64]{2,1,0:T(8,128)} %bitcast.55, bf16[16,64,64]{2,1,0:T(8,128)(2,1)} %broadcast_select_fusion.2.refs_1_), custom_call_target="tpu_custom_call" | custom-call | bytes 786432 | tf_op jit(solution)/shard_map/pallas_call | solution.py:66
  116.5 1.1 copy.55
  117.6 0.2 reshape.164
  117.8 1.7 reduce_sum.35
  119.5 0.8 fusion.8.refs_1_
  120.3 33.4 %shard_map.103 = (bf16[16,64,64]{2,1,0:T(8,128)(2,1)}, bf16[16,64,64]{2,1,0:T(8,128)(2,1)}) custom-call(bf16[1,64,64]{2,1,0:T(8,128)(2,1)} %bitcast.60, bf16[1,64,64]{2,1,0:T(8,128)(2,1)} %fusion.8.refs_1_), custom_call_target="tpu_custom_call" | custom-call | bytes 524288 | tf_op jit(solution)/shard_map/pallas_call | solution.py:66
  153.7 1.3 fusion.6
  155.0 0.0 all-gather.3.cloned.1.call-done
  155.1 1.4 convolution_convert_fusion.2
  156.5 0.1 pad_maximum_fusion.1
  156.6 1.0 convolution_convert_fusion
  157.5 0.9 copy.62
  158.4 40.2 %all_to_all.10 = bf16[32,576,64]{1,2,0:T(8,128)(2,1)S(1)} all-to-all(bf16[32,576,64]{1,2,0:T(8,128)(2,1)S(1)} %copy.62), channel_id=1, replica_groups=mesh['dp'=32,'mp'=16] {'dp'}, dimensions={0} | all-to-all | bytes 4718592 | tf_op jit(solution)/shard_map/all_to_all | solution.py:147
  198.7 1.8 fusion.3
  200.4 0.7 slice.25
  201.1 0.0 all-gather.5.cloned.1.call-update
  201.1 0.2 reduce-scatter.2.cloned.1.call-start
  201.4 3.3 fusion.34
  204.7 0.9 copy-done.1
  205.6 0.4 fusion.10
  206.0 1.2 copy-done.4
  207.2 3.5 fusion.2
  210.7 0.9 copy.64
  211.7 59.8 %all-gather.5.cloned.1.call-done = bf16[8,64,1024]{1,0,2:T(8,128)(2,1)} async-done(((bf16[8,64,64]{1,0,2:T(8,128)(2,1)}), bf16[8,64,1024]{1,0,2:T(8,128)(2,1)}) %all-gather.5.cloned.1.call-update) | async-done | bytes 1048592 | tf_op jit(solution)/shard_map/all_gather | solution.py:152
  271.5 3.3 copy.65
  274.8 75.6 %reduce-scatter.2.cloned.1.call-done = f32[64,1024]{1,0:T(8,128)} async-done(((f32[1024,1024]{1,0:T(8,128)}), f32[64,1024]{1,0:T(8,128)}) %reduce-scatter.2.cloned.1.call-update) | async-done | bytes 262160 | tf_op jit(solution)/shard_map/reduce_scatter | solution.py:114
  350.4 1.8 fusion.7
  (22 shorter events, 0.2 us)
Async XLA Ops:
  7.2 55.9 %copy-start = (bf16[1024,512]{1,0:T(8,128)(2,1)S(1)}, bf16[1024,512]{1,0:T(8,128)(2,1)}, u32[]{:S(2)}) copy-start(bf16[1024,512]{1,0:T(8,128)(2,1)} %param.7) | copy-start | bytes 3145732
  7.2 147.9 %all-gather.3.cloned.1.call-start = ((), (), s32[]{:S(2)}) async-start(), calls=%async_computation.4 | async-start | bytes 2228224 | tf_op jit(solution)/shard_map/all_gather | solution.py:110
  17.4 43.1 %all-to-all-start = ((bf16[32,576,64]{1,2,0:T(8,128)(2,1)}), bf16[32,576,64]{1,2,0:T(8,128)(2,1)}, u32[]{:S(2)}, u32[]{:S(2)}) async-start(bf16[32,576,64]{1,2,0:T(8,128)(2,1)} %broadcast_select_fusion), calls=%async_computation.1 | async-start | bytes 5242880 | tf_op jit(solution)/shard_map/all_to_all | solution.py:106
  27.5 244.0 %all-gather.5.cloned.1.call-start = ((), (), s32[]{:S(2)}) async-start(), calls=%async_computation.5 | async-start | bytes 2228224 | tf_op jit(solution)/shard_map/all_gather | solution.py:152
  63.6 55.9 %copy-start.2 = (bf16[64,1024]{1,0:T(8,128)(2,1)S(1)}, bf16[64,1024]{1,0:T(8,128)(2,1)}, u32[]{:S(2)}) copy-start(bf16[64,1024]{1,0:T(8,128)(2,1)} %param.11) | copy-start | bytes 393220
  198.7 2.7 copy-start.5
  201.1 149.3 %reduce-scatter.2.cloned.1.call-start = ((), (), s32[]{:S(2)}) async-start(), calls=%async_computation.3 | async-start | bytes 4456448 | tf_op jit(solution)/shard_map/reduce_scatter | solution.py:114
  204.7 0.9 copy-start.1
  205.6 1.6 copy-start.4
  210.7 139.7 %copy-start.3 = (bf16[64,64]{1,0:T(8,128)(2,1)S(1)}, bf16[64,64]{1,0:T(8,128)(2,1)}, u32[]{:S(2)}) copy-start(bf16[64,64]{1,0:T(8,128)(2,1)} %reduce_sum.35) | copy-start | bytes 24580
Sparse Core Ops, SparseCore 0:
  10.1 91.8 all-gather.2
  201.3 70.2 all-gather.4
  274.4 75.9 reduce-scatter.1

commit v4 on v3

--- a/solution.py
+++ b/solution.py
@@ -107,7 +107,16 @@
     mine_got = jnp.take(got, my_owner, axis=0)
     panel_a = mine_got[:, :width_dev]
     panel_b_cols = mine_got[:, width_dev:]
-    cot_all = lax.all_gather(cotangent, "mp", axis=0, tiled=True)
+    ahead, behind = [cotangent], [cotangent]
+    to_right = [(i, (i + 1) % n_split) for i in range(n_split)]
+    to_left = [(i, (i - 1) % n_split) for i in range(n_split)]
+    for step in range(n_split // 2):
+        ahead.append(lax.ppermute(ahead[-1], "mp", to_right))
+        if step < n_split // 2 - 1:
+            behind.append(lax.ppermute(behind[-1], "mp", to_left))
+    by_offset = [cotangent] + behind[1:] + ahead[:0:-1]
+    stacked = jnp.concatenate(by_offset + by_offset, axis=0)
+    cot_all = lax.dynamic_slice_in_dim(stacked, (n_split - my_part) * own_rows, rows, 0)
 
     token_blocks = tokens.reshape(blocks, BLOCK_ROWS, width_dev)
     partial_value = jnp.dot(tokens, value_weight, preferred_element_type=jnp.float32)
@@ -125,6 +134,7 @@
     my_back = jnp.einsum(
         "nc,kc->nk", cotangent, my_up, preferred_element_type=jnp.float32
     ).astype(jnp.bfloat16)
+    base, my_down, my_back = lax.optimization_barrier((base, my_down, my_back))
     down, back = mp_exchange([my_down[None], my_back[None]], [True, True], n_split, 1)
     down = down.reshape(rows, RANK).astype(jnp.bfloat16)
     back = back.reshape(blocks, BLOCK_ROWS, RANK)
@@ -132,24 +142,32 @@
     projected = (base + lifted).astype(jnp.bfloat16)
 
     cot_blocks = cot_all.reshape(blocks, BLOCK_ROWS, kv_full)
-    block_grad_a = jnp.einsum(
-        "bnd,bnk->bdk", token_blocks, back, preferred_element_type=jnp.float32
-    ).astype(jnp.bfloat16)
+    select_bf = select_mask.astype(jnp.bfloat16)
+    pick_bf = pick_mask.astype(jnp.bfloat16)
     cot_share = lax.dynamic_slice_in_dim(cot_blocks, my_part * kv_part, kv_part, 2)
     block_grad_b = jnp.einsum(
         "bnk,bnc->bkc", down.reshape(blocks, BLOCK_ROWS, RANK), cot_share,
         preferred_element_type=jnp.float32,
     ).astype(jnp.bfloat16)
-    grads = jnp.concatenate([block_grad_a, block_grad_b], axis=1)
-    send_g = jnp.einsum(
-        "bo,bdk->odk", select_mask.astype(jnp.bfloat16), grads, preferred_element_type=jnp.float32
+    send_gb = jnp.einsum(
+        "bo,bkc->okc", select_bf, block_grad_b, preferred_element_type=jnp.float32
     ).astype(jnp.bfloat16)
-    recv_g = lax.all_to_all(send_g, "dp", split_axis=0, concat_axis=0, tiled=True)
-    grad_both = jnp.einsum(
-        "ra,rdk->adk", pick_mask.astype(jnp.bfloat16), recv_g, preferred_element_type=jnp.float32
+    recv_gb = lax.all_to_all(send_gb, "dp", split_axis=0, concat_axis=0, tiled=True)
+    grad_share = jnp.einsum(
+        "ra,rkc->akc", pick_bf, recv_gb, preferred_element_type=jnp.float32
     ).astype(jnp.bfloat16)
-    grad_down = grad_both[:, :width_dev]
-    grad_up = lax.all_gather(grad_both[:, width_dev:], "mp", axis=2, tiled=True)
+    grad_up = lax.all_gather(grad_share, "mp", axis=2, tiled=True)
+
+    block_grad_a = jnp.einsum(
+        "bnd,bnk->bdk", token_blocks, back, preferred_element_type=jnp.float32
+    ).astype(jnp.bfloat16)
+    send_ga = jnp.einsum(
+        "bo,bdk->odk", select_bf, block_grad_a, preferred_element_type=jnp.float32
+    ).astype(jnp.bfloat16)
+    recv_ga = lax.all_to_all(send_ga, "dp", split_axis=0, concat_axis=0, tiled=True)
+    grad_down = jnp.einsum(
+        "ra,rdk->adk", pick_bf, recv_ga, preferred_element_type=jnp.float32
+    ).astype(jnp.bfloat16)
 
     grad_base = jnp.einsum("nc,dc->nd", cot_all, value_weight, preferred_element_type=jnp.float32)
     through = jnp.einsum("bnk,bdk->bnd", back, panel_a, preferred_element_type=jnp.float32)

time: 360 us -> 320 us (0.89)
  waiting for transfers between devices: 169 us -> 79.3 us
  starting transfers between devices: 10.4 us -> 82.1 us
  blocking collectives: 40.2 us -> 0 us
  local copies, waits for them, and re-layouts: 17 us -> 45.5 us
  Pallas kernels: 83.8 us -> 70.2 us
  matrix products: 15.6 us -> 19.7 us
    reduce_scatter x1, waiting for transfers between devices: 75.6 us -> 0.01 us  [per_device(): lax.psum_scatter(partial_value, 'mp', scatter_dimension=0, tiled=True)]
    ppermute x0 -> x15, starting transfers between devices: none -> 59.4 us  [the longest x7 44.1 us: per_device(): behind.append(lax.ppermute(behind[-1], 'mp', to_left))]
    all_to_all x1 -> x0, blocking collectives: 40.2 us -> none  [per_device(): lax.all_to_all(send_g, 'dp', split_axis=0, concat_axis=0, tiled=True)]
    all_to_all x1, waiting for transfers between devices: 32.8 us -> 0.01 us  [per_device(): lax.all_to_all(jnp.take(both, wanted, axis=0), 'dp', split_axis=0, concat...]
    unnamed x14 -> x55, local copies, waits for them, and re-layouts: 6.38 us -> 29.1 us
    all_to_all x0 -> x2, waiting for transfers between devices: none -> 18.3 us  [the longest x1 16.1 us: per_device(): lax.all_to_all(send_ga, 'dp', split_axis=0, concat_axis=0, tiled=True)]
    ppermute x0 -> x15, waiting for transfers between devices: none -> 18.2 us  [the longest x7 12 us: per_device(): behind.append(lax.ppermute(behind[-1], 'mp', to_left))]
    all_gather x2 -> x1, waiting for transfers between devices: 59.9 us -> 42.9 us  [per_device(): grad_up = lax.all_gather(grad_share, 'mp', axis=2, tiled=True)]
  transfers between devices with their start and end apart: 4 -> 20, of which waited for: 3 -> 9; matrix products, arithmetic and copies ran while one was open for 9% -> 19% of each run, Pallas kernels for 23% -> 13%
where the time goes in v4:
time: 320 us; the launch traced here: 319 us
  starting transfers between devices  82.1 us (26%)
  waiting for transfers between devices  79.3 us (25%)
  Pallas kernels  70.2 us (22%)
  local copies, waits for them, and re-layouts  45.5 us (14%)
  matrix products  19.7 us (6%)
  between operations  14.5 us (5%)
  other arithmetic  7.44 us (2%)
    pallas_call x2, Pallas kernels, mp_exchange(): pl.pallas_call(functools.partial(_exchange_kernel, n, tuple(spread)), out...  70.2 us
    ppermute x7, starting transfers between devices, per_device(): behind.append(lax.ppermute(behind[-1], 'mp', to_left))  44.1 us
    all_gather x1, waiting for transfers between devices, per_device(): grad_up = lax.all_gather(grad_share, 'mp', axis=2, tiled=True)  42.9 us
    unnamed x55, local copies, waits for them, and re-layouts  29.1 us
    all_to_all x1, waiting for transfers between devices, per_device(): lax.all_to_all(send_ga, 'dp', split_axis=0, concat_axis=0, tiled=True)  16.1 us
    ppermute x8, starting transfers between devices, per_device(): ahead.append(lax.ppermute(ahead[-1], 'mp', to_right))  15.3 us
    ppermute x7, waiting for transfers between devices, per_device(): behind.append(lax.ppermute(behind[-1], 'mp', to_left))  12 us
    all_to_all x1, starting transfers between devices, per_device(): lax.all_to_all(send_gb, 'dp', split_axis=0, concat_axis=0, tiled=True)  8.91 us
  transfers between devices with their start and end apart: 20, of which 9 were waited for; matrix products, arithmetic and copies ran while one was open for 19% of the time, Pallas kernels for 13%

profile of v4, /device:TPU:24, one launch (start us, length us, event | category | flops | bytes accessed | tf_op | source)
XLA Modules:
  0.0 318.8 jit_solution(4882060150563998131)
XLA Ops:
  7.2 1.2 copy-done
  8.4 4.4 %fusion.40 = f32[1024,1024]{1,0:T(8,128)} fusion(bf16[1024,512]{1,0:T(8,128)(2,1)S(1)} %copy-done, bf16[512,1024]{1,0:T(8,128)(2,1)} %param.8), kind=kOutput, calls=%fused_computation.115 | convolution fusion | flops 1073741824 | bytes 6291456 | tf_op jit(solution)/shard_map/dot_general | solution.py:122
  13.7 11.4 %collective-permute-start = (bf16[64,1024]{1,0:T(8,128)(2,1)S(1)}, bf16[64,1024]{1,0:T(8,128)(2,1)S(1)}, u32[]{:S(2)}, u32[]{:S(2)}) collective-permute-start(bf16[64,1024]{1,0:T(8,128)(2,1)S(1)} %copy-done.2), channel_id=1, source_target_pairs={{0,15},{1,0},{2,1},{3,2},{4,3},{5,4},{6,5},{7,6},{8,7},{9,8},{10,9... | collective-permute-start | bytes 393224 | tf_op jit(solution)/shard_map/ppermute | solution.py:116
  25.1 1.9 collective-permute-start.7
  29.4 2.5 gather_fusion
  31.9 1.3 collective-permute-done.7
  33.2 1.9 collective-permute-start.8
  35.1 3.7 %broadcast_select_fusion = bf16[32,576,64]{1,2,0:T(8,128)(2,1)} fusion(bf16[32,576,64]{1,2,0:T(8,128)(2,1)} %gather_fusion, pred[32]{0:T(512)(128)(4,1)S(1)} %compare_and_fusion.1), kind=kLoop, calls=%fused_computation.3 | loop fusion | flops 1179648 | bytes 4718624 | tf_op jit(solution)/shard_map/jit(_take)/select_n | solution.py:106
  38.8 7.4 %all-to-all-start = ((bf16[32,576,64]{1,2,0:T(8,128)(2,1)}), bf16[32,576,64]{1,2,0:T(8,128)(2,1)}, u32[]{:S(2)}, u32[]{:S(2)}) async-start(bf16[32,576,64]{1,2,0:T(8,128)(2,1)} %broadcast_select_fusion), calls=%async_computation.1 | async-start | bytes 5242880 | tf_op jit(solution)/shard_map/all_to_all | solution.py:106
  46.2 5.1 %collective-permute-start.1 = (bf16[64,1024]{1,0:T(8,128)(2,1)S(1)}, bf16[64,1024]{1,0:T(8,128)(2,1)S(1)}, u32[]{:S(2)}, u32[]{:S(2)}) collective-permute-start(bf16[64,1024]{1,0:T(8,128)(2,1)S(1)} %collective-permute-done), channel_id=1, source_target_pairs={{0,15},{1,0},{2,1},{3,2},{4,3},{5,4},{6,5},{7,6},{8,7},{9,8},{10,9... | collective-permute-start | bytes 393224 | tf_op jit(solution)/shard_map/ppermute | solution.py:116
  52.0 1.9 collective-permute-start.9
  54.0 3.6 %collective-permute-done.1 = bf16[64,1024]{1,0:T(8,128)(2,1)S(1)} collective-permute-done((bf16[64,1024]{1,0:T(8,128)(2,1)S(1)}, bf16[64,1024]{1,0:T(8,128)(2,1)S(1)}, u32[]{:S(2)}, u32[]{:S(2)}) %collective-permute-start.1) | collective-permute-done | bytes 131104 | tf_op jit(solution)/shard_map/ppermute | solution.py:116
  57.6 5.6 %collective-permute-start.2 = (bf16[64,1024]{1,0:T(8,128)(2,1)S(1)}, bf16[64,1024]{1,0:T(8,128)(2,1)S(1)}, u32[]{:S(2)}, u32[]{:S(2)}) collective-permute-start(bf16[64,1024]{1,0:T(8,128)(2,1)S(1)} %collective-permute-done.1), channel_id=1, source_target_pairs={{0,15},{1,0},{2,1},{3,2},{4,3},{5,4},{6,5},{7,6},{8,7},{9,8},{10,9... | collective-permute-start | bytes 393224 | tf_op jit(solution)/shard_map/ppermute | solution.py:116
  63.2 1.9 collective-permute-start.10
  65.1 3.5 %collective-permute-done.2 = bf16[64,1024]{1,0:T(8,128)(2,1)S(1)} collective-permute-done((bf16[64,1024]{1,0:T(8,128)(2,1)S(1)}, bf16[64,1024]{1,0:T(8,128)(2,1)S(1)}, u32[]{:S(2)}, u32[]{:S(2)}) %collective-permute-start.2) | collective-permute-done | bytes 131104 | tf_op jit(solution)/shard_map/ppermute | solution.py:116
  68.6 5.6 %collective-permute-start.3 = (bf16[64,1024]{1,0:T(8,128)(2,1)S(1)}, bf16[64,1024]{1,0:T(8,128)(2,1)S(1)}, u32[]{:S(2)}, u32[]{:S(2)}) collective-permute-start(bf16[64,1024]{1,0:T(8,128)(2,1)S(1)} %collective-permute-done.2), channel_id=1, source_target_pairs={{0,15},{1,0},{2,1},{3,2},{4,3},{5,4},{6,5},{7,6},{8,7},{9,8},{10,9... | collective-permute-start | bytes 393224 | tf_op jit(solution)/shard_map/ppermute | solution.py:116
  74.3 1.9 collective-permute-start.11
  76.2 3.2 collective-permute-done.3
  79.4 5.6 %collective-permute-start.4 = (bf16[64,1024]{1,0:T(8,128)(2,1)S(1)}, bf16[64,1024]{1,0:T(8,128)(2,1)S(1)}, u32[]{:S(2)}, u32[]{:S(2)}) collective-permute-start(bf16[64,1024]{1,0:T(8,128)(2,1)S(1)} %collective-permute-done.3), channel_id=1, source_target_pairs={{0,15},{1,0},{2,1},{3,2},{4,3},{5,4},{6,5},{7,6},{8,7},{9,8},{10,9... | collective-permute-start | bytes 393224 | tf_op jit(solution)/shard_map/ppermute | solution.py:116
  85.6 1.9 collective-permute-start.12
  88.2 1.7 collective-permute-done.4
  90.0 5.6 %collective-permute-start.5 = (bf16[64,1024]{1,0:T(8,128)(2,1)S(1)}, bf16[64,1024]{1,0:T(8,128)(2,1)S(1)}, u32[]{:S(2)}, u32[]{:S(2)}) collective-permute-start(bf16[64,1024]{1,0:T(8,128)(2,1)S(1)} %collective-permute-done.4), channel_id=1, source_target_pairs={{0,15},{1,0},{2,1},{3,2},{4,3},{5,4},{6,5},{7,6},{8,7},{9,8},{10,9... | collective-permute-start | bytes 393224 | tf_op jit(solution)/shard_map/ppermute | solution.py:116
  96.2 1.9 collective-permute-start.13
  98.8 5.3 %collective-permute-start.6 = (bf16[64,1024]{1,0:T(8,128)(2,1)S(1)}, bf16[64,1024]{1,0:T(8,128)(2,1)S(1)}, u32[]{:S(2)}, u32[]{:S(2)}) collective-permute-start(bf16[64,1024]{1,0:T(8,128)(2,1)S(1)} %collective-permute-done.5), channel_id=1, source_target_pairs={{0,15},{1,0},{2,1},{3,2},{4,3},{5,4},{6,5},{7,6},{8,7},{9,8},{10,9... | collective-permute-start | bytes 393224 | tf_op jit(solution)/shard_map/ppermute | solution.py:116
  104.7 1.9 collective-permute-start.14
  108.0 4.8 %collective-permute-done.14 = bf16[64,1024]{1,0:T(8,128)(2,1)S(1)} collective-permute-done((bf16[64,1024]{1,0:T(8,128)(2,1)S(1)}, bf16[64,1024]{1,0:T(8,128)(2,1)S(1)}, u32[]{:S(2)}, u32[]{:S(2)}) %collective-permute-start.14) | collective-permute-done | bytes 131104 | tf_op jit(solution)/shard_map/ppermute | solution.py:114
  128.6 3.1 constant_dynamic-slice_fusion
  131.7 2.4 gather_fusion.1
  137.3 41.3 %shard_map.102 = (f32[16,64,64]{2,1,0:T(8,128)}, bf16[16,64,64]{2,1,0:T(8,128)(2,1)}) custom-call(f32[16,64,64]{2,1,0:T(8,128)} %bitcast.55, bf16[16,64,64]{2,1,0:T(8,128)(2,1)} %broadcast_select_fusion.2.refs_1_), custom_call_target="tpu_custom_call" | custom-call | bytes 786432 | tf_op jit(solution)/shard_map/pallas_call | solution.py:66
  178.6 1.1 copy.63
  179.9 1.7 reduce_sum.35
  182.4 29.0 %shard_map.103 = (bf16[16,64,64]{2,1,0:T(8,128)(2,1)}, bf16[16,64,64]{2,1,0:T(8,128)(2,1)}) custom-call(bf16[1,64,64]{2,1,0:T(8,128)(2,1)} %bitcast.60, bf16[1,64,64]{2,1,0:T(8,128)(2,1)} %bitcast.61), custom_call_target="tpu_custom_call" | custom-call | bytes 524288 | tf_op jit(solution)/shard_map/pallas_call | solution.py:66
  211.4 1.4 convolution_convert_fusion.3
  213.4 1.1 reshape.186
  214.5 8.9 %all-to-all-start.2 = ((bf16[32,2,2048]{2,1,0:T(2,128)(2,1)}), bf16[32,2,2048]{2,1,0:T(2,128)(2,1)S(1)}, u32[]{:S(2)}, u32[]{:S(2)}) async-start(bf16[32,2,2048]{2,1,0:T(2,128)(2,1)} %reshape.186), calls=%async_computation.3 | async-start | bytes 524288 | tf_op jit(solution)/shard_map/all_to_all | solution.py:155
  223.4 1.3 fusion.6
  225.6 2.5 copy.68
  228.1 2.2 all-to-all-done.2
  230.3 6.1 %all-to-all-start.1 = ((bf16[32,512,64]{1,2,0:T(8,128)(2,1)}), bf16[32,512,64]{1,2,0:T(8,128)(2,1)S(1)}, u32[]{:S(2)}, u32[]{:S(2)}) async-start(bf16[32,512,64]{1,2,0:T(8,128)(2,1)} %copy.68), calls=%async_computation.2 | async-start | bytes 4194304 | tf_op jit(solution)/shard_map/all_to_all | solution.py:167
  236.6 1.2 reshape.187
  237.8 1.4 convolution_convert_fusion.4
  240.1 1.8 fusion.7
  241.8 1.5 fusion.11
  243.4 4.1 %fusion = bf16[1024,512]{1,0:T(8,128)(2,1)} fusion(f32[8,128,512]{2,1,0:T(8,128)S(1)} %fusion.11, bf16[1024,1024]{1,0:T(8,128)(2,1)} %constant_dynamic-slice_fusion, bf16[512,1024]{1,0:T(8,128)(2,1)} %param.8), kind=kOutput, calls=%fused_computation.5 | convolution fusion | flops 1074790400 | bytes 6291456 | tf_op jit(solution)/shard_map/nc,dc->nd/dot_general | solution.py:172
  247.5 16.1 %all-to-all-done.1 = bf16[32,512,64]{1,2,0:T(8,128)(2,1)S(1)} async-done(((bf16[32,512,64]{1,2,0:T(8,128)(2,1)}), bf16[32,512,64]{1,2,0:T(8,128)(2,1)S(1)}, u32[]{:S(2)}, u32[]{:S(2)}) %all-to-all-start.1) | async-done | bytes 2097184 | tf_op jit(solution)/shard_map/all_to_all | solution.py:167
  263.6 1.2 fusion.3
  265.8 42.9 %all-gather.2.cloned.1.call-done = bf16[8,64,1024]{1,0,2:T(8,128)(2,1)} async-done(((bf16[8,64,64]{1,0,2:T(8,128)(2,1)}), bf16[8,64,1024]{1,0,2:T(8,128)(2,1)}) %all-gather.2.cloned.1.call-update) | async-done | bytes 1048592 | tf_op jit(solution)/shard_map/all_gather | solution.py:159
  308.6 3.3 %copy.77 = bf16[8,64,1024]{2,1,0:T(8,128)(2,1)} copy(bf16[8,64,1024]{1,0,2:T(8,128)(2,1)} %all-gather.2.cloned.1.call-done) | data formatting | bytes 2097152
  (95 shorter events, 32.0 us)
Async XLA Ops:
  7.2 1.2 copy-start
  7.2 175.2 %reduce-scatter.2.cloned.1.call-start = ((), (), s32[]{:S(2)}) async-start(), calls=%async_computation.4 | async-start | bytes 4456448 | tf_op jit(solution)/shard_map/reduce_scatter | solution.py:123
  12.8 0.9 copy-start.2
  12.8 15.4 %copy-start.8 = (s32[256]{0:T(256)S(1)}, s32[256]{0:T(256)}, u32[]{:S(2)}) copy-start(s32[256]{0:T(256)} %param.13) | copy-start | bytes 3076
  12.8 15.4 %copy-start.9 = (s32[256]{0:T(256)S(1)}, s32[256]{0:T(256)}, u32[]{:S(2)}) copy-start(s32[256]{0:T(256)} %param.12) | copy-start | bytes 3076
  12.8 16.5 %copy-start.3 = (bf16[8,512,64]{1,2,0:T(8,128)(2,1)S(1)}, bf16[8,512,64]{1,2,0:T(8,128)(2,1)}, u32[]{:S(2)}) copy-start(bf16[8,512,64]{1,2,0:T(8,128)(2,1)} %param.9) | copy-start | bytes 1572868
  13.7 32.5 %collective-permute-start = (bf16[64,1024]{1,0:T(8,128)(2,1)S(1)}, bf16[64,1024]{1,0:T(8,128)(2,1)S(1)}, u32[]{:S(2)}, u32[]{:S(2)}) collective-permute-start(bf16[64,1024]{1,0:T(8,128)(2,1)S(1)} %copy-done.2), channel_id=1, source_target_pairs={{0,15},{1,0},{2,1},{3,2},{4,3},{5,4},{6,5},{7,6},{8,7},{9,8},{10,9... | collective-permute-start | bytes 393224 | tf_op jit(solution)/shard_map/ppermute | solution.py:116
  25.1 8.1 %collective-permute-start.7 = (bf16[64,1024]{1,0:T(8,128)(2,1)S(1)}, bf16[64,1024]{1,0:T(8,128)(2,1)S(1)}, u32[]{:S(2)}, u32[]{:S(2)}) collective-permute-start(bf16[64,1024]{1,0:T(8,128)(2,1)S(1)} %copy-done.2), channel_id=1, source_target_pairs={{0,1},{1,2},{2,3},{3,4},{4,5},{5,6},{6,7},{7,8},{8,9},{9,10},{10,1... | collective-permute-start | bytes 393224 | tf_op jit(solution)/shard_map/ppermute | solution.py:114
  29.3 2.6 copy-start.6
  33.2 18.8 %collective-permute-start.8 = (bf16[64,1024]{1,0:T(8,128)(2,1)S(1)}, bf16[64,1024]{1,0:T(8,128)(2,1)S(1)}, u32[]{:S(2)}, u32[]{:S(2)}) collective-permute-start(bf16[64,1024]{1,0:T(8,128)(2,1)S(1)} %collective-permute-done.7), channel_id=1, source_target_pairs={{0,1},{1,2},{2,3},{3,4},{4,5},{5,6},{6,7},{7,8},{8,9},{9,10},{10,1... | collective-permute-start | bytes 393224 | tf_op jit(solution)/shard_map/ppermute | solution.py:114
  38.8 92.9 %all-to-all-start = ((bf16[32,576,64]{1,2,0:T(8,128)(2,1)}), bf16[32,576,64]{1,2,0:T(8,128)(2,1)}, u32[]{:S(2)}, u32[]{:S(2)}) async-start(bf16[32,576,64]{1,2,0:T(8,128)(2,1)} %broadcast_select_fusion), calls=%async_computation.1 | async-start | bytes 5242880 | tf_op jit(solution)/shard_map/all_to_all | solution.py:106
  46.2 11.3 %collective-permute-start.1 = (bf16[64,1024]{1,0:T(8,128)(2,1)S(1)}, bf16[64,1024]{1,0:T(8,128)(2,1)S(1)}, u32[]{:S(2)}, u32[]{:S(2)}) collective-permute-start(bf16[64,1024]{1,0:T(8,128)(2,1)S(1)} %collective-permute-done), channel_id=1, source_target_pairs={{0,15},{1,0},{2,1},{3,2},{4,3},{5,4},{6,5},{7,6},{8,7},{9,8},{10,9... | collective-permute-start | bytes 393224 | tf_op jit(solution)/shard_map/ppermute | solution.py:116
  52.0 11.1 %collective-permute-start.9 = (bf16[64,1024]{1,0:T(8,128)(2,1)S(1)}, bf16[64,1024]{1,0:T(8,128)(2,1)S(1)}, u32[]{:S(2)}, u32[]{:S(2)}) collective-permute-start(bf16[64,1024]{1,0:T(8,128)(2,1)S(1)} %collective-permute-done.8), channel_id=1, source_target_pairs={{0,1},{1,2},{2,3},{3,4},{4,5},{5,6},{6,7},{7,8},{8,9},{9,10},{10,1... | collective-permute-start | bytes 393224 | tf_op jit(solution)/shard_map/ppermute | solution.py:114
  57.6 11.1 %collective-permute-start.2 = (bf16[64,1024]{1,0:T(8,128)(2,1)S(1)}, bf16[64,1024]{1,0:T(8,128)(2,1)S(1)}, u32[]{:S(2)}, u32[]{:S(2)}) collective-permute-start(bf16[64,1024]{1,0:T(8,128)(2,1)S(1)} %collective-permute-done.1), channel_id=1, source_target_pairs={{0,15},{1,0},{2,1},{3,2},{4,3},{5,4},{6,5},{7,6},{8,7},{9,8},{10,9... | collective-permute-start | bytes 393224 | tf_op jit(solution)/shard_map/ppermute | solution.py:116
  63.2 11.1 %collective-permute-start.10 = (bf16[64,1024]{1,0:T(8,128)(2,1)S(1)}, bf16[64,1024]{1,0:T(8,128)(2,1)S(1)}, u32[]{:S(2)}, u32[]{:S(2)}) collective-permute-start(bf16[64,1024]{1,0:T(8,128)(2,1)S(1)} %collective-permute-done.9), channel_id=1, source_target_pairs={{0,1},{1,2},{2,3},{3,4},{4,5},{5,6},{6,7},{7,8},{8,9},{9,10},{10,1... | collective-permute-start | bytes 393224 | tf_op jit(solution)/shard_map/ppermute | solution.py:114
  68.6 10.8 %collective-permute-start.3 = (bf16[64,1024]{1,0:T(8,128)(2,1)S(1)}, bf16[64,1024]{1,0:T(8,128)(2,1)S(1)}, u32[]{:S(2)}, u32[]{:S(2)}) collective-permute-start(bf16[64,1024]{1,0:T(8,128)(2,1)S(1)} %collective-permute-done.2), channel_id=1, source_target_pairs={{0,15},{1,0},{2,1},{3,2},{4,3},{5,4},{6,5},{7,6},{8,7},{9,8},{10,9... | collective-permute-start | bytes 393224 | tf_op jit(solution)/shard_map/ppermute | solution.py:116
  74.3 11.4 %collective-permute-start.11 = (bf16[64,1024]{1,0:T(8,128)(2,1)S(1)}, bf16[64,1024]{1,0:T(8,128)(2,1)S(1)}, u32[]{:S(2)}, u32[]{:S(2)}) collective-permute-start(bf16[64,1024]{1,0:T(8,128)(2,1)S(1)} %collective-permute-done.10), channel_id=1, source_target_pairs={{0,1},{1,2},{2,3},{3,4},{4,5},{5,6},{6,7},{7,8},{8,9},{9,10},{10,1... | collective-permute-start | bytes 393224 | tf_op jit(solution)/shard_map/ppermute | solution.py:114
  79.4 10.6 %collective-permute-start.4 = (bf16[64,1024]{1,0:T(8,128)(2,1)S(1)}, bf16[64,1024]{1,0:T(8,128)(2,1)S(1)}, u32[]{:S(2)}, u32[]{:S(2)}) collective-permute-start(bf16[64,1024]{1,0:T(8,128)(2,1)S(1)} %collective-permute-done.3), channel_id=1, source_target_pairs={{0,15},{1,0},{2,1},{3,2},{4,3},{5,4},{6,5},{7,6},{8,7},{9,8},{10,9... | collective-permute-start | bytes 393224 | tf_op jit(solution)/shard_map/ppermute | solution.py:116
  85.6 10.6 %collective-permute-start.12 = (bf16[64,1024]{1,0:T(8,128)(2,1)S(1)}, bf16[64,1024]{1,0:T(8,128)(2,1)S(1)}, u32[]{:S(2)}, u32[]{:S(2)}) collective-permute-start(bf16[64,1024]{1,0:T(8,128)(2,1)S(1)} %collective-permute-done.11), channel_id=1, source_target_pairs={{0,1},{1,2},{2,3},{3,4},{4,5},{5,6},{6,7},{7,8},{8,9},{9,10},{10,1... | collective-permute-start | bytes 393224 | tf_op jit(solution)/shard_map/ppermute | solution.py:114
  90.0 8.9 %collective-permute-start.5 = (bf16[64,1024]{1,0:T(8,128)(2,1)S(1)}, bf16[64,1024]{1,0:T(8,128)(2,1)S(1)}, u32[]{:S(2)}, u32[]{:S(2)}) collective-permute-start(bf16[64,1024]{1,0:T(8,128)(2,1)S(1)} %collective-permute-done.4), channel_id=1, source_target_pairs={{0,15},{1,0},{2,1},{3,2},{4,3},{5,4},{6,5},{7,6},{8,7},{9,8},{10,9... | collective-permute-start | bytes 393224 | tf_op jit(solution)/shard_map/ppermute | solution.py:116
  96.2 8.5 %collective-permute-start.13 = (bf16[64,1024]{1,0:T(8,128)(2,1)S(1)}, bf16[64,1024]{1,0:T(8,128)(2,1)S(1)}, u32[]{:S(2)}, u32[]{:S(2)}) collective-permute-start(bf16[64,1024]{1,0:T(8,128)(2,1)S(1)} %collective-permute-done.12), channel_id=1, source_target_pairs={{0,1},{1,2},{2,3},{3,4},{4,5},{5,6},{6,7},{7,8},{8,9},{9,10},{10,1... | collective-permute-start | bytes 393224 | tf_op jit(solution)/shard_map/ppermute | solution.py:114
  98.8 8.5 %collective-permute-start.6 = (bf16[64,1024]{1,0:T(8,128)(2,1)S(1)}, bf16[64,1024]{1,0:T(8,128)(2,1)S(1)}, u32[]{:S(2)}, u32[]{:S(2)}) collective-permute-start(bf16[64,1024]{1,0:T(8,128)(2,1)S(1)} %collective-permute-done.5), channel_id=1, source_target_pairs={{0,15},{1,0},{2,1},{3,2},{4,3},{5,4},{6,5},{7,6},{8,7},{9,8},{10,9... | collective-permute-start | bytes 393224 | tf_op jit(solution)/shard_map/ppermute | solution.py:116
  104.7 8.1 %collective-permute-start.14 = (bf16[64,1024]{1,0:T(8,128)(2,1)S(1)}, bf16[64,1024]{1,0:T(8,128)(2,1)S(1)}, u32[]{:S(2)}, u32[]{:S(2)}) collective-permute-start(bf16[64,1024]{1,0:T(8,128)(2,1)S(1)} %collective-permute-done.13), channel_id=1, source_target_pairs={{0,1},{1,2},{2,3},{3,4},{4,5},{5,6},{6,7},{7,8},{8,9},{9,10},{10,1... | collective-permute-start | bytes 393224 | tf_op jit(solution)/shard_map/ppermute | solution.py:114
  134.3 79.1 %copy-start.1 = (bf16[8,576,64]{1,2,0:T(8,128)(2,1)}, bf16[8,576,64]{1,2,0:T(8,128)(2,1)S(1)}, u32[]{:S(2)}) copy-start(bf16[8,576,64]{1,2,0:T(8,128)(2,1)S(1)} %broadcast_select_fusion.1) | copy-start | bytes 1769476
  214.5 15.7 %all-to-all-start.2 = ((bf16[32,2,2048]{2,1,0:T(2,128)(2,1)}), bf16[32,2,2048]{2,1,0:T(2,128)(2,1)S(1)}, u32[]{:S(2)}, u32[]{:S(2)}) async-start(bf16[32,2,2048]{2,1,0:T(2,128)(2,1)} %reshape.186), calls=%async_computation.3 | async-start | bytes 524288 | tf_op jit(solution)/shard_map/all_to_all | solution.py:155
  225.6 14.5 %copy-start.4 = (bf16[64,64]{1,0:T(8,128)(2,1)S(1)}, bf16[64,64]{1,0:T(8,128)(2,1)}, u32[]{:S(2)}) copy-start(bf16[64,64]{1,0:T(8,128)(2,1)} %reduce_sum.35) | copy-start | bytes 24580
  230.3 33.3 %all-to-all-start.1 = ((bf16[32,512,64]{1,2,0:T(8,128)(2,1)}), bf16[32,512,64]{1,2,0:T(8,128)(2,1)S(1)}, u32[]{:S(2)}, u32[]{:S(2)}) async-start(bf16[32,512,64]{1,2,0:T(8,128)(2,1)} %copy.68), calls=%async_computation.2 | async-start | bytes 4194304 | tf_op jit(solution)/shard_map/all_to_all | solution.py:167
  236.4 72.2 %all-gather.2.cloned.1.call-start = ((), (), s32[]{:S(2)}) async-start(), calls=%async_computation.5 | async-start | bytes 2228224 | tf_op jit(solution)/shard_map/all_gather | solution.py:159
  243.4 20.2 %copy-start.5 = (pred[32]{0:T(512)(128)(4,1)S(1)}, pred[32]{0:T(512)(128)(4,1)}, u32[]{:S(2)}) copy-start(pred[32]{0:T(512)(128)(4,1)} %get-tuple-element.38) | copy-start | bytes 100
  243.4 20.2 %copy-start.7 = (s32[32]{0:T(128)S(1)}, s32[32]{0:T(128)}, u32[]{:S(2)}) copy-start(s32[32]{0:T(128)} %copy-done.6) | copy-start | bytes 388
Sparse Core Ops, SparseCore 0:
  13.0 90.5 reduce-scatter.1
  240.2 68.3 all-gather.1

commit v5 on v4

--- a/solution.py
+++ b/solution.py
@@ -107,16 +107,8 @@
     mine_got = jnp.take(got, my_owner, axis=0)
     panel_a = mine_got[:, :width_dev]
     panel_b_cols = mine_got[:, width_dev:]
-    ahead, behind = [cotangent], [cotangent]
-    to_right = [(i, (i + 1) % n_split) for i in range(n_split)]
-    to_left = [(i, (i - 1) % n_split) for i in range(n_split)]
-    for step in range(n_split // 2):
-        ahead.append(lax.ppermute(ahead[-1], "mp", to_right))
-        if step < n_split // 2 - 1:
-            behind.append(lax.ppermute(behind[-1], "mp", to_left))
-    by_offset = [cotangent] + behind[1:] + ahead[:0:-1]
-    stacked = jnp.concatenate(by_offset + by_offset, axis=0)
-    cot_all = lax.dynamic_slice_in_dim(stacked, (n_split - my_part) * own_rows, rows, 0)
+    (cot_all,) = mp_exchange([cotangent[None]], [True], n_split, 2)
+    cot_all = cot_all.reshape(rows, kv_full)
 
     token_blocks = tokens.reshape(blocks, BLOCK_ROWS, width_dev)
     partial_value = jnp.dot(tokens, value_weight, preferred_element_type=jnp.float32)

time: 320 us -> 361 us (1.13)
  Pallas kernels: 70.2 us -> 208 us
  starting transfers between devices: 82.1 us -> 24.1 us
  local copies, waits for them, and re-layouts: 45.5 us -> 21.9 us
  waiting for transfers between devices: 79.3 us -> 66.4 us
    pallas_call x2 -> x3, Pallas kernels: 70.2 us -> 208 us  [mp_exchange(): pl.pallas_call(functools.partial(_exchange_kernel, n, tuple(spread)), out...]
    ppermute x15 -> x0, starting transfers between devices: 59.4 us -> none  [the longest x7 44.1 us: per_device(): behind.append(lax.ppermute(behind[-1], 'mp', to_left))]
    unnamed x55 -> x28, local copies, waits for them, and re-layouts: 29.1 us -> 9.2 us
    ppermute x15 -> x0, waiting for transfers between devices: 18.2 us -> none  [the longest x7 12 us: per_device(): behind.append(lax.ppermute(behind[-1], 'mp', to_left))]
  transfers between devices with their start and end apart: 20 -> 5, of which waited for: 9 -> 3; matrix products, arithmetic and copies ran while one was open for 19% -> 9% of each run, Pallas kernels for 13% -> 48%
where the time goes in v5:
time: 361 us; the launch traced here: 360 us
  Pallas kernels  208 us (58%)
  waiting for transfers between devices  66.4 us (18%)
  starting transfers between devices  24.1 us (7%)
  local copies, waits for them, and re-layouts  21.9 us (6%)
  matrix products  17.9 us (5%)
  between operations  14.4 us (4%)
  other arithmetic  7.46 us (2%)
    pallas_call x3, Pallas kernels, mp_exchange(): pl.pallas_call(functools.partial(_exchange_kernel, n, tuple(spread)), out...  208 us
    all_gather x1, waiting for transfers between devices, per_device(): grad_up = lax.all_gather(grad_share, 'mp', axis=2, tiled=True)  45.1 us
    all_to_all x1, waiting for transfers between devices, per_device(): lax.all_to_all(send_ga, 'dp', split_axis=0, concat_axis=0, tiled=True)  17.7 us
    all_to_all x1, starting transfers between devices, per_device(): lax.all_to_all(jnp.take(both, wanted, axis=0), 'dp', split_axis=0, concat...  10.1 us
    unnamed x28, local copies, waits for them, and re-layouts  9.2 us
    all_to_all x1, starting transfers between devices, per_device(): lax.all_to_all(send_gb, 'dp', split_axis=0, concat_axis=0, tiled=True)  7.56 us
  transfers between devices with their start and end apart: 5, of which 3 were waited for; matrix products, arithmetic and copies ran while one was open for 9% of the time, Pallas kernels for 48%

profile of v5, /device:TPU:24, one launch (start us, length us, event | category | flops | bytes accessed | tf_op | source)
XLA Modules:
  0.0 360.4 jit_solution(5759446977190321442)
XLA Ops:
  7.2 1.2 copy-done
  8.4 4.4 %fusion.40 = f32[1024,1024]{1,0:T(8,128)} fusion(bf16[1024,512]{1,0:T(8,128)(2,1)S(1)} %copy-done, bf16[512,1024]{1,0:T(8,128)(2,1)} %param.8), kind=kOutput, calls=%fused_computation.82 | convolution fusion | flops 1073741824 | bytes 6291456 | tf_op jit(solution)/shard_map/dot_general | solution.py:114
  12.9 0.6 copy-done.9
  13.5 0.2 select_reduce_fusion
  13.8 1.0 constant_dynamic-slice_fusion
  14.8 0.1 copy.43
  14.9 0.7 fusion.38
  15.7 0.1 fusion.17
  15.9 2.4 gather_fusion
  18.3 3.6 %broadcast_select_fusion = bf16[32,576,64]{1,2,0:T(8,128)(2,1)} fusion(bf16[32,576,64]{1,2,0:T(8,128)(2,1)} %gather_fusion, pred[32]{0:T(512)(128)(4,1)S(1)} %compare_and_fusion.1), kind=kLoop, calls=%fused_computation.3 | loop fusion | flops 1179648 | bytes 4718624 | tf_op jit(solution)/shard_map/jit(_take)/select_n | solution.py:106
  22.0 10.1 %all-to-all-start = ((bf16[32,576,64]{1,2,0:T(8,128)(2,1)}), bf16[32,576,64]{1,2,0:T(8,128)(2,1)}, u32[]{:S(2)}, u32[]{:S(2)}) async-start(bf16[32,576,64]{1,2,0:T(8,128)(2,1)} %broadcast_select_fusion), calls=%async_computation.1 | async-start | bytes 5242880 | tf_op jit(solution)/shard_map/all_to_all | solution.py:106
  32.1 124.8 %shard_map.103 = bf16[16,64,1024]{2,1,0:T(8,128)(2,1)} custom-call(bf16[1,64,1024]{2,1,0:T(8,128)(2,1)} %bitcast.61), custom_call_target="tpu_custom_call" | custom-call | bytes 4194304 | tf_op jit(solution)/shard_map/pallas_call | solution.py:66
  157.1 2.4 gather_fusion.1
  159.5 0.1 broadcast_select_fusion.1
  159.7 0.8 copy-done.1
  160.5 0.5 convolution_bitcast_fusion
  161.0 1.0 copy.44
  162.0 0.1 copy.45
  162.1 0.6 gather_fusion.2
  162.7 0.8 broadcast_select_fusion.2.refs_1_
  163.5 48.1 %shard_map.102 = (f32[16,64,64]{2,1,0:T(8,128)}, bf16[16,64,64]{2,1,0:T(8,128)(2,1)}) custom-call(f32[16,64,64]{2,1,0:T(8,128)} %bitcast.58, bf16[16,64,64]{2,1,0:T(8,128)(2,1)} %broadcast_select_fusion.2.refs_1_), custom_call_target="tpu_custom_call" | custom-call | bytes 786432 | tf_op jit(solution)/shard_map/pallas_call | solution.py:66
  211.7 1.1 copy.46
  212.8 0.2 reshape.156
  213.0 1.7 reduce_sum.35
  214.7 0.8 fusion.8
  215.5 35.4 %shard_map.104 = (bf16[16,64,64]{2,1,0:T(8,128)(2,1)}, bf16[16,64,64]{2,1,0:T(8,128)(2,1)}) custom-call(bf16[1,64,64]{2,1,0:T(8,128)(2,1)} %bitcast.64, bf16[1,64,64]{2,1,0:T(8,128)(2,1)} %bitcast.65), custom_call_target="tpu_custom_call" | custom-call | bytes 524288 | tf_op jit(solution)/shard_map/pallas_call | solution.py:66
  250.9 1.3 fusion.6
  252.2 1.4 convolution_convert_fusion.3
  253.6 0.4 convolution_convert_fusion.2
  254.0 0.2 copy.56
  254.2 1.1 reshape.186
  255.3 7.6 %all-to-all-start.2 = ((bf16[32,2,2048]{2,1,0:T(2,128)(2,1)}), bf16[32,2,2048]{2,1,0:T(2,128)(2,1)S(1)}, u32[]{:S(2)}, u32[]{:S(2)}) async-start(bf16[32,2,2048]{2,1,0:T(2,128)(2,1)} %reshape.186), calls=%async_computation.3 | async-start | bytes 524288 | tf_op jit(solution)/shard_map/all_to_all | solution.py:147
  262.9 0.8 convolution_convert_fusion
  263.7 2.5 copy.51
  266.2 3.5 all-to-all-done.2
  269.7 6.1 %all-to-all-start.1 = ((bf16[32,512,64]{1,2,0:T(8,128)(2,1)}), bf16[32,512,64]{1,2,0:T(8,128)(2,1)S(1)}, u32[]{:S(2)}, u32[]{:S(2)}) async-start(bf16[32,512,64]{1,2,0:T(8,128)(2,1)} %copy.51), calls=%async_computation.2 | async-start | bytes 4194304 | tf_op jit(solution)/shard_map/all_to_all | solution.py:159
  275.8 0.2 all-gather.2.cloned.1.call-start
  276.0 1.2 reshape.187
  277.2 1.4 convolution_convert_fusion.4
  278.6 0.8 copy.58
  279.5 1.9 fusion.7
  281.4 1.5 fusion.11
  283.0 2.3 fusion
  285.2 17.7 %all-to-all-done.1 = bf16[32,512,64]{1,2,0:T(8,128)(2,1)S(1)} async-done(((bf16[32,512,64]{1,2,0:T(8,128)(2,1)}), bf16[32,512,64]{1,2,0:T(8,128)(2,1)S(1)}, u32[]{:S(2)}, u32[]{:S(2)}) %all-to-all-start.1) | async-done | bytes 2097184 | tf_op jit(solution)/shard_map/all_to_all | solution.py:159
  303.0 1.2 fusion.3
  304.2 1.0 copy.59
  305.2 45.1 %all-gather.2.cloned.1.call-done = bf16[8,64,1024]{1,0,2:T(8,128)(2,1)} async-done(((bf16[8,64,64]{1,0,2:T(8,128)(2,1)}), bf16[8,64,1024]{1,0,2:T(8,128)(2,1)}) %all-gather.2.cloned.1.call-update) | async-done | bytes 1048592 | tf_op jit(solution)/shard_map/all_gather | solution.py:151
  350.3 3.3 copy.60
  (38 shorter events, 0.4 us)
Async XLA Ops:
  7.2 1.2 copy-start
  7.2 208.3 %reduce-scatter.2.cloned.1.call-start = ((), (), s32[]{:S(2)}) async-start(), calls=%async_computation.4 | async-start | bytes 4456448 | tf_op jit(solution)/shard_map/reduce_scatter | solution.py:115
  12.8 0.7 copy-start.9
  12.8 0.7 copy-start.10
  12.8 3.0 copy-start.4
  15.8 2.6 copy-start.7
  22.0 135.1 %all-to-all-start = ((bf16[32,576,64]{1,2,0:T(8,128)(2,1)}), bf16[32,576,64]{1,2,0:T(8,128)(2,1)}, u32[]{:S(2)}, u32[]{:S(2)}) async-start(bf16[32,576,64]{1,2,0:T(8,128)(2,1)} %broadcast_select_fusion), calls=%async_computation.1 | async-start | bytes 5242880 | tf_op jit(solution)/shard_map/all_to_all | solution.py:106
  159.7 0.8 copy-start.1
  161.0 53.7 %copy-start.3 = (bf16[64,1024]{1,0:T(8,128)(2,1)S(1)}, bf16[64,1024]{1,0:T(8,128)(2,1)}, u32[]{:S(2)}) copy-start(bf16[64,1024]{1,0:T(8,128)(2,1)} %param.11) | copy-start | bytes 393220
  255.3 14.4 %all-to-all-start.2 = ((bf16[32,2,2048]{2,1,0:T(2,128)(2,1)}), bf16[32,2,2048]{2,1,0:T(2,128)(2,1)S(1)}, u32[]{:S(2)}, u32[]{:S(2)}) async-start(bf16[32,2,2048]{2,1,0:T(2,128)(2,1)} %reshape.186), calls=%async_computation.3 | async-start | bytes 524288 | tf_op jit(solution)/shard_map/all_to_all | solution.py:147
  266.2 13.3 %copy-start.5 = (bf16[64,64]{1,0:T(8,128)(2,1)S(1)}, bf16[64,64]{1,0:T(8,128)(2,1)}, u32[]{:S(2)}) copy-start(bf16[64,64]{1,0:T(8,128)(2,1)} %reduce_sum.35) | copy-start | bytes 24580
  269.7 33.3 %all-to-all-start.1 = ((bf16[32,512,64]{1,2,0:T(8,128)(2,1)}), bf16[32,512,64]{1,2,0:T(8,128)(2,1)S(1)}, u32[]{:S(2)}, u32[]{:S(2)}) async-start(bf16[32,512,64]{1,2,0:T(8,128)(2,1)} %copy.51), calls=%async_computation.2 | async-start | bytes 4194304 | tf_op jit(solution)/shard_map/all_to_all | solution.py:159
  275.8 74.5 %all-gather.2.cloned.1.call-start = ((), (), s32[]{:S(2)}) async-start(), calls=%async_computation.5 | async-start | bytes 2228224 | tf_op jit(solution)/shard_map/all_gather | solution.py:151
  279.5 3.5 copy-start.2
  279.5 3.5 copy-start.11
  283.0 20.0 %copy-start.6 = (pred[32]{0:T(512)(128)(4,1)S(1)}, pred[32]{0:T(512)(128)(4,1)}, u32[]{:S(2)}) copy-start(pred[32]{0:T(512)(128)(4,1)} %get-tuple-element.34) | copy-start | bytes 100
  283.0 20.0 %copy-start.8 = (s32[32]{0:T(128)S(1)}, s32[32]{0:T(128)}, u32[]{:S(2)}) copy-start(s32[32]{0:T(128)} %copy-done.7) | copy-start | bytes 388
Sparse Core Ops, SparseCore 0:
  13.0 182.8 reduce-scatter.1
  279.6 70.6 all-gather.1

commit v6 on v2

--- a/solution.py
+++ b/solution.py
@@ -1,10 +1,85 @@
+import functools
+
 import jax
 import jax.numpy as jnp
 from jax import lax
+from jax.experimental import pallas as pl
+from jax.experimental.pallas import tpu as pltpu
 from jax.sharding import PartitionSpec as P
 
 RANK = 64
 BLOCK_ROWS = 128
+
+
+def _ring_kernel(n, k, *refs):
+    ins, outs = refs[:k], refs[k:2 * k]
+    send_sems, recv_sems, local_sem = refs[2 * k:]
+    me = lax.axis_index("mp")
+    row = lax.axis_index("dp")
+    right = lax.rem(me + 1, n)
+    left = lax.rem(me + n - 1, n)
+    barrier = pltpu.get_barrier_semaphore()
+    for peer in (left, right):
+        pl.semaphore_signal(
+            barrier, inc=1, device_id=(row, peer), device_id_type=pl.DeviceIdType.MESH
+        )
+    pl.semaphore_wait(barrier, 2)
+    for a in range(k):
+        local = pltpu.make_async_copy(ins[a].at[0], outs[a].at[me], local_sem.at[a])
+        local.start()
+        local.wait()
+    reach = (n // 2, n - 1 - n // 2)
+    streams = ((0, right, -1), (1, left, 1))
+
+    def link(a, way, step, slot, peer):
+        return pltpu.make_async_remote_copy(
+            src_ref=outs[a].at[slot],
+            dst_ref=outs[a].at[slot],
+            send_sem=send_sems.at[a, way, step],
+            recv_sem=recv_sems.at[a, way, step],
+            device_id=(row, peer),
+            device_id_type=pl.DeviceIdType.MESH,
+        )
+
+    started = []
+    for step in range(1, reach[0] + 1):
+        for way, peer, sign in streams:
+            if step > reach[way]:
+                continue
+            slot = lax.rem(me + n + sign * (step - 1), n)
+            for a in range(k):
+                if step > 1:
+                    link(a, way, step - 1, slot, peer).wait_recv()
+                copy = link(a, way, step, slot, peer)
+                copy.start()
+                started.append(copy)
+    for way, peer, sign in streams:
+        last = reach[way]
+        slot = lax.rem(me + n + sign * last, n)
+        for a in range(k):
+            link(a, way, last, slot, peer).wait_recv()
+    for copy in started:
+        copy.wait_send()
+
+
+def ring_gather(arrays, n, tag):
+    outs = tuple(jax.ShapeDtypeStruct((n,) + x.shape[1:], x.dtype) for x in arrays)
+    moved = sum(x.size * x.dtype.itemsize for x in outs)
+    vmem = pl.BlockSpec(memory_space=pltpu.VMEM)
+    k = len(arrays)
+    return pl.pallas_call(
+        functools.partial(_ring_kernel, n, k),
+        out_shape=outs,
+        in_specs=[vmem] * k,
+        out_specs=tuple([vmem] * k),
+        scratch_shapes=[
+            pltpu.SemaphoreType.DMA((k, 2, n // 2 + 1)),
+            pltpu.SemaphoreType.DMA((k, 2, n // 2 + 1)),
+            pltpu.SemaphoreType.DMA((k,)),
+        ],
+        compiler_params=pltpu.CompilerParams(collective_id=tag, has_side_effects=True),
+        cost_estimate=pl.CostEstimate(flops=0, transcendentals=0, bytes_accessed=2 * moved),
+    )(*arrays)
 
 
 def per_device(
@@ -36,47 +111,55 @@
     mine_got = jnp.take(got, my_owner, axis=0)
     panel_a = mine_got[:, :width_dev]
     panel_b_cols = mine_got[:, width_dev:]
-    cot_all = lax.all_gather(cotangent, "mp", axis=0, tiled=True)
-    panel_b = lax.all_gather(panel_b_cols, "mp", axis=2, tiled=True)
+    (cot_all,) = ring_gather([cotangent[None]], n_split, 0)
+    cot_all = cot_all.reshape(rows, kv_full)
+    cot_blocks = cot_all.reshape(blocks, BLOCK_ROWS, kv_full)
 
     token_blocks = tokens.reshape(blocks, BLOCK_ROWS, width_dev)
     partial_value = jnp.dot(tokens, value_weight, preferred_element_type=jnp.float32)
     base = lax.psum_scatter(partial_value, "mp", scatter_dimension=0, tiled=True)
     down_part = jnp.einsum(
         "bnd,bdk->bnk", token_blocks, panel_a, preferred_element_type=jnp.float32
-    )
-    first_row = my_part * own_rows
-    my_down = lax.psum_scatter(
-        down_part.reshape(rows, RANK), "mp", scatter_dimension=0, tiled=True
     ).astype(jnp.bfloat16)
-    down = lax.all_gather(my_down, "mp", axis=0, tiled=True)
-
-    cot_blocks = cot_all.reshape(blocks, BLOCK_ROWS, kv_full)
+    parts_down, parts_up = ring_gather([down_part[None], panel_b_cols[None]], n_split, 1)
+    down = jnp.sum(parts_down.astype(jnp.float32), axis=0).astype(jnp.bfloat16)
+    panel_b = parts_up.transpose(1, 2, 0, 3).reshape(blocks, RANK, kv_full)
     back = jnp.einsum(
         "bnc,bkc->bnk", cot_blocks, panel_b, preferred_element_type=jnp.float32
     ).astype(jnp.bfloat16)
+
+    first_row = my_part * own_rows
+    my_down = lax.dynamic_slice_in_dim(down.reshape(rows, RANK), first_row, own_rows, 0)
+    my_up = lax.dynamic_index_in_dim(panel_b, first_row // BLOCK_ROWS, 0, keepdims=False)
+    lifted = jnp.dot(my_down, my_up, preferred_element_type=jnp.float32)
+    projected = (base + lifted).astype(jnp.bfloat16)
+
+    select_bf = select_mask.astype(jnp.bfloat16)
+    pick_bf = pick_mask.astype(jnp.bfloat16)
+    cot_share = lax.dynamic_slice_in_dim(cot_blocks, my_part * kv_part, kv_part, 2)
+    block_grad_b = jnp.einsum(
+        "bnk,bnc->bkc", down, cot_share, preferred_element_type=jnp.float32
+    ).astype(jnp.bfloat16)
+    send_gb = jnp.einsum(
+        "bo,bkc->okc", select_bf, block_grad_b, preferred_element_type=jnp.float32
+    ).astype(jnp.bfloat16)
+    recv_gb = lax.all_to_all(send_gb, "dp", split_axis=0, concat_axis=0, tiled=True)
+    grad_share = jnp.einsum(
+        "ra,rkc->akc", pick_bf, recv_gb, preferred_element_type=jnp.float32
+    ).astype(jnp.bfloat16)
+
     block_grad_a = jnp.einsum(
         "bnd,bnk->bdk", token_blocks, back, preferred_element_type=jnp.float32
     ).astype(jnp.bfloat16)
-    cot_share = lax.dynamic_slice_in_dim(cot_blocks, my_part * kv_part, kv_part, 2)
-    block_grad_b = jnp.einsum(
-        "bnk,bnc->bkc", down.reshape(blocks, BLOCK_ROWS, RANK), cot_share,
-        preferred_element_type=jnp.float32,
+    send_ga = jnp.einsum(
+        "bo,bdk->odk", select_bf, block_grad_a, preferred_element_type=jnp.float32
     ).astype(jnp.bfloat16)
-    grads = jnp.concatenate([block_grad_a, block_grad_b], axis=1)
-    send_g = jnp.einsum(
-        "bo,bdk->odk", select_mask.astype(jnp.bfloat16), grads, preferred_element_type=jnp.float32
+    recv_ga = lax.all_to_all(send_ga, "dp", split_axis=0, concat_axis=0, tiled=True)
+    grad_down = jnp.einsum(
+        "ra,rdk->adk", pick_bf, recv_ga, preferred_element_type=jnp.float32
     ).astype(jnp.bfloat16)
-    recv_g = lax.all_to_all(send_g, "dp", split_axis=0, concat_axis=0, tiled=True)
-    grad_both = jnp.einsum(
-        "ra,rdk->adk", pick_mask.astype(jnp.bfloat16), recv_g, preferred_element_type=jnp.float32
-    ).astype(jnp.bfloat16)
-    grad_down = grad_both[:, :width_dev]
-    grad_up = lax.all_gather(grad_both[:, width_dev:], "mp", axis=2, tiled=True)
-
-    my_up = lax.dynamic_index_in_dim(panel_b, first_row // BLOCK_ROWS, 0, keepdims=False)
-    lifted = jnp.dot(my_down, my_up, preferred_element_type=jnp.float32)
-    projected = (base + lifted).astype(jnp.bfloat16)
+    (shares,) = ring_gather([grad_share[None]], n_split, 2)
+    grad_up = shares.transpose(1, 2, 0, 3).reshape(stored, RANK, kv_full)
 
     grad_base = jnp.einsum("nc,dc->nd", cot_all, value_weight, preferred_element_type=jnp.float32)
     through = jnp.einsum("bnk,bdk->bnd", back, panel_a, preferred_element_type=jnp.float32)

time: 443 us -> 282 us (0.64)
  waiting for transfers between devices: 311 us -> 0.78 us
  Pallas kernels: 0 us -> 183 us
  blocking collectives: 68.1 us -> 0 us
  local copies, waits for them, and re-layouts: 15.7 us -> 32.3 us
  starting transfers between devices: 10.4 us -> 24.3 us
    all_gather x3 -> x0, waiting for transfers between devices: 187 us -> none  [the longest x1 72.1 us: per_device(): grad_up = lax.all_gather(grad_both[:, width_dev:], 'mp', axis=2, tiled=True)]
    pallas_call x0 -> x3, Pallas kernels: none -> 183 us  [ring_gather(): pl.pallas_call(functools.partial(_ring_kernel, n, k), out_shape=outs, in_...]
    unnamed x6 -> x1, waiting for transfers between devices: 63.9 us -> 0.02 us
    all_to_all x1 -> x0, blocking collectives: 39.2 us -> none  [per_device(): lax.all_to_all(send_g, 'dp', split_axis=0, concat_axis=0, tiled=True)]
    all_to_all x1, waiting for transfers between devices: 32.9 us -> 0.01 us  [per_device(): lax.all_to_all(jnp.take(both, wanted, axis=0), 'dp', split_axis=0, concat...]
    all_gather x1 -> x0, blocking collectives: 28.9 us -> none  [per_device(): down = lax.all_gather(my_down, 'mp', axis=0, tiled=True)]
    reduce_scatter x1, waiting for transfers between devices: 27.3 us -> 0.01 us  [per_device(): lax.psum_scatter(partial_value, 'mp', scatter_dimension=0, tiled=True)]
    all_to_all x0 -> x2, starting transfers between devices: none -> 14.1 us  [the longest x1 7.32 us: per_device(): lax.all_to_all(send_gb, 'dp', split_axis=0, concat_axis=0, tiled=True)]
  transfers between devices with their start and end apart: 6 -> 4, of which waited for: 6 -> 1; matrix products, arithmetic and copies ran while one was open for 5% -> 18% of each run, Pallas kernels for 0% -> 65%
where the time goes in v6:
time: 282 us; the launch traced here: 281 us
  Pallas kernels  183 us (65%)
  local copies, waits for them, and re-layouts  32.3 us (11%)
  starting transfers between devices  24.3 us (9%)
  matrix products  18.1 us (6%)
  between operations  14.3 us (5%)
  other arithmetic  7.79 us (3%)
    pallas_call x3, Pallas kernels, ring_gather(): pl.pallas_call(functools.partial(_ring_kernel, n, k), out_shape=outs, in_...  183 us
    all_to_all x1, starting transfers between devices, per_device(): lax.all_to_all(jnp.take(both, wanted, axis=0), 'dp', split_axis=0, concat...  10.1 us
    all_to_all x1, starting transfers between devices, per_device(): lax.all_to_all(send_gb, 'dp', split_axis=0, concat_axis=0, tiled=True)  7.32 us
    unnamed x19, local copies, waits for them, and re-layouts  7.01 us
    all_to_all x1, starting transfers between devices, per_device(): lax.all_to_all(send_ga, 'dp', split_axis=0, concat_axis=0, tiled=True)  6.78 us
  transfers between devices with their start and end apart: 4, of which 1 were waited for; matrix products, arithmetic and copies ran while one was open for 18% of the time, Pallas kernels for 65%

profile of v6, /device:TPU:24, one launch (start us, length us, event | category | flops | bytes accessed | tf_op | source)
XLA Modules:
  0.0 280.6 jit_solution(4145887836145863510)
XLA Ops:
  7.2 0.0 reduce-scatter.2.cloned.1.call-start
  7.2 1.2 copy-done
  8.4 4.4 %fusion.44 = f32[1024,1024]{1,0:T(8,128)} fusion(bf16[1024,512]{1,0:T(8,128)(2,1)S(1)} %copy-done, bf16[512,1024]{1,0:T(8,128)(2,1)} %param.8), kind=kOutput, calls=%fused_computation.73 | convolution fusion | flops 1073741824 | bytes 6291456 | tf_op jit(solution)/shard_map/dot_general | solution.py:119
  12.8 1.1 constant_dynamic-slice_fusion
  13.9 0.1 copy.95
  14.1 0.2 select_reduce_fusion
  14.3 0.1 reduce_sum.35
  14.3 0.1 fusion.42
  14.5 0.1 fusion.20
  14.6 0.1 pad_maximum_fusion
  14.7 2.4 gather_fusion
  17.1 3.6 %broadcast_select_fusion = bf16[32,576,64]{1,2,0:T(8,128)(2,1)} fusion(bf16[32,576,64]{1,2,0:T(8,128)(2,1)} %gather_fusion, pred[32]{0:T(512)(128)(4,1)S(1)} %compare_and_fusion), kind=kLoop, calls=%fused_computation.2 | loop fusion | flops 1179648 | bytes 4718624 | tf_op jit(solution)/shard_map/jit(_take)/select_n | solution.py:110
  20.7 10.1 %all-to-all-start = ((bf16[32,576,64]{1,2,0:T(8,128)(2,1)}), bf16[32,576,64]{1,2,0:T(8,128)(2,1)}, u32[]{:S(2)}, u32[]{:S(2)}) async-start(bf16[32,576,64]{1,2,0:T(8,128)(2,1)} %broadcast_select_fusion), calls=%async_computation.1 | async-start | bytes 5242880 | tf_op jit(solution)/shard_map/all_to_all | solution.py:110
  30.9 68.4 %shard_map.103 = bf16[16,64,1024]{2,1,0:T(8,128)(2,1)} custom-call(bf16[1,64,1024]{2,1,0:T(8,128)(2,1)} %bitcast.68), custom_call_target="tpu_custom_call" | custom-call | bytes 4194304 | tf_op jit(solution)/shard_map/pallas_call | solution.py:70
  99.4 2.4 gather_fusion.1
  101.8 0.7 copy.96
  102.5 0.2 broadcast_select_fusion.1
  102.7 0.5 convolution_convert_fusion.5
  103.2 0.9 copy.98
  104.1 0.7 slice_bitcast_fusion.refs_1_
  104.7 73.0 %shard_map.102 = (bf16[16,8,128,64]{3,2,1,0:T(8,128)(2,1)}, bf16[16,8,64,64]{3,2,1,0:T(8,128)(2,1)}) custom-call(bf16[1,8,128,64]{3,2,1,0:T(8,128)(2,1)} %bitcast.66, bf16[1,8,64,64]{3,2,1,0:T(8,128)(2,1)} %slice_bitcast_fusion.refs_1_), custom_call_target="tpu_custom_call" | custom-call | bytes 6291456 | tf_op jit(solution)/shard_map/pallas_call | solution.py:70
  177.7 4.3 %copy.100 = bf16[8,64,16,64]{3,2,1,0:T(8,128)(2,1)} copy(bf16[8,64,16,64]{3,1,0,2:T(8,128)(2,1)} %bitcast.64) | data formatting | bytes 2097152 | tf_op jit(solution)/shard_map/transpose | solution.py:126
  182.0 3.2 %reshape.90 = bf16[8,64,1024]{2,1,0:T(8,128)(2,1)S(1)} reshape(bf16[8,64,16,64]{3,2,1,0:T(8,128)(2,1)} %copy.100) | data formatting | bytes 2097152 | tf_op jit(solution)/shard_map/reshape | solution.py:126
  185.2 3.4 %reduce_sum.38 = bf16[8,128,64]{2,1,0:T(8,128)(2,1)S(1)} reduce(bf16[16,8,128,64]{3,2,1,0:T(8,128)(2,1)} %get-tuple-element.6, bf16[]{:T(256)} %constant.91.clone.1), dimensions={0}, to_apply=%region_3.4 | reduce | flops 983040 | bytes 2228226 | tf_op jit(solution)/shard_map/reduce_sum | solution.py:125
  188.7 1.4 convolution_convert_fusion.3
  190.1 0.4 convolution_convert_fusion.2
  190.5 1.0 copy.108
  191.5 2.1 reshape.112
  193.6 7.3 %all-to-all-start.2 = ((bf16[32,2,2048]{2,1,0:T(2,128)(2,1)}), bf16[32,2,2048]{2,1,0:T(2,128)(2,1)}, u32[]{:S(2)}, u32[]{:S(2)}) async-start(bf16[32,2,2048]{2,1,0:T(2,128)(2,1)} %reshape.112), calls=%async_computation.3 | async-start | bytes 524288 | tf_op jit(solution)/shard_map/all_to_all | solution.py:146
  201.0 2.4 convolution_convert_fusion.4
  203.4 0.3 fusion.6
  203.7 0.8 convolution_convert_fusion
  204.5 2.5 copy.103
  207.0 0.8 all-to-all-done.2
  207.8 6.8 %all-to-all-start.1 = ((bf16[32,512,64]{1,2,0:T(8,128)(2,1)}), bf16[32,512,64]{1,2,0:T(8,128)(2,1)}, u32[]{:S(2)}, u32[]{:S(2)}) async-start(bf16[32,512,64]{1,2,0:T(8,128)(2,1)} %copy.103), calls=%async_computation.2 | async-start | bytes 4194304 | tf_op jit(solution)/shard_map/all_to_all | solution.py:157
  214.6 0.5 fusion.8
  215.1 0.7 copy-done.7
  215.8 0.7 copy-done.1
  216.5 2.3 fusion
  218.8 1.3 reshape.113
  220.1 0.4 fusion.11
  220.5 0.7 copy.132
  221.2 41.7 %shard_map.104 = bf16[16,8,64,64]{3,2,1,0:T(8,128)(2,1)} custom-call(bf16[1,8,64,64]{3,2,1,0:T(8,128)(2,1)} %bitcast.67), custom_call_target="tpu_custom_call" | custom-call | bytes 2097152 | tf_op jit(solution)/shard_map/pallas_call | solution.py:70
  262.9 3.0 %copy.111 = bf16[8,64,16,64]{3,2,1,0:T(8,128)(2,1)S(1)} copy(bf16[8,64,16,64]{3,1,0,2:T(8,128)(2,1)} %bitcast.63) | data formatting | bytes 2097152 | tf_op jit(solution)/shard_map/transpose | solution.py:162
  265.8 2.3 reshape.93
  268.1 2.8 %fusion.3 = bf16[8,512,64]{1,0,2:T(8,128)(2,1)S(1)} fusion(bf16[32,512,64]{1,2,0:T(8,128)(2,1)} %all-to-all-done.1, s32[32]{0:T(128)S(1)} %fusion.20, pred[32]{0:T(512)(128)(4,1)S(1)} %get-tuple-element.36), kind=kOutput, calls=%fused_computation.9 | convolution fusion | flops 17039872 | bytes 2621600 | tf_op jit(solution)/shard_map/ra,rdk->adk/dot_general | solution.py:158
  270.9 1.0 copy.112
  271.9 1.9 fusion.7
  (23 shorter events, 0.1 us)
Async XLA Ops:
  7.2 1.2 copy-start
  7.2 264.7 %reduce-scatter.2.cloned.1.call-start = ((), (), s32[]{:S(2)}) async-start(), calls=%async_computation.4 | async-start | bytes 4456448 | tf_op jit(solution)/shard_map/reduce_scatter | solution.py:120
  12.8 1.3 copy-start.5
  12.8 1.3 copy-start.6
  12.8 1.8 copy-start.4
  20.7 78.6 %all-to-all-start = ((bf16[32,576,64]{1,2,0:T(8,128)(2,1)}), bf16[32,576,64]{1,2,0:T(8,128)(2,1)}, u32[]{:S(2)}, u32[]{:S(2)}) async-start(bf16[32,576,64]{1,2,0:T(8,128)(2,1)} %broadcast_select_fusion), calls=%async_computation.1 | async-start | bytes 5242880 | tf_op jit(solution)/shard_map/all_to_all | solution.py:110
  185.2 15.7 %copy-start.2 = (bf16[8,64,1024]{2,1,0:T(8,128)(2,1)}, bf16[8,64,1024]{2,1,0:T(8,128)(2,1)S(1)}, u32[]{:S(2)}) copy-start(bf16[8,64,1024]{2,1,0:T(8,128)(2,1)S(1)} %reshape.90) | copy-start | bytes 3145732
  188.7 5.0 %copy-start.3 = (bf16[8,128,64]{2,1,0:T(8,128)(2,1)}, bf16[8,128,64]{2,1,0:T(8,128)(2,1)S(1)}, u32[]{:S(2)}) copy-start(bf16[8,128,64]{2,1,0:T(8,128)(2,1)S(1)} %reduce_sum.38) | copy-start | bytes 393220
  193.6 14.2 %all-to-all-start.2 = ((bf16[32,2,2048]{2,1,0:T(2,128)(2,1)}), bf16[32,2,2048]{2,1,0:T(2,128)(2,1)}, u32[]{:S(2)}, u32[]{:S(2)}) async-start(bf16[32,2,2048]{2,1,0:T(2,128)(2,1)} %reshape.112), calls=%async_computation.3 | async-start | bytes 524288 | tf_op jit(solution)/shard_map/all_to_all | solution.py:146
  207.8 60.3 %all-to-all-start.1 = ((bf16[32,512,64]{1,2,0:T(8,128)(2,1)}), bf16[32,512,64]{1,2,0:T(8,128)(2,1)}, u32[]{:S(2)}, u32[]{:S(2)}) async-start(bf16[32,512,64]{1,2,0:T(8,128)(2,1)} %copy.103), calls=%async_computation.2 | async-start | bytes 4194304 | tf_op jit(solution)/shard_map/all_to_all | solution.py:157
  214.6 1.2 copy-start.7
  214.6 1.9 copy-start.1
Sparse Core Ops, SparseCore 0:
  13.0 94.6 reduce-scatter.1

commit v7 on v6

--- a/solution.py
+++ b/solution.py
@@ -11,7 +11,7 @@
 BLOCK_ROWS = 128
 
 
-def _ring_kernel(n, k, *refs):
+def _ring_kernel(n, k, pieces, *refs):
     ins, outs = refs[:k], refs[k:2 * k]
     send_sems, recv_sems, local_sem = refs[2 * k:]
     me = lax.axis_index("mp")
@@ -31,12 +31,14 @@
     reach = (n // 2, n - 1 - n // 2)
     streams = ((0, right, -1), (1, left, 1))
 
-    def link(a, way, step, slot, peer):
+    def link(a, way, step, slot, peer, i):
+        size = outs[a].shape[1] // pieces
+        part = outs[a].at[slot, pl.ds(i * size, size)]
         return pltpu.make_async_remote_copy(
-            src_ref=outs[a].at[slot],
-            dst_ref=outs[a].at[slot],
-            send_sem=send_sems.at[a, way, step],
-            recv_sem=recv_sems.at[a, way, step],
+            src_ref=part,
+            dst_ref=part,
+            send_sem=send_sems.at[a, way, step, i],
+            recv_sem=recv_sems.at[a, way, step, i],
             device_id=(row, peer),
             device_id_type=pl.DeviceIdType.MESH,
         )
@@ -48,33 +50,35 @@
                 continue
             slot = lax.rem(me + n + sign * (step - 1), n)
             for a in range(k):
-                if step > 1:
-                    link(a, way, step - 1, slot, peer).wait_recv()
-                copy = link(a, way, step, slot, peer)
-                copy.start()
-                started.append(copy)
+                for i in range(pieces):
+                    if step > 1:
+                        link(a, way, step - 1, slot, peer, i).wait_recv()
+                    copy = link(a, way, step, slot, peer, i)
+                    copy.start()
+                    started.append(copy)
     for way, peer, sign in streams:
         last = reach[way]
         slot = lax.rem(me + n + sign * last, n)
         for a in range(k):
-            link(a, way, last, slot, peer).wait_recv()
+            for i in range(pieces):
+                link(a, way, last, slot, peer, i).wait_recv()
     for copy in started:
         copy.wait_send()
 
 
-def ring_gather(arrays, n, tag):
+def ring_gather(arrays, n, tag, pieces=4):
     outs = tuple(jax.ShapeDtypeStruct((n,) + x.shape[1:], x.dtype) for x in arrays)
     moved = sum(x.size * x.dtype.itemsize for x in outs)
     vmem = pl.BlockSpec(memory_space=pltpu.VMEM)
     k = len(arrays)
     return pl.pallas_call(
-        functools.partial(_ring_kernel, n, k),
+        functools.partial(_ring_kernel, n, k, pieces),
         out_shape=outs,
         in_specs=[vmem] * k,
         out_specs=tuple([vmem] * k),
         scratch_shapes=[
-            pltpu.SemaphoreType.DMA((k, 2, n // 2 + 1)),
-            pltpu.SemaphoreType.DMA((k, 2, n // 2 + 1)),
+            pltpu.SemaphoreType.DMA((k, 2, n // 2 + 1, pieces)),
+            pltpu.SemaphoreType.DMA((k, 2, n // 2 + 1, pieces)),
             pltpu.SemaphoreType.DMA((k,)),
         ],
         compiler_params=pltpu.CompilerParams(collective_id=tag, has_side_effects=True),
@@ -139,13 +143,14 @@
     cot_share = lax.dynamic_slice_in_dim(cot_blocks, my_part * kv_part, kv_part, 2)
     block_grad_b = jnp.einsum(
         "bnk,bnc->bkc", down, cot_share, preferred_element_type=jnp.float32
-    ).astype(jnp.bfloat16)
+    )
     send_gb = jnp.einsum(
-        "bo,bkc->okc", select_bf, block_grad_b, preferred_element_type=jnp.float32
-    ).astype(jnp.bfloat16)
+        "bo,bkc->okc", select_mask.astype(jnp.float32), block_grad_b,
+        precision=lax.Precision.HIGHEST,
+    )
     recv_gb = lax.all_to_all(send_gb, "dp", split_axis=0, concat_axis=0, tiled=True)
     grad_share = jnp.einsum(
-        "ra,rkc->akc", pick_bf, recv_gb, preferred_element_type=jnp.float32
+        "ra,rkc->akc", pick_mask.astype(jnp.float32), recv_gb, precision=lax.Precision.HIGHEST
     ).astype(jnp.bfloat16)
 
     block_grad_a = jnp.einsum(

time: 282 us -> 286 us (1.014)
  Pallas kernels: 183 us -> 180 us
  other arithmetic: 7.79 us -> 10.7 us
    pallas_call x3, Pallas kernels: 183 us -> 180 us  [ring_gather(): pl.pallas_call(functools.partial(_ring_kernel, n, k, pieces), out_shape=o...]
    all_to_all x0 -> x1, other arithmetic: none -> 2.94 us  [per_device(): lax.all_to_all(send_gb, 'dp', split_axis=0, concat_axis=0, tiled=True)]
  transfers between devices with their start and end apart: 4 -> 4, of which waited for: 1 -> 1; matrix products, arithmetic and copies ran while one was open for 18% -> 19% of each run, Pallas kernels for 65% -> 63%
where the time goes in v7:
time: 286 us; the launch traced here: 285 us
  Pallas kernels  180 us (63%)
  local copies, waits for them, and re-layouts  33 us (12%)
  starting transfers between devices  24.6 us (9%)
  matrix products  19 us (7%)
  between operations  14.3 us (5%)
  other arithmetic  10.7 us (4%)
  waiting for transfers between devices  3.46 us (1%)
    pallas_call x3, Pallas kernels, ring_gather(): pl.pallas_call(functools.partial(_ring_kernel, n, k, pieces), out_shape=o...  180 us
    all_to_all x1, starting transfers between devices, per_device(): lax.all_to_all(jnp.take(both, wanted, axis=0), 'dp', split_axis=0, concat...  10.1 us
    all_to_all x1, starting transfers between devices, per_device(): lax.all_to_all(send_gb, 'dp', split_axis=0, concat_axis=0, tiled=True)  7.46 us
    all_to_all x1, starting transfers between devices, per_device(): lax.all_to_all(send_ga, 'dp', split_axis=0, concat_axis=0, tiled=True)  6.98 us
    unnamed x19, local copies, waits for them, and re-layouts  6.63 us
  transfers between devices with their start and end apart: 4, of which 1 were waited for; matrix products, arithmetic and copies ran while one was open for 19% of the time, Pallas kernels for 63%

profile of v7, /device:TPU:24, one launch (start us, length us, event | category | flops | bytes accessed | tf_op | source)
XLA Modules:
  0.0 284.7 jit_solution(13300962533160222339)
XLA Ops:
  7.2 1.2 copy-done
  8.4 4.4 %fusion.46 = f32[1024,1024]{1,0:T(8,128)} fusion(bf16[1024,512]{1,0:T(8,128)(2,1)S(1)} %copy-done, bf16[512,1024]{1,0:T(8,128)(2,1)} %param.8), kind=kOutput, calls=%fused_computation.73 | convolution fusion | flops 1073741824 | bytes 6291456 | tf_op jit(solution)/shard_map/dot_general | solution.py:123
  12.8 1.1 constant_dynamic-slice_fusion
  13.9 0.1 copy.95
  14.1 0.2 select_reduce_fusion
  14.3 0.1 reduce_sum.35
  14.3 0.1 fusion.44
  14.5 0.1 fusion.22
  14.7 2.4 gather_fusion
  17.1 3.6 %broadcast_select_fusion = bf16[32,576,64]{1,2,0:T(8,128)(2,1)} fusion(bf16[32,576,64]{1,2,0:T(8,128)(2,1)} %gather_fusion, pred[32]{0:T(512)(128)(4,1)S(1)} %compare_and_fusion), kind=kLoop, calls=%fused_computation.2 | loop fusion | flops 1179648 | bytes 4718624 | tf_op jit(solution)/shard_map/jit(_take)/select_n | solution.py:114
  20.8 10.1 %all-to-all-start = ((bf16[32,576,64]{1,2,0:T(8,128)(2,1)}), bf16[32,576,64]{1,2,0:T(8,128)(2,1)}, u32[]{:S(2)}, u32[]{:S(2)}) async-start(bf16[32,576,64]{1,2,0:T(8,128)(2,1)} %broadcast_select_fusion), calls=%async_computation.1 | async-start | bytes 5242880 | tf_op jit(solution)/shard_map/all_to_all | solution.py:114
  30.9 58.4 %shard_map.103 = bf16[16,64,1024]{2,1,0:T(8,128)(2,1)} custom-call(bf16[1,64,1024]{2,1,0:T(8,128)(2,1)} %bitcast.68), custom_call_target="tpu_custom_call" | custom-call | bytes 4194304 | tf_op jit(solution)/shard_map/pallas_call | solution.py:74
  89.3 2.4 gather_fusion.1
  91.8 0.7 copy.96
  92.5 0.2 broadcast_select_fusion.1
  92.7 0.5 convolution_convert_fusion.3
  93.2 0.9 copy.98
  94.0 0.7 slice_bitcast_fusion.refs_1_
  94.7 83.6 %shard_map.102 = (bf16[16,8,128,64]{3,2,1,0:T(8,128)(2,1)}, bf16[16,8,64,64]{3,2,1,0:T(8,128)(2,1)}) custom-call(bf16[1,8,128,64]{3,2,1,0:T(8,128)(2,1)} %bitcast.66, bf16[1,8,64,64]{3,2,1,0:T(8,128)(2,1)} %slice_bitcast_fusion.refs_1_), custom_call_target="tpu_custom_call" | custom-call | bytes 6291456 | tf_op jit(solution)/shard_map/pallas_call | solution.py:74
  178.3 4.3 %copy.100 = bf16[8,64,16,64]{3,2,1,0:T(8,128)(2,1)} copy(bf16[8,64,16,64]{3,1,0,2:T(8,128)(2,1)} %bitcast.64) | data formatting | bytes 2097152 | tf_op jit(solution)/shard_map/transpose | solution.py:130
  182.6 3.2 %reshape.90 = bf16[8,64,1024]{2,1,0:T(8,128)(2,1)S(1)} reshape(bf16[8,64,16,64]{3,2,1,0:T(8,128)(2,1)} %copy.100) | data formatting | bytes 2097152 | tf_op jit(solution)/shard_map/reshape | solution.py:130
  185.8 3.4 %reduce_sum.38 = bf16[8,128,64]{2,1,0:T(8,128)(2,1)S(1)} reduce(bf16[16,8,128,64]{3,2,1,0:T(8,128)(2,1)} %get-tuple-element.6, bf16[]{:T(256)} %constant.91.clone.1), dimensions={0}, to_apply=%region_3.4 | reduce | flops 983040 | bytes 2228226 | tf_op jit(solution)/shard_map/reduce_sum | solution.py:129
  189.3 1.4 fusion.16
  190.6 0.7 fusion.14
  191.3 1.6 copy.108
  192.9 2.7 reshape.112
  195.6 7.5 %all-to-all-start.2 = ((f32[32,1,4096]{2,1,0:T(1,128)}), f32[32,1,4096]{2,1,0:T(1,128)}, u32[]{:S(2)}, u32[]{:S(2)}) async-start(f32[32,1,4096]{2,1,0:T(1,128)} %reshape.112), calls=%async_computation.3 | async-start | bytes 1048576 | tf_op jit(solution)/shard_map/all_to_all | solution.py:151
  203.1 2.4 convolution_convert_fusion.2
  205.5 0.3 fusion.6
  205.8 0.8 convolution_convert_fusion
  206.6 2.5 copy.103
  209.1 3.4 %all-to-all-done.2 = f32[32,1,4096]{2,1,0:T(1,128)} async-done(((f32[32,1,4096]{2,1,0:T(1,128)}), f32[32,1,4096]{2,1,0:T(1,128)}, u32[]{:S(2)}, u32[]{:S(2)}) %all-to-all-start.2) | async-done | bytes 524320 | tf_op jit(solution)/shard_map/all_to_all | solution.py:151
  212.6 7.0 %all-to-all-start.1 = ((bf16[32,512,64]{1,2,0:T(8,128)(2,1)}), bf16[32,512,64]{1,2,0:T(8,128)(2,1)}, u32[]{:S(2)}, u32[]{:S(2)}) async-start(bf16[32,512,64]{1,2,0:T(8,128)(2,1)} %copy.103), calls=%async_computation.2 | async-start | bytes 4194304 | tf_op jit(solution)/shard_map/all_to_all | solution.py:162
  219.6 0.5 fusion.10
  220.1 0.7 copy-done.7
  220.8 0.7 copy-done.1
  221.5 2.3 fusion
  223.8 0.5 broadcast.95
  224.3 2.9 %reduce.1 = f32[32,4096]{1,0:T(8,128)S(1)} reduce(f32[32,1,4096]{2,1,0:T(1,128)} %all-to-all-done.2, f32[]{:T(128)} %broadcast.95), dimensions={1}, to_apply=%all_to_all.11.reduce_sub_computation | reduce | bytes 1048580 | tf_op jit(solution)/shard_map/all_to_all | solution.py:151
  227.2 0.4 reshape.113
  227.6 1.0 fusion.8
  228.7 0.7 copy.132
  229.4 37.6 %shard_map.104 = bf16[16,8,64,64]{3,2,1,0:T(8,128)(2,1)} custom-call(bf16[1,8,64,64]{3,2,1,0:T(8,128)(2,1)} %bitcast.67), custom_call_target="tpu_custom_call" | custom-call | bytes 2097152 | tf_op jit(solution)/shard_map/pallas_call | solution.py:74
  266.9 3.0 %copy.111 = bf16[8,64,16,64]{3,2,1,0:T(8,128)(2,1)S(1)} copy(bf16[8,64,16,64]{3,1,0,2:T(8,128)(2,1)} %bitcast.63) | data formatting | bytes 2097152 | tf_op jit(solution)/shard_map/transpose | solution.py:167
  269.9 2.3 reshape.93
  272.2 2.8 fusion.3
  275.0 1.0 copy.112
  276.0 1.9 fusion.7
  (25 shorter events, 0.2 us)
Async XLA Ops:
  7.2 1.2 copy-start
  7.2 268.8 %reduce-scatter.2.cloned.1.call-start = ((), (), s32[]{:S(2)}) async-start(), calls=%async_computation.4 | async-start | bytes 4456448 | tf_op jit(solution)/shard_map/reduce_scatter | solution.py:124
  12.8 1.3 copy-start.5
  12.8 1.3 copy-start.6
  12.8 1.8 copy-start.4
  20.8 68.6 %all-to-all-start = ((bf16[32,576,64]{1,2,0:T(8,128)(2,1)}), bf16[32,576,64]{1,2,0:T(8,128)(2,1)}, u32[]{:S(2)}, u32[]{:S(2)}) async-start(bf16[32,576,64]{1,2,0:T(8,128)(2,1)} %broadcast_select_fusion), calls=%async_computation.1 | async-start | bytes 5242880 | tf_op jit(solution)/shard_map/all_to_all | solution.py:114
  185.8 17.3 %copy-start.2 = (bf16[8,64,1024]{2,1,0:T(8,128)(2,1)}, bf16[8,64,1024]{2,1,0:T(8,128)(2,1)S(1)}, u32[]{:S(2)}) copy-start(bf16[8,64,1024]{2,1,0:T(8,128)(2,1)S(1)} %reshape.90) | copy-start | bytes 3145732
  189.3 3.7 %copy-start.3 = (bf16[8,128,64]{2,1,0:T(8,128)(2,1)}, bf16[8,128,64]{2,1,0:T(8,128)(2,1)S(1)}, u32[]{:S(2)}) copy-start(bf16[8,128,64]{2,1,0:T(8,128)(2,1)S(1)} %reduce_sum.38) | copy-start | bytes 393220
  195.6 17.0 %all-to-all-start.2 = ((f32[32,1,4096]{2,1,0:T(1,128)}), f32[32,1,4096]{2,1,0:T(1,128)}, u32[]{:S(2)}, u32[]{:S(2)}) async-start(f32[32,1,4096]{2,1,0:T(1,128)} %reshape.112), calls=%async_computation.3 | async-start | bytes 1048576 | tf_op jit(solution)/shard_map/all_to_all | solution.py:151
  212.6 59.6 %all-to-all-start.1 = ((bf16[32,512,64]{1,2,0:T(8,128)(2,1)}), bf16[32,512,64]{1,2,0:T(8,128)(2,1)}, u32[]{:S(2)}, u32[]{:S(2)}) async-start(bf16[32,512,64]{1,2,0:T(8,128)(2,1)} %copy.103), calls=%async_computation.2 | async-start | bytes 4194304 | tf_op jit(solution)/shard_map/all_to_all | solution.py:162
  219.6 1.2 copy-start.7
  219.6 1.9 copy-start.1
Sparse Core Ops, SparseCore 0:
  13.0 101.6 reduce-scatter.1

commit v8 on v7

--- a/solution.py
+++ b/solution.py
@@ -125,8 +125,14 @@
     down_part = jnp.einsum(
         "bnd,bdk->bnk", token_blocks, panel_a, preferred_element_type=jnp.float32
     ).astype(jnp.bfloat16)
-    parts_down, parts_up = ring_gather([down_part[None], panel_b_cols[None]], n_split, 1)
-    down = jnp.sum(parts_down.astype(jnp.float32), axis=0).astype(jnp.bfloat16)
+    down_rows = down_part.size // kv_full
+    packed = jnp.concatenate(
+        [down_part.reshape(down_rows, kv_full), panel_b_cols.reshape(-1, kv_full)], axis=0
+    )
+    (parts,) = ring_gather([packed[None]], n_split, 1, pieces=3)
+    down = jnp.sum(parts[:, :down_rows].astype(jnp.float32), axis=0)
+    down = down.astype(jnp.bfloat16).reshape(blocks, BLOCK_ROWS, RANK)
+    parts_up = parts[:, down_rows:].reshape(n_split, blocks, RANK, kv_part)
     panel_b = parts_up.transpose(1, 2, 0, 3).reshape(blocks, RANK, kv_full)
     back = jnp.einsum(
         "bnc,bkc->bnk", cot_blocks, panel_b, preferred_element_type=jnp.float32
@@ -163,7 +169,8 @@
     grad_down = jnp.einsum(
         "ra,rdk->adk", pick_bf, recv_ga, preferred_element_type=jnp.float32
     ).astype(jnp.bfloat16)
-    (shares,) = ring_gather([grad_share[None]], n_split, 2)
+    (shares,) = ring_gather([grad_share.reshape(1, -1, kv_full)], n_split, 2, pieces=2)
+    shares = shares.reshape(n_split, stored, RANK, kv_part)
     grad_up = shares.transpose(1, 2, 0, 3).reshape(stored, RANK, kv_full)
 
     grad_base = jnp.einsum("nc,dc->nd", cot_all, value_weight, preferred_element_type=jnp.float32)

time: 286 us -> 249 us (0.87)
  Pallas kernels: 180 us -> 139 us
  local copies, waits for them, and re-layouts: 33 us -> 37.2 us
    pallas_call x3, Pallas kernels: 180 us -> 139 us  [ring_gather(): pl.pallas_call(functools.partial(_ring_kernel, n, k, pieces), out_shape=o...]
    reshape x0 -> x6, local copies, waits for them, and re-layouts: none -> 6.62 us  [the longest x1 2.96 us: per_device(): shares = shares.reshape(n_split, stored, RANK, kv_part)]
    unnamed x19 -> x17, local copies, waits for them, and re-layouts: 6.63 us -> 5.24 us
  transfers between devices with their start and end apart: 4 -> 4, of which waited for: 1 -> 1; matrix products, arithmetic and copies ran while one was open for 19% -> 23% of each run, Pallas kernels for 63% -> 56%
where the time goes in v8:
time: 249 us; the launch traced here: 248 us
  Pallas kernels  139 us (56%)
  local copies, waits for them, and re-layouts  37.2 us (15%)
  starting transfers between devices  24.9 us (10%)
  matrix products  18.7 us (8%)
  between operations  14.4 us (6%)
  other arithmetic  10.1 us (4%)
  waiting for transfers between devices  3.82 us (2%)
    pallas_call x3, Pallas kernels, ring_gather(): pl.pallas_call(functools.partial(_ring_kernel, n, k, pieces), out_shape=o...  139 us
    all_to_all x1, starting transfers between devices, per_device(): lax.all_to_all(jnp.take(both, wanted, axis=0), 'dp', split_axis=0, concat...  10.1 us
    all_to_all x1, starting transfers between devices, per_device(): lax.all_to_all(send_gb, 'dp', split_axis=0, concat_axis=0, tiled=True)  7.75 us
    all_to_all x1, starting transfers between devices, per_device(): lax.all_to_all(send_ga, 'dp', split_axis=0, concat_axis=0, tiled=True)  6.98 us
    unnamed x17, local copies, waits for them, and re-layouts  5.24 us
  transfers between devices with their start and end apart: 4, of which 1 were waited for; matrix products, arithmetic and copies ran while one was open for 23% of the time, Pallas kernels for 56%

profile of v8, /device:TPU:24, one launch (start us, length us, event | category | flops | bytes accessed | tf_op | source)
XLA Modules:
  0.0 247.9 jit_solution(17975703751398033732)
XLA Ops:
  7.2 1.2 copy-done
  8.4 4.4 %fusion.45 = f32[1024,1024]{1,0:T(8,128)} fusion(bf16[1024,512]{1,0:T(8,128)(2,1)S(1)} %copy-done, bf16[512,1024]{1,0:T(8,128)(2,1)} %param.8), kind=kOutput, calls=%fused_computation.73 | convolution fusion | flops 1073741824 | bytes 6291456 | tf_op jit(solution)/shard_map/dot_general | solution.py:123
  12.8 1.1 constant_dynamic-slice_fusion
  14.1 0.2 select_reduce_fusion
  14.3 0.1 fusion.43
  14.7 2.4 gather_fusion
  17.1 3.6 %broadcast_select_fusion = bf16[32,576,64]{1,2,0:T(8,128)(2,1)} fusion(bf16[32,576,64]{1,2,0:T(8,128)(2,1)} %gather_fusion, pred[32]{0:T(512)(128)(4,1)S(1)} %compare_and_fusion), kind=kLoop, calls=%fused_computation.2 | loop fusion | flops 1179648 | bytes 4718624 | tf_op jit(solution)/shard_map/jit(_take)/select_n | solution.py:114
  20.8 10.1 %all-to-all-start = ((bf16[32,576,64]{1,2,0:T(8,128)(2,1)}), bf16[32,576,64]{1,2,0:T(8,128)(2,1)}, u32[]{:S(2)}, u32[]{:S(2)}) async-start(bf16[32,576,64]{1,2,0:T(8,128)(2,1)} %broadcast_select_fusion), calls=%async_computation.1 | async-start | bytes 5242880 | tf_op jit(solution)/shard_map/all_to_all | solution.py:114
  30.9 58.4 %shard_map.103 = bf16[16,64,1024]{2,1,0:T(8,128)(2,1)} custom-call(bf16[1,64,1024]{2,1,0:T(8,128)(2,1)} %bitcast.60), custom_call_target="tpu_custom_call" | custom-call | bytes 4194304 | tf_op jit(solution)/shard_map/pallas_call | solution.py:74
  89.3 2.4 gather_fusion.1
  92.1 0.1 reshape.105
  92.2 0.5 fusion.8
  92.7 0.2 copy.41
  92.9 0.2 reshape.104
  93.1 0.7 maximum_bitcast_fusion.refs_0_
  93.8 49.1 %shard_map.102 = bf16[16,96,1024]{2,1,0:T(8,128)(2,1)} custom-call(bf16[1,96,1024]{2,1,0:T(8,128)(2,1)} %maximum_bitcast_fusion.refs_0_), custom_call_target="tpu_custom_call" | custom-call | bytes 6291456 | tf_op jit(solution)/shard_map/pallas_call | solution.py:74
  142.9 1.2 slice-done
  144.1 2.4 reshape.106
  146.5 3.0 %copy.43 = bf16[8,64,16,64]{3,2,1,0:T(8,128)(2,1)S(1)} copy(bf16[8,64,16,64]{3,1,0,2:T(8,128)(2,1)} %bitcast.58) | data formatting | bytes 2097152 | tf_op jit(solution)/shard_map/transpose | solution.py:136
  149.5 2.3 reshape.107
  151.7 2.1 slice_reduce_fusion
  153.8 0.2 reshape.110
  154.0 0.3 fusion.16
  154.4 0.7 fusion.14
  155.0 1.6 copy.50
  156.6 2.7 %reshape.132 = f32[32,1,4096]{2,1,0:T(1,128)} reshape(f32[32,64,64]{2,1,0:T(8,128)} %copy.50) | data formatting | bytes 1048576
  159.3 7.8 %all-to-all-start.2 = ((f32[32,1,4096]{2,1,0:T(1,128)}), f32[32,1,4096]{2,1,0:T(1,128)}, u32[]{:S(2)}, u32[]{:S(2)}) async-start(f32[32,1,4096]{2,1,0:T(1,128)} %reshape.132), calls=%async_computation.3 | async-start | bytes 1048576 | tf_op jit(solution)/shard_map/all_to_all | solution.py:157
  167.1 2.1 convolution_convert_fusion.3
  169.1 0.3 fusion.6
  169.4 0.8 convolution_convert_fusion
  170.3 2.5 %copy.45 = bf16[32,512,64]{1,2,0:T(8,128)(2,1)} copy(bf16[32,512,64]{1,0,2:T(8,128)(2,1)S(1)} %convolution_convert_fusion) | data formatting | bytes 4194304 | tf_op jit(solution)/shard_map/convert_element_type | solution.py:167
  172.8 3.8 %all-to-all-done.2 = f32[32,1,4096]{2,1,0:T(1,128)} async-done(((f32[32,1,4096]{2,1,0:T(1,128)}), f32[32,1,4096]{2,1,0:T(1,128)}, u32[]{:S(2)}, u32[]{:S(2)}) %all-to-all-start.2) | async-done | bytes 524320 | tf_op jit(solution)/shard_map/all_to_all | solution.py:157
  176.6 7.0 %all-to-all-start.1 = ((bf16[32,512,64]{1,2,0:T(8,128)(2,1)}), bf16[32,512,64]{1,2,0:T(8,128)(2,1)}, u32[]{:S(2)}, u32[]{:S(2)}) async-start(bf16[32,512,64]{1,2,0:T(8,128)(2,1)} %copy.45), calls=%async_computation.2 | async-start | bytes 4194304 | tf_op jit(solution)/shard_map/all_to_all | solution.py:168
  183.6 0.9 reshape_reshape.6
  184.5 1.6 fusion.11
  186.1 2.3 fusion
  188.4 0.5 broadcast.95
  188.9 2.9 %reduce.1 = f32[32,4096]{1,0:T(8,128)S(1)} reduce(f32[32,1,4096]{2,1,0:T(1,128)} %all-to-all-done.2, f32[]{:T(128)} %broadcast.95), dimensions={1}, to_apply=%all_to_all.11.reduce_sub_computation | reduce | bytes 1048580 | tf_op jit(solution)/shard_map/all_to_all | solution.py:157
  191.8 0.4 reshape.133
  192.3 1.0 convolution_convert_fusion.2
  193.3 0.8 reshape.111.refs_0_
  194.1 31.5 %shard_map.104 = bf16[16,32,1024]{2,1,0:T(8,128)(2,1)} custom-call(bf16[1,32,1024]{2,1,0:T(8,128)(2,1)} %reshape.111.refs_0_), custom_call_target="tpu_custom_call" | custom-call | bytes 2097152 | tf_op jit(solution)/shard_map/pallas_call | solution.py:74
  225.6 3.0 %reshape.112 = bf16[16,8,64,64]{3,2,1,0:T(8,128)(2,1)S(1)} reshape(bf16[16,32,1024]{2,1,0:T(8,128)(2,1)} %shard_map.104) | data formatting | bytes 2097152 | tf_op jit(solution)/shard_map/reshape | solution.py:173
  228.6 2.8 %copy.53 = bf16[8,64,16,64]{3,2,1,0:T(8,128)(2,1)} copy(bf16[8,64,16,64]{3,1,0,2:T(8,128)(2,1)S(1)} %bitcast.59) | data formatting | bytes 2097152 | tf_op jit(solution)/shard_map/transpose | solution.py:174
  231.4 4.1 %reshape.113 = bf16[8,64,1024]{2,1,0:T(8,128)(2,1)} reshape(bf16[8,64,16,64]{3,2,1,0:T(8,128)(2,1)} %copy.53) | data formatting | bytes 2097152 | tf_op jit(solution)/shard_map/reshape | solution.py:174
  235.5 2.8 %fusion.3 = bf16[8,512,64]{1,0,2:T(8,128)(2,1)S(1)} fusion(bf16[32,512,64]{1,2,0:T(8,128)(2,1)} %all-to-all-done.1, s32[32]{0:T(128)S(1)} %fusion.21, pred[32]{0:T(512)(128)(4,1)S(1)} %get-tuple-element.20), kind=kOutput, calls=%fused_computation.10 | convolution fusion | flops 17039872 | bytes 2621600 | tf_op jit(solution)/shard_map/ra,rdk->adk/dot_general | solution.py:169
  238.3 1.0 copy.54
  239.2 1.9 fusion.7
  (33 shorter events, 0.9 us)
Async XLA Ops:
  7.2 1.2 copy-start
  7.2 232.1 %reduce-scatter.2.cloned.1.call-start = ((), (), s32[]{:S(2)}) async-start(), calls=%async_computation.4 | async-start | bytes 4456448 | tf_op jit(solution)/shard_map/reduce_scatter | solution.py:124
  12.8 1.3 copy-start.4
  12.8 1.3 copy-start.5
  12.8 1.8 copy-start.3
  20.8 68.6 %all-to-all-start = ((bf16[32,576,64]{1,2,0:T(8,128)(2,1)}), bf16[32,576,64]{1,2,0:T(8,128)(2,1)}, u32[]{:S(2)}, u32[]{:S(2)}) async-start(bf16[32,576,64]{1,2,0:T(8,128)(2,1)} %broadcast_select_fusion), calls=%async_computation.1 | async-start | bytes 5242880 | tf_op jit(solution)/shard_map/all_to_all | solution.py:114
  91.9 1.9 copy-start.2
  142.9 1.2 slice-start
  151.7 2.3 copy-start.1
  159.3 17.3 %all-to-all-start.2 = ((f32[32,1,4096]{2,1,0:T(1,128)}), f32[32,1,4096]{2,1,0:T(1,128)}, u32[]{:S(2)}, u32[]{:S(2)}) async-start(f32[32,1,4096]{2,1,0:T(1,128)} %reshape.132), calls=%async_computation.3 | async-start | bytes 1048576 | tf_op jit(solution)/shard_map/all_to_all | solution.py:157
  176.6 58.9 %all-to-all-start.1 = ((bf16[32,512,64]{1,2,0:T(8,128)(2,1)}), bf16[32,512,64]{1,2,0:T(8,128)(2,1)}, u32[]{:S(2)}, u32[]{:S(2)}) async-start(bf16[32,512,64]{1,2,0:T(8,128)(2,1)} %copy.45), calls=%async_computation.2 | async-start | bytes 4194304 | tf_op jit(solution)/shard_map/all_to_all | solution.py:168
  184.5 1.6 copy-start.6
Sparse Core Ops, SparseCore 0:
  13.0 102.1 reduce-scatter.1

commit v9 on v8

--- a/solution.py
+++ b/solution.py
@@ -115,9 +115,8 @@
     mine_got = jnp.take(got, my_owner, axis=0)
     panel_a = mine_got[:, :width_dev]
     panel_b_cols = mine_got[:, width_dev:]
-    (cot_all,) = ring_gather([cotangent[None]], n_split, 0)
-    cot_all = cot_all.reshape(rows, kv_full)
-    cot_blocks = cot_all.reshape(blocks, BLOCK_ROWS, kv_full)
+    early = own_rows // 2
+    (cot_early,) = ring_gather([cotangent[None, :early]], n_split, 0, pieces=2)
 
     token_blocks = tokens.reshape(blocks, BLOCK_ROWS, width_dev)
     partial_value = jnp.dot(tokens, value_weight, preferred_element_type=jnp.float32)
@@ -126,13 +125,22 @@
         "bnd,bdk->bnk", token_blocks, panel_a, preferred_element_type=jnp.float32
     ).astype(jnp.bfloat16)
     down_rows = down_part.size // kv_full
+    up_rows = panel_b_cols.size // kv_full
     packed = jnp.concatenate(
-        [down_part.reshape(down_rows, kv_full), panel_b_cols.reshape(-1, kv_full)], axis=0
-    )
-    (parts,) = ring_gather([packed[None]], n_split, 1, pieces=3)
+        [
+            down_part.reshape(down_rows, kv_full),
+            panel_b_cols.reshape(up_rows, kv_full),
+            cotangent[early:],
+        ],
+        axis=0,
+    )
+    (parts,) = ring_gather([packed[None]], n_split, 1, pieces=8)
+    cot_all = jnp.concatenate([cot_early, parts[:, down_rows + up_rows:]], axis=1)
+    cot_all = cot_all.reshape(rows, kv_full)
+    cot_blocks = cot_all.reshape(blocks, BLOCK_ROWS, kv_full)
     down = jnp.sum(parts[:, :down_rows].astype(jnp.float32), axis=0)
     down = down.astype(jnp.bfloat16).reshape(blocks, BLOCK_ROWS, RANK)
-    parts_up = parts[:, down_rows:].reshape(n_split, blocks, RANK, kv_part)
+    parts_up = parts[:, down_rows:down_rows + up_rows].reshape(n_split, blocks, RANK, kv_part)
     panel_b = parts_up.transpose(1, 2, 0, 3).reshape(blocks, RANK, kv_full)
     back = jnp.einsum(
         "bnc,bkc->bnk", cot_blocks, panel_b, preferred_element_type=jnp.float32

time: 249 us -> 253 us (1.016)
  local copies, waits for them, and re-layouts: 37.2 us -> 44.8 us
  waiting for transfers between devices: 3.82 us -> 0.03 us
    all_to_all x1, waiting for transfers between devices: 3.8 us -> 0.01 us  [per_device(): lax.all_to_all(send_gb, 'dp', split_axis=0, concat_axis=0, tiled=True)]
    unnamed x17 -> x19, local copies, waits for them, and re-layouts: 5.24 us -> 5.89 us
  transfers between devices with their start and end apart: 4 -> 4, of which waited for: 1 -> 0; matrix products, arithmetic and copies ran while one was open for 23% -> 26% of each run, Pallas kernels for 56% -> 55%
where the time goes in v9:
time: 253 us; the launch traced here: 251 us
  Pallas kernels  138 us (55%)
  local copies, waits for them, and re-layouts  44.8 us (18%)
  starting transfers between devices  25.1 us (10%)
  matrix products  18.7 us (7%)
  between operations  14.4 us (6%)
  other arithmetic  10.1 us (4%)
    pallas_call x3, Pallas kernels, ring_gather(): pl.pallas_call(functools.partial(_ring_kernel, n, k, pieces), out_shape=o...  138 us
    all_to_all x1, starting transfers between devices, per_device(): lax.all_to_all(jnp.take(both, wanted, axis=0), 'dp', split_axis=0, concat...  10.3 us
    all_to_all x1, starting transfers between devices, per_device(): lax.all_to_all(send_ga, 'dp', split_axis=0, concat_axis=0, tiled=True)  7.45 us
    all_to_all x1, starting transfers between devices, per_device(): lax.all_to_all(send_gb, 'dp', split_axis=0, concat_axis=0, tiled=True)  7.39 us
    unnamed x19, local copies, waits for them, and re-layouts  5.89 us
  transfers between devices with their start and end apart: 4, of which 0 were waited for; matrix products, arithmetic and copies ran while one was open for 26% of the time, Pallas kernels for 55%

profile of v9, /device:TPU:24, one launch (start us, length us, event | category | flops | bytes accessed | tf_op | source)
XLA Modules:
  0.0 251.1 jit_solution(2122563130535992108)
XLA Ops:
  7.2 1.2 copy-done
  8.4 4.4 %fusion.46 = f32[1024,1024]{1,0:T(8,128)} fusion(bf16[1024,512]{1,0:T(8,128)(2,1)S(1)} %copy-done, bf16[512,1024]{1,0:T(8,128)(2,1)} %param.8), kind=kOutput, calls=%fused_computation.76 | convolution fusion | flops 1073741824 | bytes 6291456 | tf_op jit(solution)/shard_map/dot_general | solution.py:122
  12.9 0.6 copy-done.5
  13.5 0.2 select_reduce_fusion
  13.9 1.0 constant_dynamic-slice_fusion
  15.3 2.4 gather_fusion
  17.7 3.6 %broadcast_select_fusion = bf16[32,576,64]{1,2,0:T(8,128)(2,1)} fusion(bf16[32,576,64]{1,2,0:T(8,128)(2,1)} %gather_fusion, pred[32]{0:T(512)(128)(4,1)S(1)} %compare_and_fusion), kind=kLoop, calls=%fused_computation.2 | loop fusion | flops 1179648 | bytes 4718624 | tf_op jit(solution)/shard_map/jit(_take)/select_n | solution.py:114
  21.3 10.3 %all-to-all-start = ((bf16[32,576,64]{1,2,0:T(8,128)(2,1)}), bf16[32,576,64]{1,2,0:T(8,128)(2,1)}, u32[]{:S(2)}, u32[]{:S(2)}) async-start(bf16[32,576,64]{1,2,0:T(8,128)(2,1)} %broadcast_select_fusion), calls=%async_computation.1 | async-start | bytes 5242880 | tf_op jit(solution)/shard_map/all_to_all | solution.py:114
  31.6 0.6 slice_bitcast_fusion
  32.3 43.0 %shard_map.103 = bf16[16,32,1024]{2,1,0:T(8,128)(2,1)} custom-call(bf16[1,32,1024]{2,1,0:T(8,128)(2,1)} %get-tuple-element.27.refs_0_), custom_call_target="tpu_custom_call" | custom-call | bytes 2097152 | tf_op jit(solution)/shard_map/pallas_call | solution.py:74
  75.3 2.4 gather_fusion.1
  78.2 0.5 fusion.8
  78.7 0.2 copy.41
  78.9 0.2 reshape.104
  79.1 0.7 maximum_bitcast_fusion.refs_0_
  79.8 63.9 %shard_map.102 = bf16[16,128,1024]{2,1,0:T(8,128)(2,1)} custom-call(bf16[1,128,1024]{2,1,0:T(8,128)(2,1)} %maximum_bitcast_fusion.refs_0_), custom_call_target="tpu_custom_call" | custom-call | bytes 8388608 | tf_op jit(solution)/shard_map/pallas_call | solution.py:74
  143.7 1.9 slice_reduce_fusion
  145.7 0.2 reshape.110
  145.9 2.9 %fusion.45 = (bf16[16,32,1024]{2,1,0:T(8,128)(2,1)S(1)}, bf16[16,32,1024]{2,1,0:T(8,128)(2,1)}) fusion(bf16[16,128,1024]{2,1,0:T(8,128)(2,1)} %shard_map.102), kind=kLoop, calls=%fused_computation.75 | loop fusion | bytes 4194304 | tf_op jit(solution)/shard_map/slice | solution.py:138
  148.7 0.2 pad_maximum_fusion
  149.0 0.3 fusion.16
  149.3 0.7 fusion.14
  150.0 1.6 copy.50
  151.6 2.7 %reshape.132 = f32[32,1,4096]{2,1,0:T(1,128)} reshape(f32[32,64,64]{2,1,0:T(8,128)} %copy.50) | data formatting | bytes 1048576
  154.2 7.4 %all-to-all-start.2 = ((f32[32,1,4096]{2,1,0:T(1,128)}), f32[32,1,4096]{2,1,0:T(1,128)}, u32[]{:S(2)}, u32[]{:S(2)}) async-start(f32[32,1,4096]{2,1,0:T(1,128)} %reshape.132), calls=%async_computation.3 | async-start | bytes 1048576 | tf_op jit(solution)/shard_map/all_to_all | solution.py:165
  161.6 4.1 %reshape.106 = bf16[16,8,64,64]{3,2,1,0:T(8,128)(2,1)} reshape(bf16[16,32,1024]{2,1,0:T(8,128)(2,1)} %get-tuple-element.26) | data formatting | bytes 2097152 | tf_op jit(solution)/shard_map/reshape | solution.py:143
  165.7 4.3 %copy.43 = bf16[8,64,16,64]{3,2,1,0:T(8,128)(2,1)} copy(bf16[8,64,16,64]{3,1,0,2:T(8,128)(2,1)} %bitcast.59) | data formatting | bytes 2097152 | tf_op jit(solution)/shard_map/transpose | solution.py:144
  170.0 4.1 %reshape.107 = bf16[8,64,1024]{2,1,0:T(8,128)(2,1)} reshape(bf16[8,64,16,64]{3,2,1,0:T(8,128)(2,1)} %copy.43) | data formatting | bytes 2097152 | tf_op jit(solution)/shard_map/reshape | solution.py:144
  174.1 2.1 convolution_convert_fusion.3
  176.1 0.3 fusion.6
  176.4 0.8 convolution_convert_fusion
  177.3 2.5 %copy.45 = bf16[32,512,64]{1,2,0:T(8,128)(2,1)} copy(bf16[32,512,64]{1,0,2:T(8,128)(2,1)S(1)} %convolution_convert_fusion) | data formatting | bytes 4194304 | tf_op jit(solution)/shard_map/convert_element_type | solution.py:175
  179.8 7.4 %all-to-all-start.1 = ((bf16[32,512,64]{1,2,0:T(8,128)(2,1)}), bf16[32,512,64]{1,2,0:T(8,128)(2,1)}, u32[]{:S(2)}, u32[]{:S(2)}) async-start(bf16[32,512,64]{1,2,0:T(8,128)(2,1)} %copy.45), calls=%async_computation.2 | async-start | bytes 4194304 | tf_op jit(solution)/shard_map/all_to_all | solution.py:176
  187.2 0.9 reshape_reshape.6
  188.1 1.6 fusion.11
  189.8 2.3 fusion
  192.0 0.5 broadcast.95
  192.6 2.9 %reduce.1 = f32[32,4096]{1,0:T(8,128)S(1)} reduce(f32[32,1,4096]{2,1,0:T(1,128)} %all-to-all-done.2, f32[]{:T(128)} %broadcast.95), dimensions={1}, to_apply=%all_to_all.11.reduce_sub_computation | reduce | bytes 1048580 | tf_op jit(solution)/shard_map/all_to_all | solution.py:165
  195.5 0.4 reshape.133
  195.9 1.0 convolution_convert_fusion.2
  197.0 0.8 reshape.111.refs_0_
  197.8 31.0 %shard_map.104 = bf16[16,32,1024]{2,1,0:T(8,128)(2,1)} custom-call(bf16[1,32,1024]{2,1,0:T(8,128)(2,1)} %reshape.111.refs_0_), custom_call_target="tpu_custom_call" | custom-call | bytes 2097152 | tf_op jit(solution)/shard_map/pallas_call | solution.py:74
  228.7 3.0 %reshape.112 = bf16[16,8,64,64]{3,2,1,0:T(8,128)(2,1)S(1)} reshape(bf16[16,32,1024]{2,1,0:T(8,128)(2,1)} %shard_map.104) | data formatting | bytes 2097152 | tf_op jit(solution)/shard_map/reshape | solution.py:181
  231.7 2.8 %copy.53 = bf16[8,64,16,64]{3,2,1,0:T(8,128)(2,1)} copy(bf16[8,64,16,64]{3,1,0,2:T(8,128)(2,1)S(1)} %bitcast.60) | data formatting | bytes 2097152 | tf_op jit(solution)/shard_map/transpose | solution.py:182
  234.5 4.1 %reshape.113 = bf16[8,64,1024]{2,1,0:T(8,128)(2,1)} reshape(bf16[8,64,16,64]{3,2,1,0:T(8,128)(2,1)} %copy.53) | data formatting | bytes 2097152 | tf_op jit(solution)/shard_map/reshape | solution.py:182
  238.6 2.8 %fusion.3 = bf16[8,512,64]{1,0,2:T(8,128)(2,1)S(1)} fusion(bf16[32,512,64]{1,2,0:T(8,128)(2,1)} %all-to-all-done.1, s32[32]{0:T(128)S(1)} %fusion.21, pred[32]{0:T(512)(128)(4,1)S(1)} %get-tuple-element.20), kind=kOutput, calls=%fused_computation.11 | convolution fusion | flops 17039872 | bytes 2621600 | tf_op jit(solution)/shard_map/ra,rdk->adk/dot_general | solution.py:177
  241.4 1.0 copy.54
  242.3 1.9 fusion.7
  (36 shorter events, 1.2 us)
Async XLA Ops:
  7.2 1.2 copy-start
  7.2 235.2 %reduce-scatter.2.cloned.1.call-start = ((), (), s32[]{:S(2)}) async-start(), calls=%async_computation.4 | async-start | bytes 4456448 | tf_op jit(solution)/shard_map/reduce_scatter | solution.py:123
  12.8 0.7 copy-start.5
  12.8 0.7 copy-start.6
  12.8 2.4 copy-start.3
  21.3 10.3 %copy-start.4 = (bf16[64,1024]{1,0:T(8,128)(2,1)S(1)}, bf16[64,1024]{1,0:T(8,128)(2,1)}, u32[]{:S(2)}) copy-start(bf16[64,1024]{1,0:T(8,128)(2,1)} %param.11) | copy-start | bytes 393220
  21.3 54.0 %all-to-all-start = ((bf16[32,576,64]{1,2,0:T(8,128)(2,1)}), bf16[32,576,64]{1,2,0:T(8,128)(2,1)}, u32[]{:S(2)}, u32[]{:S(2)}) async-start(bf16[32,576,64]{1,2,0:T(8,128)(2,1)} %broadcast_select_fusion), calls=%async_computation.1 | async-start | bytes 5242880 | tf_op jit(solution)/shard_map/all_to_all | solution.py:114
  77.9 65.8 %copy-start.1 = (bf16[8,576,64]{1,2,0:T(8,128)(2,1)}, bf16[8,576,64]{1,2,0:T(8,128)(2,1)S(1)}, u32[]{:S(2)}) copy-start(bf16[8,576,64]{1,2,0:T(8,128)(2,1)S(1)} %broadcast_select_fusion.1) | copy-start | bytes 1769476
  145.9 2.9 %copy-start.2 = (bf16[16,32,1024]{2,1,0:T(8,128)(2,1)S(1)}, bf16[16,32,1024]{2,1,0:T(8,128)(2,1)}, u32[]{:S(2)}) copy-start(bf16[16,32,1024]{2,1,0:T(8,128)(2,1)} %shard_map.103) | copy-start | bytes 3145732
  154.2 25.5 %all-to-all-start.2 = ((f32[32,1,4096]{2,1,0:T(1,128)}), f32[32,1,4096]{2,1,0:T(1,128)}, u32[]{:S(2)}, u32[]{:S(2)}) async-start(f32[32,1,4096]{2,1,0:T(1,128)} %reshape.132), calls=%async_computation.3 | async-start | bytes 1048576 | tf_op jit(solution)/shard_map/all_to_all | solution.py:165
  179.8 58.8 %all-to-all-start.1 = ((bf16[32,512,64]{1,2,0:T(8,128)(2,1)}), bf16[32,512,64]{1,2,0:T(8,128)(2,1)}, u32[]{:S(2)}, u32[]{:S(2)}) async-start(bf16[32,512,64]{1,2,0:T(8,128)(2,1)} %copy.45), calls=%async_computation.2 | async-start | bytes 4194304 | tf_op jit(solution)/shard_map/all_to_all | solution.py:176
  188.1 1.6 copy-start.7
Sparse Core Ops, SparseCore 0:
  13.0 95.6 reduce-scatter.1

commit v10 on v8

--- a/solution.py
+++ b/solution.py
@@ -109,8 +109,9 @@
     my_owner = lax.dynamic_index_in_dim(owner_all, myself, 0, keepdims=False)
     select_mask = my_owner[:, None] == jnp.arange(n_owners, dtype=jnp.int32)[None, :]
 
-    up_cols = lax.dynamic_slice_in_dim(up_panels, my_part * kv_part, kv_part, 2)
-    both = jnp.concatenate([down_panels, up_cols], axis=1)
+    share = RANK // n_split
+    up_rows_mine = lax.dynamic_slice_in_dim(up_panels, my_part * share, share, 1)
+    both = jnp.concatenate([down_panels, up_rows_mine.reshape(stored, -1, RANK)], axis=1)
     got = lax.all_to_all(jnp.take(both, wanted, axis=0), "dp", split_axis=0, concat_axis=0, tiled=True)
     mine_got = jnp.take(got, my_owner, axis=0)
     panel_a = mine_got[:, :width_dev]
@@ -132,23 +133,23 @@
     (parts,) = ring_gather([packed[None]], n_split, 1, pieces=3)
     down = jnp.sum(parts[:, :down_rows].astype(jnp.float32), axis=0)
     down = down.astype(jnp.bfloat16).reshape(blocks, BLOCK_ROWS, RANK)
-    parts_up = parts[:, down_rows:].reshape(n_split, blocks, RANK, kv_part)
-    panel_b = parts_up.transpose(1, 2, 0, 3).reshape(blocks, RANK, kv_full)
+    parts_up = parts[:, down_rows:].reshape(n_split, blocks, share, kv_full)
     back = jnp.einsum(
-        "bnc,bkc->bnk", cot_blocks, panel_b, preferred_element_type=jnp.float32
-    ).astype(jnp.bfloat16)
+        "bnc,jbqc->bnjq", cot_blocks, parts_up, preferred_element_type=jnp.float32
+    ).reshape(blocks, BLOCK_ROWS, RANK).astype(jnp.bfloat16)
 
     first_row = my_part * own_rows
     my_down = lax.dynamic_slice_in_dim(down.reshape(rows, RANK), first_row, own_rows, 0)
-    my_up = lax.dynamic_index_in_dim(panel_b, first_row // BLOCK_ROWS, 0, keepdims=False)
+    my_up = lax.dynamic_index_in_dim(parts_up, first_row // BLOCK_ROWS, 1, keepdims=False)
+    my_up = my_up.reshape(RANK, kv_full)
     lifted = jnp.dot(my_down, my_up, preferred_element_type=jnp.float32)
     projected = (base + lifted).astype(jnp.bfloat16)
 
     select_bf = select_mask.astype(jnp.bfloat16)
     pick_bf = pick_mask.astype(jnp.bfloat16)
-    cot_share = lax.dynamic_slice_in_dim(cot_blocks, my_part * kv_part, kv_part, 2)
+    down_share = lax.dynamic_slice_in_dim(down, my_part * share, share, 2)
     block_grad_b = jnp.einsum(
-        "bnk,bnc->bkc", down, cot_share, preferred_element_type=jnp.float32
+        "bnq,bnc->bqc", down_share, cot_blocks, preferred_element_type=jnp.float32
     )
     send_gb = jnp.einsum(
         "bo,bkc->okc", select_mask.astype(jnp.float32), block_grad_b,
@@ -170,8 +171,8 @@
         "ra,rdk->adk", pick_bf, recv_ga, preferred_element_type=jnp.float32
     ).astype(jnp.bfloat16)
     (shares,) = ring_gather([grad_share.reshape(1, -1, kv_full)], n_split, 2, pieces=2)
-    shares = shares.reshape(n_split, stored, RANK, kv_part)
-    grad_up = shares.transpose(1, 2, 0, 3).reshape(stored, RANK, kv_full)
+    shares = shares.reshape(n_split, stored, share, kv_full)
+    grad_up = shares.transpose(1, 0, 2, 3).reshape(stored, RANK, kv_full)
 
     grad_base = jnp.einsum("nc,dc->nd", cot_all, value_weight, preferred_element_type=jnp.float32)
     through = jnp.einsum("bnk,bdk->bnd", back, panel_a, preferred_element_type=jnp.float32)

time: 249 us -> 235 us (0.944)
  local copies, waits for them, and re-layouts: 37.2 us -> 24.5 us
  other arithmetic: 10.1 us -> 5.35 us
    reshape x4 -> x6, local copies, waits for them, and re-layouts: 11.7 us -> 5.11 us  [the longest x1 2.24 us: per_device(): parts_up = parts[:, down_rows:].reshape(n_split, blocks, share, kv_full)]
    transpose x2 -> x1, local copies, waits for them, and re-layouts: 5.76 us -> 0.42 us  [per_device(): grad_up = shares.transpose(1, 0, 2, 3).reshape(stored, RANK, kv_full)]
    all_to_all x1 -> x0, other arithmetic: 2.94 us -> none  [per_device(): lax.all_to_all(send_gb, 'dp', split_axis=0, concat_axis=0, tiled=True)]
  transfers between devices with their start and end apart: 4 -> 4, of which waited for: 1 -> 1; matrix products, arithmetic and copies ran while one was open for 23% -> 18% of each run, Pallas kernels for 56% -> 59%
where the time goes in v10:
time: 235 us; the launch traced here: 234 us
  Pallas kernels  139 us (59%)
  starting transfers between devices  24.7 us (11%)
  local copies, waits for them, and re-layouts  24.5 us (10%)
  matrix products  20.4 us (9%)
  between operations  14.4 us (6%)
  waiting for transfers between devices  5.92 us (3%)
  other arithmetic  5.35 us (2%)
    pallas_call x3, Pallas kernels, ring_gather(): pl.pallas_call(functools.partial(_ring_kernel, n, k, pieces), out_shape=o...  139 us
    all_to_all x1, starting transfers between devices, per_device(): lax.all_to_all(jnp.take(both, wanted, axis=0), 'dp', split_axis=0, concat...  10.1 us
    all_to_all x1, starting transfers between devices, per_device(): lax.all_to_all(send_gb, 'dp', split_axis=0, concat_axis=0, tiled=True)  7.56 us
    all_to_all x1, starting transfers between devices, per_device(): lax.all_to_all(send_ga, 'dp', split_axis=0, concat_axis=0, tiled=True)  7 us
    all_to_all x1, waiting for transfers between devices, per_device(): lax.all_to_all(send_gb, 'dp', split_axis=0, concat_axis=0, tiled=True)  5.89 us
  transfers between devices with their start and end apart: 4, of which 1 were waited for; matrix products, arithmetic and copies ran while one was open for 18% of the time, Pallas kernels for 59%

profile of v10, /device:TPU:24, one launch (start us, length us, event | category | flops | bytes accessed | tf_op | source)
XLA Modules:
  0.0 234.2 jit_solution(14301739102249294529)
XLA Ops:
  7.2 1.2 copy-done
  8.4 4.4 %fusion.47 = f32[1024,1024]{1,0:T(8,128)} fusion(bf16[1024,512]{1,0:T(8,128)(2,1)S(1)} %copy-done, bf16[512,1024]{1,0:T(8,128)(2,1)} %param.8), kind=kOutput, calls=%fused_computation.76 | convolution fusion | flops 1073741824 | bytes 6291456 | tf_op jit(solution)/shard_map/dot_general | solution.py:124
  12.8 0.6 copy-done.5
  13.5 0.2 select_reduce_fusion
  13.8 1.0 constant_dynamic-slice_fusion.1
  14.7 0.1 reshape.109
  14.9 0.1 copy.43
  15.0 0.1 fusion.45
  15.4 2.4 %gather_fusion = bf16[32,576,64]{1,2,0:T(8,128)(2,1)} fusion(bf16[8,576,64]{1,2,0:T(8,128)(2,1)S(1)} %pad_maximum_fusion, s32[1024]{0:T(1024)S(1)} %pad_clamp_fusion.1), kind=kCustom, calls=%fused_computation | custom fusion | bytes 4718720 | tf_op jit(solution)/shard_map/jit(_take)/gather | solution.py:115
  17.8 3.6 %broadcast_select_fusion = bf16[32,576,64]{1,2,0:T(8,128)(2,1)} fusion(bf16[32,576,64]{1,2,0:T(8,128)(2,1)} %gather_fusion, pred[32]{0:T(512)(128)(4,1)S(1)} %compare_and_fusion), kind=kLoop, calls=%fused_computation.2 | loop fusion | flops 1179648 | bytes 4718624 | tf_op jit(solution)/shard_map/jit(_take)/select_n | solution.py:115
  21.4 10.1 %all-to-all-start = ((bf16[32,576,64]{1,2,0:T(8,128)(2,1)}), bf16[32,576,64]{1,2,0:T(8,128)(2,1)}, u32[]{:S(2)}, u32[]{:S(2)}) async-start(bf16[32,576,64]{1,2,0:T(8,128)(2,1)} %broadcast_select_fusion), calls=%async_computation.1 | async-start | bytes 5242880 | tf_op jit(solution)/shard_map/all_to_all | solution.py:115
  31.5 58.2 %shard_map.103 = bf16[16,64,1024]{2,1,0:T(8,128)(2,1)} custom-call(bf16[1,64,1024]{2,1,0:T(8,128)(2,1)} %bitcast.58), custom_call_target="tpu_custom_call" | custom-call | bytes 4194304 | tf_op jit(solution)/shard_map/pallas_call | solution.py:74
  89.8 2.4 %gather_fusion.1 = bf16[8,576,64]{1,2,0:T(8,128)(2,1)S(1)} fusion(bf16[32,576,64]{1,2,0:T(8,128)(2,1)} %all-to-all-done, s32[1024]{0:T(1024)S(1)} %pad_clamp_fusion), kind=kCustom, calls=%fused_computation.1 | custom fusion | bytes 1179680 | tf_op jit(solution)/shard_map/jit(_take)/gather | solution.py:116
  92.3 0.1 broadcast_select_fusion.1
  92.4 0.1 copy.45
  92.6 0.1 reshape.112
  92.7 0.5 fusion.9
  93.2 0.2 copy.44
  93.4 0.2 reshape.111
  93.6 0.7 maximum_bitcast_fusion.refs_0_
  94.3 48.3 %shard_map.102 = bf16[16,96,1024]{2,1,0:T(8,128)(2,1)} custom-call(bf16[1,96,1024]{2,1,0:T(8,128)(2,1)} %maximum_bitcast_fusion.refs_0_), custom_call_target="tpu_custom_call" | custom-call | bytes 6291456 | tf_op jit(solution)/shard_map/pallas_call | solution.py:74
  142.6 2.4 %slice.15 = bf16[16,32,1024]{2,1,0:T(8,128)(2,1)} slice(bf16[16,96,1024]{2,1,0:T(8,128)(2,1)} %shard_map.102), slice={[0:16], [64:96], [0:1024]} | slice | bytes 2097152 | tf_op jit(solution)/shard_map/slice | solution.py:136
  145.1 2.2 reshape.113
  147.3 2.4 %fusion.8 = bf16[8,128,16,4]{1,2,3,0:T(8,128)(2,1)S(1)} fusion(bf16[8,128,1024,1]{2,1,3,0:T(8,128)(2,1)S(1)} %bitcast.52, bf16[16,8,4,1024]{3,2,1,0:T(4,128)(2,1)} %reshape.113), kind=kOutput, calls=%fused_computation.16 | convolution fusion | flops 134283264 | bytes 3276800 | tf_op jit(solution)/shard_map/bnc,jbqc->bnjq/dot_general | solution.py:137
  149.8 0.3 slice_reduce_fusion
  150.1 0.9 reshape.117
  151.0 1.5 fusion.16
  152.5 0.5 fusion.18
  153.0 1.1 copy.55
  154.1 7.6 %all-to-all-start.2 = ((f32[32,4,1024]{2,1,0:T(4,128)}), f32[32,4,1024]{2,1,0:T(4,128)}, u32[]{:S(2)}, u32[]{:S(2)}) async-start(f32[32,4,1024]{2,1,0:T(4,128)} %copy.55), calls=%async_computation.3 | async-start | bytes 1048576 | tf_op jit(solution)/shard_map/all_to_all | solution.py:158
  161.7 0.3 fusion.6
  162.0 0.8 convolution_convert_fusion
  162.8 2.5 %copy.51 = bf16[32,512,64]{1,2,0:T(8,128)(2,1)} copy(bf16[32,512,64]{1,0,2:T(8,128)(2,1)S(1)} %convolution_convert_fusion) | data formatting | bytes 4194304 | tf_op jit(solution)/shard_map/convert_element_type | solution.py:168
  165.3 5.9 %all-to-all-done.2 = f32[32,4,1024]{2,1,0:T(4,128)} async-done(((f32[32,4,1024]{2,1,0:T(4,128)}), f32[32,4,1024]{2,1,0:T(4,128)}, u32[]{:S(2)}, u32[]{:S(2)}) %all-to-all-start.2) | async-done | bytes 524320 | tf_op jit(solution)/shard_map/all_to_all | solution.py:158
  171.2 7.0 %all-to-all-start.1 = ((bf16[32,512,64]{1,2,0:T(8,128)(2,1)}), bf16[32,512,64]{1,2,0:T(8,128)(2,1)}, u32[]{:S(2)}, u32[]{:S(2)}) async-start(bf16[32,512,64]{1,2,0:T(8,128)(2,1)} %copy.51), calls=%async_computation.2 | async-start | bytes 4194304 | tf_op jit(solution)/shard_map/all_to_all | solution.py:169
  178.2 0.9 reshape_reshape.6
  179.2 0.9 constant_dynamic-slice_fusion
  180.2 1.6 fusion.13
  181.8 2.3 fusion
  184.1 1.6 convolution_convert_fusion.4
  185.7 0.6 reshape.118.refs_0_
  186.4 32.4 %shard_map.104 = bf16[16,32,1024]{2,1,0:T(8,128)(2,1)} custom-call(bf16[1,32,1024]{2,1,0:T(8,128)(2,1)} %reshape.118.refs_0_), custom_call_target="tpu_custom_call" | custom-call | bytes 2097152 | tf_op jit(solution)/shard_map/pallas_call | solution.py:74
  218.8 1.5 reshape.119
  220.3 0.4 copy.58
  220.7 1.1 reshape.120
  221.8 2.8 %fusion.3 = bf16[8,512,64]{1,0,2:T(8,128)(2,1)S(1)} fusion(bf16[32,512,64]{1,2,0:T(8,128)(2,1)} %all-to-all-done.1, s32[32]{0:T(128)S(1)} %fusion.23, pred[32]{0:T(512)(128)(4,1)S(1)} %get-tuple-element.20), kind=kOutput, calls=%fused_computation.10 | convolution fusion | flops 17039872 | bytes 2621600 | tf_op jit(solution)/shard_map/ra,rdk->adk/dot_general | solution.py:170
  224.7 1.0 copy.59
  225.6 1.8 fusion.7
  (32 shorter events, 0.6 us)
Async XLA Ops:
  7.2 1.2 copy-start
  7.2 218.4 %reduce-scatter.2.cloned.1.call-start = ((), (), s32[]{:S(2)}) async-start(), calls=%async_computation.4 | async-start | bytes 4456448 | tf_op jit(solution)/shard_map/reduce_scatter | solution.py:125
  12.8 0.7 copy-start.5
  12.8 0.7 copy-start.6
  12.8 2.5 %copy-start.4 = (bf16[8,512,64]{1,2,0:T(8,128)(2,1)S(1)}, bf16[8,512,64]{1,2,0:T(8,128)(2,1)}, u32[]{:S(2)}) copy-start(bf16[8,512,64]{1,2,0:T(8,128)(2,1)} %param.9) | copy-start | bytes 1572868
  21.4 68.4 %all-to-all-start = ((bf16[32,576,64]{1,2,0:T(8,128)(2,1)}), bf16[32,576,64]{1,2,0:T(8,128)(2,1)}, u32[]{:S(2)}, u32[]{:S(2)}) async-start(bf16[32,576,64]{1,2,0:T(8,128)(2,1)} %broadcast_select_fusion), calls=%async_computation.1 | async-start | bytes 5242880 | tf_op jit(solution)/shard_map/all_to_all | solution.py:115
  92.4 1.9 copy-start.3
  142.6 4.7 %copy-start.1 = (bf16[16,64,1024]{2,1,0:T(8,128)(2,1)S(1)}, bf16[16,64,1024]{2,1,0:T(8,128)(2,1)}, u32[]{:S(2)}) copy-start(bf16[16,64,1024]{2,1,0:T(8,128)(2,1)} %shard_map.103) | copy-start | bytes 6291460
  147.3 2.5 %copy-start.2 = (bf16[16,96,1024]{2,1,0:T(8,128)(2,1)S(1)}, bf16[16,96,1024]{2,1,0:T(8,128)(2,1)}, u32[]{:S(2)}) copy-start(bf16[16,96,1024]{2,1,0:T(8,128)(2,1)} %shard_map.102) | copy-start | bytes 9437188
  154.1 17.1 %all-to-all-start.2 = ((f32[32,4,1024]{2,1,0:T(4,128)}), f32[32,4,1024]{2,1,0:T(4,128)}, u32[]{:S(2)}, u32[]{:S(2)}) async-start(f32[32,4,1024]{2,1,0:T(4,128)} %copy.55), calls=%async_computation.3 | async-start | bytes 1048576 | tf_op jit(solution)/shard_map/all_to_all | solution.py:158
  171.2 50.6 %all-to-all-start.1 = ((bf16[32,512,64]{1,2,0:T(8,128)(2,1)}), bf16[32,512,64]{1,2,0:T(8,128)(2,1)}, u32[]{:S(2)}, u32[]{:S(2)}) async-start(bf16[32,512,64]{1,2,0:T(8,128)(2,1)} %copy.51), calls=%async_computation.2 | async-start | bytes 4194304 | tf_op jit(solution)/shard_map/all_to_all | solution.py:169
  180.1 1.6 copy-start.7
Sparse Core Ops, SparseCore 0:
  13.0 101.7 reduce-scatter.1

commit v11 on v10

--- a/solution.py
+++ b/solution.py
@@ -113,16 +113,17 @@
     up_rows_mine = lax.dynamic_slice_in_dim(up_panels, my_part * share, share, 1)
     both = jnp.concatenate([down_panels, up_rows_mine.reshape(stored, -1, RANK)], axis=1)
     got = lax.all_to_all(jnp.take(both, wanted, axis=0), "dp", split_axis=0, concat_axis=0, tiled=True)
+
+    (cot_all,) = ring_gather([cotangent[None]], n_split, 0)
+    got, cot_all = lax.optimization_barrier((got, cot_all))
     mine_got = jnp.take(got, my_owner, axis=0)
     panel_a = mine_got[:, :width_dev]
     panel_b_cols = mine_got[:, width_dev:]
-    (cot_all,) = ring_gather([cotangent[None]], n_split, 0)
     cot_all = cot_all.reshape(rows, kv_full)
     cot_blocks = cot_all.reshape(blocks, BLOCK_ROWS, kv_full)
 
     token_blocks = tokens.reshape(blocks, BLOCK_ROWS, width_dev)
     partial_value = jnp.dot(tokens, value_weight, preferred_element_type=jnp.float32)
-    base = lax.psum_scatter(partial_value, "mp", scatter_dimension=0, tiled=True)
     down_part = jnp.einsum(
         "bnd,bdk->bnk", token_blocks, panel_a, preferred_element_type=jnp.float32
     ).astype(jnp.bfloat16)
@@ -131,6 +132,8 @@
         [down_part.reshape(down_rows, kv_full), panel_b_cols.reshape(-1, kv_full)], axis=0
     )
     (parts,) = ring_gather([packed[None]], n_split, 1, pieces=3)
+    partial_value, parts = lax.optimization_barrier((partial_value, parts))
+    base = lax.psum_scatter(partial_value, "mp", scatter_dimension=0, tiled=True)
     down = jnp.sum(parts[:, :down_rows].astype(jnp.float32), axis=0)
     down = down.astype(jnp.bfloat16).reshape(blocks, BLOCK_ROWS, RANK)
     parts_up = parts[:, down_rows:].reshape(n_split, blocks, share, kv_full)

time: 235 us -> 214 us (0.911)
  Pallas kernels: 139 us -> 120 us
  local copies, waits for them, and re-layouts: 24.5 us -> 20.8 us
    pallas_call x3, Pallas kernels: 139 us -> 120 us  [ring_gather(): pl.pallas_call(functools.partial(_ring_kernel, n, k, pieces), out_shape=o...]
  transfers between devices with their start and end apart: 4 -> 4, of which waited for: 1 -> 1; matrix products, arithmetic and copies ran while one was open for 18% -> 14% of each run, Pallas kernels for 59% -> 37%
where the time goes in v11:
time: 214 us; the launch traced here: 213 us
  Pallas kernels  120 us (56%)
  starting transfers between devices  24.5 us (11%)
  local copies, waits for them, and re-layouts  20.8 us (10%)
  matrix products  19.8 us (9%)
  between operations  14.4 us (7%)
  other arithmetic  7.19 us (3%)
  waiting for transfers between devices  5.89 us (3%)
    pallas_call x3, Pallas kernels, ring_gather(): pl.pallas_call(functools.partial(_ring_kernel, n, k, pieces), out_shape=o...  120 us
    all_to_all x1, starting transfers between devices, per_device(): lax.all_to_all(jnp.take(both, wanted, axis=0), 'dp', split_axis=0, concat...  10.1 us
    all_to_all x1, starting transfers between devices, per_device(): lax.all_to_all(send_gb, 'dp', split_axis=0, concat_axis=0, tiled=True)  7.36 us
    all_to_all x1, starting transfers between devices, per_device(): lax.all_to_all(send_ga, 'dp', split_axis=0, concat_axis=0, tiled=True)  6.99 us
    all_to_all x1, waiting for transfers between devices, per_device(): lax.all_to_all(send_gb, 'dp', split_axis=0, concat_axis=0, tiled=True)  5.87 us
  transfers between devices with their start and end apart: 4, of which 1 were waited for; matrix products, arithmetic and copies ran while one was open for 14% of the time, Pallas kernels for 37%

profile of v11, /device:TPU:24, one launch (start us, length us, event | category | flops | bytes accessed | tf_op | source)
XLA Modules:
  0.0 213.0 jit_solution(8500109394075910969)
XLA Ops:
  7.2 1.0 select_reduce_fusion
  8.2 0.1 fusion.44
  8.5 0.9 constant_dynamic-slice_fusion.1
  9.5 0.1 reshape.109
  9.6 0.1 copy.43
  9.8 1.1 pad_maximum_fusion
  10.9 2.4 %gather_fusion = bf16[32,576,64]{1,2,0:T(8,128)(2,1)} fusion(bf16[8,576,64]{1,2,0:T(8,128)(2,1)S(1)} %pad_maximum_fusion, s32[1024]{0:T(1024)S(1)} %pad_clamp_fusion.1), kind=kCustom, calls=%fused_computation | custom fusion | bytes 4718720 | tf_op jit(solution)/shard_map/jit(_take)/gather | solution.py:115
  13.3 3.6 %broadcast_select_fusion = bf16[32,576,64]{1,2,0:T(8,128)(2,1)} fusion(bf16[32,576,64]{1,2,0:T(8,128)(2,1)} %gather_fusion, pred[32]{0:T(512)(128)(4,1)S(1)} %compare_and_fusion), kind=kLoop, calls=%fused_computation.2 | loop fusion | flops 1179648 | bytes 4718624 | tf_op jit(solution)/shard_map/jit(_take)/select_n | solution.py:115
  16.9 10.1 %all-to-all-start = ((bf16[32,576,64]{1,2,0:T(8,128)(2,1)}), bf16[32,576,64]{1,2,0:T(8,128)(2,1)}, u32[]{:S(2)}, u32[]{:S(2)}) async-start(bf16[32,576,64]{1,2,0:T(8,128)(2,1)} %broadcast_select_fusion), calls=%async_computation | async-start | bytes 5242880 | tf_op jit(solution)/shard_map/all_to_all | solution.py:115
  27.1 40.9 %shard_map.102 = bf16[16,64,1024]{2,1,0:T(8,128)(2,1)} custom-call(bf16[1,64,1024]{2,1,0:T(8,128)(2,1)} %bitcast.56), custom_call_target="tpu_custom_call" | custom-call | bytes 4194304 | tf_op jit(solution)/shard_map/pallas_call | solution.py:74
  68.1 3.2 %fusion.46 = f32[1024,1024]{1,0:T(8,128)} fusion(bf16[1024,512]{1,0:T(8,128)(2,1)S(1)} %copy-done, bf16[512,1024]{1,0:T(8,128)(2,1)S(1)} %copy-done.5), kind=kOutput, calls=%fused_computation.75 | convolution fusion | flops 1073741824 | bytes 6291456 | tf_op jit(solution)/shard_map/dot_general | solution.py:126
  71.2 2.4 %gather_fusion.1 = bf16[8,576,64]{1,2,0:T(8,128)(2,1)S(1)} fusion(bf16[32,576,64]{1,2,0:T(8,128)(2,1)} %all-to-all-done, s32[1024]{0:T(1024)S(1)} %pad_clamp_fusion), kind=kCustom, calls=%fused_computation.1 | custom fusion | bytes 1179680 | tf_op jit(solution)/shard_map/jit(_take)/gather | solution.py:119
  73.7 0.1 broadcast_select_fusion.1
  74.0 0.1 reshape.112
  74.1 0.5 fusion.8
  74.6 0.2 copy.44
  74.8 0.2 reshape.111
  75.0 0.7 maximum_bitcast_fusion.refs_0_
  75.7 42.0 %shard_map.103 = bf16[16,96,1024]{2,1,0:T(8,128)(2,1)} custom-call(bf16[1,96,1024]{2,1,0:T(8,128)(2,1)} %maximum_bitcast_fusion.refs_0_), custom_call_target="tpu_custom_call" | custom-call | bytes 6291456 | tf_op jit(solution)/shard_map/pallas_call | solution.py:74
  117.7 1.2 slice-done
  118.9 0.4 reshape.113
  119.4 1.0 copy-done.4
  120.3 3.0 %convolution_convert_fusion.2 = bf16[8,128,16,4]{1,2,3,0:T(8,128)(2,1)S(1)} fusion(bf16[8,128,1024,1]{2,1,3,0:T(8,128)(2,1)} %bitcast.50, bf16[16,8,4,1024]{3,2,1,0:T(4,128)(2,1)S(1)} %reshape.113), kind=kOutput, calls=%fused_computation.14 | convolution fusion | flops 134283264 | bytes 3276800 | tf_op jit(solution)/shard_map/bnc,jbqc->bnjq/dot_general | solution.py:140
  123.4 0.3 slice_reduce_fusion
  123.8 0.9 reshape.117
  124.6 0.2 copy-done.2
  124.9 1.5 fusion.15
  126.3 0.5 fusion.17
  126.8 1.1 copy.55
  128.0 7.4 %all-to-all-start.2 = ((f32[32,4,1024]{2,1,0:T(4,128)}), f32[32,4,1024]{2,1,0:T(4,128)}, u32[]{:S(2)}, u32[]{:S(2)}) async-start(f32[32,4,1024]{2,1,0:T(4,128)} %copy.55), calls=%async_computation.3 | async-start | bytes 1048576 | tf_op jit(solution)/shard_map/all_to_all | solution.py:161
  135.3 0.3 fusion.6
  135.6 0.8 convolution_convert_fusion
  136.5 2.5 %copy.51 = bf16[32,512,64]{1,2,0:T(8,128)(2,1)} copy(bf16[32,512,64]{1,0,2:T(8,128)(2,1)S(1)} %convolution_convert_fusion) | data formatting | bytes 4194304 | tf_op jit(solution)/shard_map/convert_element_type | solution.py:171
  139.0 5.9 %all-to-all-done.2 = f32[32,4,1024]{2,1,0:T(4,128)} async-done(((f32[32,4,1024]{2,1,0:T(4,128)}), f32[32,4,1024]{2,1,0:T(4,128)}, u32[]{:S(2)}, u32[]{:S(2)}) %all-to-all-start.2) | async-done | bytes 524320 | tf_op jit(solution)/shard_map/all_to_all | solution.py:161
  144.9 7.0 %all-to-all-start.1 = ((bf16[32,512,64]{1,2,0:T(8,128)(2,1)}), bf16[32,512,64]{1,2,0:T(8,128)(2,1)}, u32[]{:S(2)}, u32[]{:S(2)}) async-start(bf16[32,512,64]{1,2,0:T(8,128)(2,1)} %copy.51), calls=%async_computation.2 | async-start | bytes 4194304 | tf_op jit(solution)/shard_map/all_to_all | solution.py:172
  151.9 0.9 reshape_reshape.6
  152.8 1.0 constant_dynamic-slice_fusion
  153.8 1.6 fusion.12
  155.4 2.3 %fusion = bf16[1024,512]{1,0:T(8,128)(2,1)} fusion(f32[8,128,512]{2,1,0:T(8,128)S(1)} %fusion.12, bf16[1024,1024]{1,0:T(8,128)(2,1)S(1)} %bitcast.52, bf16[512,1024]{1,0:T(8,128)(2,1)S(1)} %copy-done.6), kind=kOutput, calls=%fused_computation.4 | convolution fusion | flops 1074790400 | bytes 6291456 | tf_op jit(solution)/shard_map/nc,dc->nd/dot_general | solution.py:180
  157.7 1.6 convolution_convert_fusion.4
  159.3 0.6 reshape.118.refs_0_
  160.0 37.6 %shard_map.104 = bf16[16,32,1024]{2,1,0:T(8,128)(2,1)} custom-call(bf16[1,32,1024]{2,1,0:T(8,128)(2,1)} %reshape.118.refs_0_), custom_call_target="tpu_custom_call" | custom-call | bytes 2097152 | tf_op jit(solution)/shard_map/pallas_call | solution.py:74
  197.6 1.5 reshape.119
  199.1 0.4 copy.58
  199.5 1.1 reshape.120
  200.6 2.8 %fusion.3 = bf16[8,512,64]{1,0,2:T(8,128)(2,1)S(1)} fusion(bf16[32,512,64]{1,2,0:T(8,128)(2,1)} %all-to-all-done.1, s32[32]{0:T(128)S(1)} %fusion.22, pred[32]{0:T(512)(128)(4,1)S(1)} %get-tuple-element.28), kind=kOutput, calls=%fused_computation.10 | convolution fusion | flops 17039872 | bytes 2621600 | tf_op jit(solution)/shard_map/ra,rdk->adk/dot_general | solution.py:173
  203.5 1.0 copy.59
  204.4 1.8 fusion.7
  (31 shorter events, 0.7 us)
Async XLA Ops:
  7.2 60.9 %copy-start = (bf16[1024,512]{1,0:T(8,128)(2,1)S(1)}, bf16[1024,512]{1,0:T(8,128)(2,1)}, u32[]{:S(2)}) copy-start(bf16[1024,512]{1,0:T(8,128)(2,1)} %param.7) | copy-start | bytes 3145732
  16.9 54.3 %all-to-all-start = ((bf16[32,576,64]{1,2,0:T(8,128)(2,1)}), bf16[32,576,64]{1,2,0:T(8,128)(2,1)}, u32[]{:S(2)}, u32[]{:S(2)}) async-start(bf16[32,576,64]{1,2,0:T(8,128)(2,1)} %broadcast_select_fusion), calls=%async_computation | async-start | bytes 5242880 | tf_op jit(solution)/shard_map/all_to_all | solution.py:115
  27.0 41.0 %copy-start.5 = (bf16[512,1024]{1,0:T(8,128)(2,1)S(1)}, bf16[512,1024]{1,0:T(8,128)(2,1)}, u32[]{:S(2)}) copy-start(bf16[512,1024]{1,0:T(8,128)(2,1)} %param.8) | copy-start | bytes 3145732
  27.1 177.4 %reduce-scatter.2.cloned.1.call-start = ((), (), s32[]{:S(2)}) async-start(), calls=%async_computation.4 | async-start | bytes 4456448 | tf_op jit(solution)/shard_map/reduce_scatter | solution.py:136
  73.8 43.9 %copy-start.3 = (bf16[8,576,64]{1,2,0:T(8,128)(2,1)}, bf16[8,576,64]{1,2,0:T(8,128)(2,1)S(1)}, u32[]{:S(2)}) copy-start(bf16[8,576,64]{1,2,0:T(8,128)(2,1)S(1)} %broadcast_select_fusion.1) | copy-start | bytes 1769476
  117.7 1.2 slice-start
  119.4 1.0 copy-start.4
  119.4 4.0 %copy-start.1 = (bf16[16,96,1024]{2,1,0:T(8,128)(2,1)S(1)}, bf16[16,96,1024]{2,1,0:T(8,128)(2,1)}, u32[]{:S(2)}) copy-start(bf16[16,96,1024]{2,1,0:T(8,128)(2,1)} %shard_map.103) | copy-start | bytes 9437188
  123.3 1.6 copy-start.2
  128.0 16.9 %all-to-all-start.2 = ((f32[32,4,1024]{2,1,0:T(4,128)}), f32[32,4,1024]{2,1,0:T(4,128)}, u32[]{:S(2)}, u32[]{:S(2)}) async-start(f32[32,4,1024]{2,1,0:T(4,128)} %copy.55), calls=%async_computation.3 | async-start | bytes 1048576 | tf_op jit(solution)/shard_map/all_to_all | solution.py:161
  144.9 55.8 %all-to-all-start.1 = ((bf16[32,512,64]{1,2,0:T(8,128)(2,1)}), bf16[32,512,64]{1,2,0:T(8,128)(2,1)}, u32[]{:S(2)}, u32[]{:S(2)}) async-start(bf16[32,512,64]{1,2,0:T(8,128)(2,1)} %copy.51), calls=%async_computation.2 | async-start | bytes 4194304 | tf_op jit(solution)/shard_map/all_to_all | solution.py:172
  153.8 1.6 copy-start.6
Sparse Core Ops, SparseCore 0:
  117.8 80.8 reduce-scatter.1

commit v12 on v11

--- a/solution.py
+++ b/solution.py
@@ -154,13 +154,12 @@
     block_grad_b = jnp.einsum(
         "bnq,bnc->bqc", down_share, cot_blocks, preferred_element_type=jnp.float32
     )
-    send_gb = jnp.einsum(
-        "bo,bkc->okc", select_mask.astype(jnp.float32), block_grad_b,
-        precision=lax.Precision.HIGHEST,
+    send_gb = jnp.sum(
+        jnp.where(select_mask[:, :, None, None], block_grad_b[:, None], 0.0), axis=0
     )
     recv_gb = lax.all_to_all(send_gb, "dp", split_axis=0, concat_axis=0, tiled=True)
-    grad_share = jnp.einsum(
-        "ra,rkc->akc", pick_mask.astype(jnp.float32), recv_gb, precision=lax.Precision.HIGHEST
+    grad_share = jnp.sum(
+        jnp.where(pick_mask[:, :, None, None], recv_gb[:, None], 0.0), axis=0
     ).astype(jnp.bfloat16)
 
     block_grad_a = jnp.einsum(

time: 214 us -> 215 us (level)
  no operation moved by 1% of the time
where the time goes in v12:
time: 215 us; the launch traced here: 214 us
  Pallas kernels  120 us (56%)
  starting transfers between devices  24.7 us (11%)
  local copies, waits for them, and re-layouts  20.8 us (10%)
  matrix products  18.9 us (9%)
  between operations  14.4 us (7%)
  other arithmetic  9.19 us (4%)
  waiting for transfers between devices  5.91 us (3%)
    pallas_call x3, Pallas kernels, ring_gather(): pl.pallas_call(functools.partial(_ring_kernel, n, k, pieces), out_shape=o...  120 us
    all_to_all x1, starting transfers between devices, per_device(): lax.all_to_all(jnp.take(both, wanted, axis=0), 'dp', split_axis=0, concat...  10.2 us
    all_to_all x1, starting transfers between devices, per_device(): lax.all_to_all(send_gb, 'dp', split_axis=0, concat_axis=0, tiled=True)  7.5 us
    all_to_all x1, starting transfers between devices, per_device(): lax.all_to_all(send_ga, 'dp', split_axis=0, concat_axis=0, tiled=True)  7.01 us
    all_to_all x1, waiting for transfers between devices, per_device(): lax.all_to_all(send_gb, 'dp', split_axis=0, concat_axis=0, tiled=True)  5.89 us
    dot_general x1, matrix products, per_device(): jnp.dot(tokens, value_weight, preferred_element_type=jnp.float32)  4.4 us
  transfers between devices with their start and end apart: 4, of which 1 were waited for; matrix products, arithmetic and copies ran while one was open for 14% of the time, Pallas kernels for 37%

profile of v12, /device:TPU:24, one launch (start us, length us, event | category | flops | bytes accessed | tf_op | source)
XLA Modules:
  0.0 214.3 jit_solution(369872081282120823)
XLA Ops:
  7.2 1.0 select_reduce_fusion.2
  8.2 0.1 fusion.32
  8.5 0.9 constant_dynamic-slice_fusion.1
  9.5 0.1 reshape.176
  9.6 0.1 copy.57
  9.8 1.1 pad_maximum_fusion
  10.9 2.4 %gather_fusion = bf16[32,576,64]{1,2,0:T(8,128)(2,1)} fusion(bf16[8,576,64]{1,2,0:T(8,128)(2,1)S(1)} %pad_maximum_fusion, s32[1024]{0:T(1024)S(1)} %pad_clamp_fusion.1), kind=kCustom, calls=%fused_computation | custom fusion | bytes 4718720 | tf_op jit(solution)/shard_map/jit(_take)/gather | solution.py:115
  13.3 3.6 %broadcast_select_fusion = bf16[32,576,64]{1,2,0:T(8,128)(2,1)} fusion(bf16[32,576,64]{1,2,0:T(8,128)(2,1)} %gather_fusion, pred[32]{0:T(512)(128)(4,1)S(1)} %compare_and_fusion), kind=kLoop, calls=%fused_computation.4 | loop fusion | flops 1179648 | bytes 4718624 | tf_op jit(solution)/shard_map/jit(_take)/select_n | solution.py:115
  16.9 10.2 %all-to-all-start = ((bf16[32,576,64]{1,2,0:T(8,128)(2,1)}), bf16[32,576,64]{1,2,0:T(8,128)(2,1)}, u32[]{:S(2)}, u32[]{:S(2)}) async-start(bf16[32,576,64]{1,2,0:T(8,128)(2,1)} %broadcast_select_fusion), calls=%async_computation | async-start | bytes 5242880 | tf_op jit(solution)/shard_map/all_to_all | solution.py:115
  27.1 40.7 %shard_map.102 = bf16[16,64,1024]{2,1,0:T(8,128)(2,1)} custom-call(bf16[1,64,1024]{2,1,0:T(8,128)(2,1)} %bitcast.54), custom_call_target="tpu_custom_call" | custom-call | bytes 4194304 | tf_op jit(solution)/shard_map/pallas_call | solution.py:74
  67.9 4.4 %fusion.34 = f32[1024,1024]{1,0:T(8,128)} fusion(bf16[1024,512]{1,0:T(8,128)(2,1)S(1)} %copy-done, bf16[512,1024]{1,0:T(8,128)(2,1)} %param.8), kind=kOutput, calls=%fused_computation.67 | convolution fusion | flops 1073741824 | bytes 6291456 | tf_op jit(solution)/shard_map/dot_general | solution.py:126
  72.3 2.4 %gather_fusion.1 = bf16[8,576,64]{1,2,0:T(8,128)(2,1)S(1)} fusion(bf16[32,576,64]{1,2,0:T(8,128)(2,1)} %all-to-all-done, s32[1024]{0:T(1024)S(1)} %pad_clamp_fusion), kind=kCustom, calls=%fused_computation.1 | custom fusion | bytes 1179680 | tf_op jit(solution)/shard_map/jit(_take)/gather | solution.py:119
  74.8 0.1 broadcast_select_fusion.1
  75.1 0.1 reshape.179
  75.2 0.5 fusion.8
  75.7 0.2 copy.58
  75.9 0.2 reshape.178
  76.1 0.7 maximum_bitcast_fusion.refs_0_
  76.8 42.0 %shard_map.103 = bf16[16,96,1024]{2,1,0:T(8,128)(2,1)} custom-call(bf16[1,96,1024]{2,1,0:T(8,128)(2,1)} %maximum_bitcast_fusion.refs_0_), custom_call_target="tpu_custom_call" | custom-call | bytes 6291456 | tf_op jit(solution)/shard_map/pallas_call | solution.py:74
  118.9 1.1 slice-done
  120.0 0.4 reshape.180
  120.5 1.0 copy-done.4
  121.4 3.0 %convolution_convert_fusion.2 = bf16[8,128,16,4]{1,2,3,0:T(8,128)(2,1)S(1)} fusion(bf16[8,128,1024,1]{2,1,3,0:T(8,128)(2,1)} %bitcast.48, bf16[16,8,4,1024]{3,2,1,0:T(4,128)(2,1)S(1)} %reshape.180), kind=kOutput, calls=%fused_computation.16 | convolution fusion | flops 134283264 | bytes 3276800 | tf_op jit(solution)/shard_map/bnc,jbqc->bnjq/dot_general | solution.py:140
  124.5 0.3 slice_reduce_fusion
  124.9 0.9 reshape.184
  125.8 0.2 copy-done.2
  126.0 1.5 fusion.14
  127.4 0.4 select_reduce_fusion.1
  127.9 1.1 copy.69
  129.0 7.5 %all-to-all-start.2 = ((f32[32,4,1024]{2,1,0:T(4,128)}), f32[32,4,1024]{2,1,0:T(4,128)}, u32[]{:S(2)}, u32[]{:S(2)}) async-start(f32[32,4,1024]{2,1,0:T(4,128)} %copy.69), calls=%async_computation.3 | async-start | bytes 1048576 | tf_op jit(solution)/shard_map/all_to_all | solution.py:160
  136.5 0.3 fusion.6
  136.8 0.8 convolution_convert_fusion
  137.7 2.5 %copy.65 = bf16[32,512,64]{1,2,0:T(8,128)(2,1)} copy(bf16[32,512,64]{1,0,2:T(8,128)(2,1)S(1)} %convolution_convert_fusion) | data formatting | bytes 4194304 | tf_op jit(solution)/shard_map/convert_element_type | solution.py:170
  140.2 5.9 %all-to-all-done.2 = f32[32,4,1024]{2,1,0:T(4,128)} async-done(((f32[32,4,1024]{2,1,0:T(4,128)}), f32[32,4,1024]{2,1,0:T(4,128)}, u32[]{:S(2)}, u32[]{:S(2)}) %all-to-all-start.2) | async-done | bytes 524320 | tf_op jit(solution)/shard_map/all_to_all | solution.py:160
  146.1 7.0 %all-to-all-start.1 = ((bf16[32,512,64]{1,2,0:T(8,128)(2,1)}), bf16[32,512,64]{1,2,0:T(8,128)(2,1)}, u32[]{:S(2)}, u32[]{:S(2)}) async-start(bf16[32,512,64]{1,2,0:T(8,128)(2,1)} %copy.65), calls=%async_computation.2 | async-start | bytes 4194304 | tf_op jit(solution)/shard_map/all_to_all | solution.py:171
  153.2 0.9 reshape_reshape.6
  154.1 1.0 constant_dynamic-slice_fusion
  155.1 1.6 fusion.11
  156.7 2.3 %fusion = bf16[1024,512]{1,0:T(8,128)(2,1)} fusion(f32[8,128,512]{2,1,0:T(8,128)S(1)} %fusion.11, bf16[1024,1024]{1,0:T(8,128)(2,1)S(1)} %bitcast.50, bf16[512,1024]{1,0:T(8,128)(2,1)S(1)} %copy-done.5), kind=kOutput, calls=%fused_computation.6 | convolution fusion | flops 1074790400 | bytes 6291456 | tf_op jit(solution)/shard_map/nc,dc->nd/dot_general | solution.py:179
  159.0 1.5 select_reduce_fusion
  160.5 0.6 convert_element_type.58.refs_0_
  161.2 37.7 %shard_map.104 = bf16[16,32,1024]{2,1,0:T(8,128)(2,1)} custom-call(bf16[1,32,1024]{2,1,0:T(8,128)(2,1)} %convert_element_type.58.refs_0_), custom_call_target="tpu_custom_call" | custom-call | bytes 2097152 | tf_op jit(solution)/shard_map/pallas_call | solution.py:74
  198.9 1.5 reshape.185
  200.4 0.4 copy.71
  200.8 1.1 reshape.186
  201.9 2.8 %fusion.3 = bf16[8,512,64]{1,0,2:T(8,128)(2,1)S(1)} fusion(bf16[32,512,64]{1,2,0:T(8,128)(2,1)} %all-to-all-done.1, s32[32]{0:T(128)S(1)} %fusion.19, pred[32]{0:T(512)(128)(4,1)S(1)} %get-tuple-element.32), kind=kOutput, calls=%fused_computation.12 | convolution fusion | flops 17039872 | bytes 2621600 | tf_op jit(solution)/shard_map/ra,rdk->adk/dot_general | solution.py:172
  204.7 1.0 copy.72
  205.7 1.8 fusion.7
  (32 shorter events, 0.9 us)
Async XLA Ops:
  7.2 60.8 %copy-start = (bf16[1024,512]{1,0:T(8,128)(2,1)S(1)}, bf16[1024,512]{1,0:T(8,128)(2,1)}, u32[]{:S(2)}) copy-start(bf16[1024,512]{1,0:T(8,128)(2,1)} %param.7) | copy-start | bytes 3145732
  16.9 55.4 %all-to-all-start = ((bf16[32,576,64]{1,2,0:T(8,128)(2,1)}), bf16[32,576,64]{1,2,0:T(8,128)(2,1)}, u32[]{:S(2)}, u32[]{:S(2)}) async-start(bf16[32,576,64]{1,2,0:T(8,128)(2,1)} %broadcast_select_fusion), calls=%async_computation | async-start | bytes 5242880 | tf_op jit(solution)/shard_map/all_to_all | solution.py:115
  27.1 178.6 %reduce-scatter.2.cloned.1.call-start = ((), (), s32[]{:S(2)}) async-start(), calls=%async_computation.4 | async-start | bytes 4456448 | tf_op jit(solution)/shard_map/reduce_scatter | solution.py:136
  74.9 43.9 %copy-start.3 = (bf16[8,576,64]{1,2,0:T(8,128)(2,1)}, bf16[8,576,64]{1,2,0:T(8,128)(2,1)S(1)}, u32[]{:S(2)}) copy-start(bf16[8,576,64]{1,2,0:T(8,128)(2,1)S(1)} %broadcast_select_fusion.1) | copy-start | bytes 1769476
  118.8 1.2 slice-start
  120.5 1.0 copy-start.4
  120.5 4.0 %copy-start.1 = (bf16[16,96,1024]{2,1,0:T(8,128)(2,1)S(1)}, bf16[16,96,1024]{2,1,0:T(8,128)(2,1)}, u32[]{:S(2)}) copy-start(bf16[16,96,1024]{2,1,0:T(8,128)(2,1)} %shard_map.103) | copy-start | bytes 9437188
  124.4 1.6 copy-start.2
  129.0 17.0 %all-to-all-start.2 = ((f32[32,4,1024]{2,1,0:T(4,128)}), f32[32,4,1024]{2,1,0:T(4,128)}, u32[]{:S(2)}, u32[]{:S(2)}) async-start(f32[32,4,1024]{2,1,0:T(4,128)} %copy.69), calls=%async_computation.3 | async-start | bytes 1048576 | tf_op jit(solution)/shard_map/all_to_all | solution.py:160
  146.1 55.8 %all-to-all-start.1 = ((bf16[32,512,64]{1,2,0:T(8,128)(2,1)}), bf16[32,512,64]{1,2,0:T(8,128)(2,1)}, u32[]{:S(2)}, u32[]{:S(2)}) async-start(bf16[32,512,64]{1,2,0:T(8,128)(2,1)} %copy.65), calls=%async_computation.2 | async-start | bytes 4194304 | tf_op jit(solution)/shard_map/all_to_all | solution.py:171
  155.1 1.6 copy-start.5
Sparse Core Ops, SparseCore 0:
  118.9 80.7 reduce-scatter.1

commit v13 on v11

--- a/solution.py
+++ b/solution.py
@@ -131,7 +131,7 @@
     packed = jnp.concatenate(
         [down_part.reshape(down_rows, kv_full), panel_b_cols.reshape(-1, kv_full)], axis=0
     )
-    (parts,) = ring_gather([packed[None]], n_split, 1, pieces=3)
+    (parts,) = ring_gather([packed[None]], n_split, 1, pieces=6)
     partial_value, parts = lax.optimization_barrier((partial_value, parts))
     base = lax.psum_scatter(partial_value, "mp", scatter_dimension=0, tiled=True)
     down = jnp.sum(parts[:, :down_rows].astype(jnp.float32), axis=0)

time: 214 us -> 215 us (level)
  no operation moved by 1% of the time
where the time goes in v13:
time: 215 us; the launch traced here: 214 us
  Pallas kernels  121 us (56%)
  starting transfers between devices  24.5 us (11%)
  local copies, waits for them, and re-layouts  20.8 us (10%)
  matrix products  19.8 us (9%)
  between operations  14.4 us (7%)
  other arithmetic  7.19 us (3%)
  waiting for transfers between devices  5.89 us (3%)
    pallas_call x3, Pallas kernels, ring_gather(): pl.pallas_call(functools.partial(_ring_kernel, n, k, pieces), out_shape=o...  121 us
    all_to_all x1, starting transfers between devices, per_device(): lax.all_to_all(jnp.take(both, wanted, axis=0), 'dp', split_axis=0, concat...  10.1 us
    all_to_all x1, starting transfers between devices, per_device(): lax.all_to_all(send_gb, 'dp', split_axis=0, concat_axis=0, tiled=True)  7.37 us
    all_to_all x1, starting transfers between devices, per_device(): lax.all_to_all(send_ga, 'dp', split_axis=0, concat_axis=0, tiled=True)  6.99 us
    all_to_all x1, waiting for transfers between devices, per_device(): lax.all_to_all(send_gb, 'dp', split_axis=0, concat_axis=0, tiled=True)  5.87 us
  transfers between devices with their start and end apart: 4, of which 1 were waited for; matrix products, arithmetic and copies ran while one was open for 14% of the time, Pallas kernels for 37%

profile of v13, /device:TPU:24, one launch (start us, length us, event | category | flops | bytes accessed | tf_op | source)
XLA Modules:
  0.0 213.7 jit_solution(14042180842524998642)
XLA Ops:
  7.2 1.0 select_reduce_fusion
  8.2 0.1 fusion.44
  8.5 0.9 constant_dynamic-slice_fusion.1
  9.5 0.1 reshape.109
  9.6 0.1 copy.43
  9.8 1.1 pad_maximum_fusion
  10.9 2.4 %gather_fusion = bf16[32,576,64]{1,2,0:T(8,128)(2,1)} fusion(bf16[8,576,64]{1,2,0:T(8,128)(2,1)S(1)} %pad_maximum_fusion, s32[1024]{0:T(1024)S(1)} %pad_clamp_fusion.1), kind=kCustom, calls=%fused_computation | custom fusion | bytes 4718720 | tf_op jit(solution)/shard_map/jit(_take)/gather | solution.py:115
  13.3 3.6 %broadcast_select_fusion = bf16[32,576,64]{1,2,0:T(8,128)(2,1)} fusion(bf16[32,576,64]{1,2,0:T(8,128)(2,1)} %gather_fusion, pred[32]{0:T(512)(128)(4,1)S(1)} %compare_and_fusion), kind=kLoop, calls=%fused_computation.2 | loop fusion | flops 1179648 | bytes 4718624 | tf_op jit(solution)/shard_map/jit(_take)/select_n | solution.py:115
  16.9 10.1 %all-to-all-start = ((bf16[32,576,64]{1,2,0:T(8,128)(2,1)}), bf16[32,576,64]{1,2,0:T(8,128)(2,1)}, u32[]{:S(2)}, u32[]{:S(2)}) async-start(bf16[32,576,64]{1,2,0:T(8,128)(2,1)} %broadcast_select_fusion), calls=%async_computation | async-start | bytes 5242880 | tf_op jit(solution)/shard_map/all_to_all | solution.py:115
  27.1 40.9 %shard_map.102 = bf16[16,64,1024]{2,1,0:T(8,128)(2,1)} custom-call(bf16[1,64,1024]{2,1,0:T(8,128)(2,1)} %bitcast.56), custom_call_target="tpu_custom_call" | custom-call | bytes 4194304 | tf_op jit(solution)/shard_map/pallas_call | solution.py:74
  68.1 3.2 %fusion.46 = f32[1024,1024]{1,0:T(8,128)} fusion(bf16[1024,512]{1,0:T(8,128)(2,1)S(1)} %copy-done, bf16[512,1024]{1,0:T(8,128)(2,1)S(1)} %copy-done.5), kind=kOutput, calls=%fused_computation.75 | convolution fusion | flops 1073741824 | bytes 6291456 | tf_op jit(solution)/shard_map/dot_general | solution.py:126
  71.2 2.4 %gather_fusion.1 = bf16[8,576,64]{1,2,0:T(8,128)(2,1)S(1)} fusion(bf16[32,576,64]{1,2,0:T(8,128)(2,1)} %all-to-all-done, s32[1024]{0:T(1024)S(1)} %pad_clamp_fusion), kind=kCustom, calls=%fused_computation.1 | custom fusion | bytes 1179680 | tf_op jit(solution)/shard_map/jit(_take)/gather | solution.py:119
  73.7 0.1 broadcast_select_fusion.1
  74.0 0.1 reshape.112
  74.1 0.5 fusion.8
  74.6 0.2 copy.44
  74.8 0.2 reshape.111
  75.0 0.7 maximum_bitcast_fusion.refs_0_
  75.7 41.9 %shard_map.103 = bf16[16,96,1024]{2,1,0:T(8,128)(2,1)} custom-call(bf16[1,96,1024]{2,1,0:T(8,128)(2,1)} %maximum_bitcast_fusion.refs_0_), custom_call_target="tpu_custom_call" | custom-call | bytes 6291456 | tf_op jit(solution)/shard_map/pallas_call | solution.py:74
  117.7 1.2 slice-done
  118.9 0.4 reshape.113
  119.3 1.0 copy-done.4
  120.3 3.0 %convolution_convert_fusion.2 = bf16[8,128,16,4]{1,2,3,0:T(8,128)(2,1)S(1)} fusion(bf16[8,128,1024,1]{2,1,3,0:T(8,128)(2,1)} %bitcast.50, bf16[16,8,4,1024]{3,2,1,0:T(4,128)(2,1)S(1)} %reshape.113), kind=kOutput, calls=%fused_computation.14 | convolution fusion | flops 134283264 | bytes 3276800 | tf_op jit(solution)/shard_map/bnc,jbqc->bnjq/dot_general | solution.py:140
  123.4 0.3 slice_reduce_fusion
  123.7 0.9 reshape.117
  124.6 0.2 copy-done.2
  124.8 1.5 fusion.15
  126.3 0.5 fusion.17
  126.8 1.1 copy.55
  127.9 7.4 %all-to-all-start.2 = ((f32[32,4,1024]{2,1,0:T(4,128)}), f32[32,4,1024]{2,1,0:T(4,128)}, u32[]{:S(2)}, u32[]{:S(2)}) async-start(f32[32,4,1024]{2,1,0:T(4,128)} %copy.55), calls=%async_computation.3 | async-start | bytes 1048576 | tf_op jit(solution)/shard_map/all_to_all | solution.py:161
  135.3 0.3 fusion.6
  135.6 0.8 convolution_convert_fusion
  136.4 2.5 %copy.51 = bf16[32,512,64]{1,2,0:T(8,128)(2,1)} copy(bf16[32,512,64]{1,0,2:T(8,128)(2,1)S(1)} %convolution_convert_fusion) | data formatting | bytes 4194304 | tf_op jit(solution)/shard_map/convert_element_type | solution.py:171
  139.0 5.9 %all-to-all-done.2 = f32[32,4,1024]{2,1,0:T(4,128)} async-done(((f32[32,4,1024]{2,1,0:T(4,128)}), f32[32,4,1024]{2,1,0:T(4,128)}, u32[]{:S(2)}, u32[]{:S(2)}) %all-to-all-start.2) | async-done | bytes 524320 | tf_op jit(solution)/shard_map/all_to_all | solution.py:161
  144.8 7.0 %all-to-all-start.1 = ((bf16[32,512,64]{1,2,0:T(8,128)(2,1)}), bf16[32,512,64]{1,2,0:T(8,128)(2,1)}, u32[]{:S(2)}, u32[]{:S(2)}) async-start(bf16[32,512,64]{1,2,0:T(8,128)(2,1)} %copy.51), calls=%async_computation.2 | async-start | bytes 4194304 | tf_op jit(solution)/shard_map/all_to_all | solution.py:172
  151.8 0.9 reshape_reshape.6
  152.7 0.9 constant_dynamic-slice_fusion
  153.7 1.6 fusion.12
  155.4 2.3 %fusion = bf16[1024,512]{1,0:T(8,128)(2,1)} fusion(f32[8,128,512]{2,1,0:T(8,128)S(1)} %fusion.12, bf16[1024,1024]{1,0:T(8,128)(2,1)S(1)} %bitcast.52, bf16[512,1024]{1,0:T(8,128)(2,1)S(1)} %copy-done.6), kind=kOutput, calls=%fused_computation.4 | convolution fusion | flops 1074790400 | bytes 6291456 | tf_op jit(solution)/shard_map/nc,dc->nd/dot_general | solution.py:180
  157.6 1.6 convolution_convert_fusion.4
  159.3 0.6 reshape.118.refs_0_
  160.0 38.3 %shard_map.104 = bf16[16,32,1024]{2,1,0:T(8,128)(2,1)} custom-call(bf16[1,32,1024]{2,1,0:T(8,128)(2,1)} %reshape.118.refs_0_), custom_call_target="tpu_custom_call" | custom-call | bytes 2097152 | tf_op jit(solution)/shard_map/pallas_call | solution.py:74
  198.3 1.5 reshape.119
  199.8 0.4 copy.58
  200.2 1.1 reshape.120
  201.3 2.8 %fusion.3 = bf16[8,512,64]{1,0,2:T(8,128)(2,1)S(1)} fusion(bf16[32,512,64]{1,2,0:T(8,128)(2,1)} %all-to-all-done.1, s32[32]{0:T(128)S(1)} %fusion.22, pred[32]{0:T(512)(128)(4,1)S(1)} %get-tuple-element.28), kind=kOutput, calls=%fused_computation.10 | convolution fusion | flops 17039872 | bytes 2621600 | tf_op jit(solution)/shard_map/ra,rdk->adk/dot_general | solution.py:173
  204.1 1.0 copy.59
  205.1 1.8 fusion.7
  (31 shorter events, 0.7 us)
Async XLA Ops:
  7.2 60.9 %copy-start = (bf16[1024,512]{1,0:T(8,128)(2,1)S(1)}, bf16[1024,512]{1,0:T(8,128)(2,1)}, u32[]{:S(2)}) copy-start(bf16[1024,512]{1,0:T(8,128)(2,1)} %param.7) | copy-start | bytes 3145732
  16.9 54.3 %all-to-all-start = ((bf16[32,576,64]{1,2,0:T(8,128)(2,1)}), bf16[32,576,64]{1,2,0:T(8,128)(2,1)}, u32[]{:S(2)}, u32[]{:S(2)}) async-start(bf16[32,576,64]{1,2,0:T(8,128)(2,1)} %broadcast_select_fusion), calls=%async_computation | async-start | bytes 5242880 | tf_op jit(solution)/shard_map/all_to_all | solution.py:115
  27.0 41.0 %copy-start.5 = (bf16[512,1024]{1,0:T(8,128)(2,1)S(1)}, bf16[512,1024]{1,0:T(8,128)(2,1)}, u32[]{:S(2)}) copy-start(bf16[512,1024]{1,0:T(8,128)(2,1)} %param.8) | copy-start | bytes 3145732
  27.1 178.0 %reduce-scatter.2.cloned.1.call-start = ((), (), s32[]{:S(2)}) async-start(), calls=%async_computation.4 | async-start | bytes 4456448 | tf_op jit(solution)/shard_map/reduce_scatter | solution.py:136
  73.8 43.8 %copy-start.3 = (bf16[8,576,64]{1,2,0:T(8,128)(2,1)}, bf16[8,576,64]{1,2,0:T(8,128)(2,1)S(1)}, u32[]{:S(2)}) copy-start(bf16[8,576,64]{1,2,0:T(8,128)(2,1)S(1)} %broadcast_select_fusion.1) | copy-start | bytes 1769476
  117.7 1.2 slice-start
  119.3 1.0 copy-start.4
  119.3 4.0 %copy-start.1 = (bf16[16,96,1024]{2,1,0:T(8,128)(2,1)S(1)}, bf16[16,96,1024]{2,1,0:T(8,128)(2,1)}, u32[]{:S(2)}) copy-start(bf16[16,96,1024]{2,1,0:T(8,128)(2,1)} %shard_map.103) | copy-start | bytes 9437188
  123.2 1.6 copy-start.2
  127.9 16.9 %all-to-all-start.2 = ((f32[32,4,1024]{2,1,0:T(4,128)}), f32[32,4,1024]{2,1,0:T(4,128)}, u32[]{:S(2)}, u32[]{:S(2)}) async-start(f32[32,4,1024]{2,1,0:T(4,128)} %copy.55), calls=%async_computation.3 | async-start | bytes 1048576 | tf_op jit(solution)/shard_map/all_to_all | solution.py:161
  144.8 56.5 %all-to-all-start.1 = ((bf16[32,512,64]{1,2,0:T(8,128)(2,1)}), bf16[32,512,64]{1,2,0:T(8,128)(2,1)}, u32[]{:S(2)}, u32[]{:S(2)}) async-start(bf16[32,512,64]{1,2,0:T(8,128)(2,1)} %copy.51), calls=%async_computation.2 | async-start | bytes 4194304 | tf_op jit(solution)/shard_map/all_to_all | solution.py:172
  153.7 1.6 copy-start.6
Sparse Core Ops, SparseCore 0:
  117.8 82.1 reduce-scatter.1

commit v14 on v11

--- a/solution.py
+++ b/solution.py
@@ -24,18 +24,20 @@
             barrier, inc=1, device_id=(row, peer), device_id_type=pl.DeviceIdType.MESH
         )
     pl.semaphore_wait(barrier, 2)
+    locals_ = []
     for a in range(k):
         local = pltpu.make_async_copy(ins[a].at[0], outs[a].at[me], local_sem.at[a])
         local.start()
-        local.wait()
+        locals_.append(local)
     reach = (n // 2, n - 1 - n // 2)
     streams = ((0, right, -1), (1, left, 1))
 
     def link(a, way, step, slot, peer, i):
         size = outs[a].shape[1] // pieces
         part = outs[a].at[slot, pl.ds(i * size, size)]
+        own = ins[a].at[0, pl.ds(i * size, size)]
         return pltpu.make_async_remote_copy(
-            src_ref=part,
+            src_ref=own if step == 1 else part,
             dst_ref=part,
             send_sem=send_sems.at[a, way, step, i],
             recv_sem=recv_sems.at[a, way, step, i],
@@ -64,6 +66,8 @@
                 link(a, way, last, slot, peer, i).wait_recv()
     for copy in started:
         copy.wait_send()
+    for local in locals_:
+        local.wait()
 
 
 def ring_gather(arrays, n, tag, pieces=4):

time: 214 us -> 215 us (level)
  no operation moved by 1% of the time
where the time goes in v14:
time: 215 us; the launch traced here: 213 us
  Pallas kernels  121 us (56%)
  starting transfers between devices  24.5 us (11%)
  local copies, waits for them, and re-layouts  20.8 us (10%)
  matrix products  19.8 us (9%)
  between operations  14.4 us (7%)
  other arithmetic  7.19 us (3%)
  waiting for transfers between devices  5.89 us (3%)
    pallas_call x3, Pallas kernels, ring_gather(): pl.pallas_call(functools.partial(_ring_kernel, n, k, pieces), out_shape=o...  121 us
    all_to_all x1, starting transfers between devices, per_device(): lax.all_to_all(jnp.take(both, wanted, axis=0), 'dp', split_axis=0, concat...  10.1 us
    all_to_all x1, starting transfers between devices, per_device(): lax.all_to_all(send_gb, 'dp', split_axis=0, concat_axis=0, tiled=True)  7.36 us
    all_to_all x1, starting transfers between devices, per_device(): lax.all_to_all(send_ga, 'dp', split_axis=0, concat_axis=0, tiled=True)  6.99 us
    all_to_all x1, waiting for transfers between devices, per_device(): lax.all_to_all(send_gb, 'dp', split_axis=0, concat_axis=0, tiled=True)  5.87 us
  transfers between devices with their start and end apart: 4, of which 1 were waited for; matrix products, arithmetic and copies ran while one was open for 14% of the time, Pallas kernels for 37%

profile of v14, /device:TPU:24, one launch (start us, length us, event | category | flops | bytes accessed | tf_op | source)
XLA Modules:
  0.0 213.1 jit_solution(15544036082562416441)
XLA Ops:
  7.2 1.0 select_reduce_fusion
  8.2 0.1 fusion.44
  8.5 0.9 constant_dynamic-slice_fusion.1
  9.5 0.1 reshape.109
  9.6 0.1 copy.43
  9.8 1.1 pad_maximum_fusion
  10.9 2.4 %gather_fusion = bf16[32,576,64]{1,2,0:T(8,128)(2,1)} fusion(bf16[8,576,64]{1,2,0:T(8,128)(2,1)S(1)} %pad_maximum_fusion, s32[1024]{0:T(1024)S(1)} %pad_clamp_fusion.1), kind=kCustom, calls=%fused_computation | custom fusion | bytes 4718720 | tf_op jit(solution)/shard_map/jit(_take)/gather | solution.py:119
  13.3 3.6 %broadcast_select_fusion = bf16[32,576,64]{1,2,0:T(8,128)(2,1)} fusion(bf16[32,576,64]{1,2,0:T(8,128)(2,1)} %gather_fusion, pred[32]{0:T(512)(128)(4,1)S(1)} %compare_and_fusion), kind=kLoop, calls=%fused_computation.2 | loop fusion | flops 1179648 | bytes 4718624 | tf_op jit(solution)/shard_map/jit(_take)/select_n | solution.py:119
  16.9 10.1 %all-to-all-start = ((bf16[32,576,64]{1,2,0:T(8,128)(2,1)}), bf16[32,576,64]{1,2,0:T(8,128)(2,1)}, u32[]{:S(2)}, u32[]{:S(2)}) async-start(bf16[32,576,64]{1,2,0:T(8,128)(2,1)} %broadcast_select_fusion), calls=%async_computation | async-start | bytes 5242880 | tf_op jit(solution)/shard_map/all_to_all | solution.py:119
  27.1 40.9 %shard_map.102 = bf16[16,64,1024]{2,1,0:T(8,128)(2,1)} custom-call(bf16[1,64,1024]{2,1,0:T(8,128)(2,1)} %bitcast.56), custom_call_target="tpu_custom_call" | custom-call | bytes 4194304 | tf_op jit(solution)/shard_map/pallas_call | solution.py:78
  68.1 3.2 %fusion.46 = f32[1024,1024]{1,0:T(8,128)} fusion(bf16[1024,512]{1,0:T(8,128)(2,1)S(1)} %copy-done, bf16[512,1024]{1,0:T(8,128)(2,1)S(1)} %copy-done.5), kind=kOutput, calls=%fused_computation.75 | convolution fusion | flops 1073741824 | bytes 6291456 | tf_op jit(solution)/shard_map/dot_general | solution.py:130
  71.2 2.4 %gather_fusion.1 = bf16[8,576,64]{1,2,0:T(8,128)(2,1)S(1)} fusion(bf16[32,576,64]{1,2,0:T(8,128)(2,1)} %all-to-all-done, s32[1024]{0:T(1024)S(1)} %pad_clamp_fusion), kind=kCustom, calls=%fused_computation.1 | custom fusion | bytes 1179680 | tf_op jit(solution)/shard_map/jit(_take)/gather | solution.py:123
  73.7 0.1 broadcast_select_fusion.1
  74.0 0.1 reshape.112
  74.1 0.5 fusion.8
  74.6 0.2 copy.44
  74.8 0.2 reshape.111
  75.0 0.7 maximum_bitcast_fusion.refs_0_
  75.7 42.0 %shard_map.103 = bf16[16,96,1024]{2,1,0:T(8,128)(2,1)} custom-call(bf16[1,96,1024]{2,1,0:T(8,128)(2,1)} %maximum_bitcast_fusion.refs_0_), custom_call_target="tpu_custom_call" | custom-call | bytes 6291456 | tf_op jit(solution)/shard_map/pallas_call | solution.py:78
  117.7 1.2 slice-done
  118.9 0.4 reshape.113
  119.4 1.0 copy-done.4
  120.3 3.0 %convolution_convert_fusion.2 = bf16[8,128,16,4]{1,2,3,0:T(8,128)(2,1)S(1)} fusion(bf16[8,128,1024,1]{2,1,3,0:T(8,128)(2,1)} %bitcast.50, bf16[16,8,4,1024]{3,2,1,0:T(4,128)(2,1)S(1)} %reshape.113), kind=kOutput, calls=%fused_computation.14 | convolution fusion | flops 134283264 | bytes 3276800 | tf_op jit(solution)/shard_map/bnc,jbqc->bnjq/dot_general | solution.py:144
  123.4 0.3 slice_reduce_fusion
  123.8 0.9 reshape.117
  124.7 0.2 copy-done.2
  124.9 1.5 fusion.15
  126.3 0.5 fusion.17
  126.8 1.1 copy.55
  128.0 7.4 %all-to-all-start.2 = ((f32[32,4,1024]{2,1,0:T(4,128)}), f32[32,4,1024]{2,1,0:T(4,128)}, u32[]{:S(2)}, u32[]{:S(2)}) async-start(f32[32,4,1024]{2,1,0:T(4,128)} %copy.55), calls=%async_computation.3 | async-start | bytes 1048576 | tf_op jit(solution)/shard_map/all_to_all | solution.py:165
  135.3 0.3 fusion.6
  135.6 0.8 convolution_convert_fusion
  136.5 2.5 %copy.51 = bf16[32,512,64]{1,2,0:T(8,128)(2,1)} copy(bf16[32,512,64]{1,0,2:T(8,128)(2,1)S(1)} %convolution_convert_fusion) | data formatting | bytes 4194304 | tf_op jit(solution)/shard_map/convert_element_type | solution.py:175
  139.0 5.9 %all-to-all-done.2 = f32[32,4,1024]{2,1,0:T(4,128)} async-done(((f32[32,4,1024]{2,1,0:T(4,128)}), f32[32,4,1024]{2,1,0:T(4,128)}, u32[]{:S(2)}, u32[]{:S(2)}) %all-to-all-start.2) | async-done | bytes 524320 | tf_op jit(solution)/shard_map/all_to_all | solution.py:165
  144.9 7.0 %all-to-all-start.1 = ((bf16[32,512,64]{1,2,0:T(8,128)(2,1)}), bf16[32,512,64]{1,2,0:T(8,128)(2,1)}, u32[]{:S(2)}, u32[]{:S(2)}) async-start(bf16[32,512,64]{1,2,0:T(8,128)(2,1)} %copy.51), calls=%async_computation.2 | async-start | bytes 4194304 | tf_op jit(solution)/shard_map/all_to_all | solution.py:176
  151.9 0.9 reshape_reshape.6
  152.8 1.0 constant_dynamic-slice_fusion
  153.8 1.6 fusion.12
  155.4 2.3 %fusion = bf16[1024,512]{1,0:T(8,128)(2,1)} fusion(f32[8,128,512]{2,1,0:T(8,128)S(1)} %fusion.12, bf16[1024,1024]{1,0:T(8,128)(2,1)S(1)} %bitcast.52, bf16[512,1024]{1,0:T(8,128)(2,1)S(1)} %copy-done.6), kind=kOutput, calls=%fused_computation.4 | convolution fusion | flops 1074790400 | bytes 6291456 | tf_op jit(solution)/shard_map/nc,dc->nd/dot_general | solution.py:184
  157.7 1.6 convolution_convert_fusion.4
  159.3 0.6 reshape.118.refs_0_
  160.0 37.7 %shard_map.104 = bf16[16,32,1024]{2,1,0:T(8,128)(2,1)} custom-call(bf16[1,32,1024]{2,1,0:T(8,128)(2,1)} %reshape.118.refs_0_), custom_call_target="tpu_custom_call" | custom-call | bytes 2097152 | tf_op jit(solution)/shard_map/pallas_call | solution.py:78
  197.7 1.5 reshape.119
  199.2 0.4 copy.58
  199.6 1.1 reshape.120
  200.7 2.8 %fusion.3 = bf16[8,512,64]{1,0,2:T(8,128)(2,1)S(1)} fusion(bf16[32,512,64]{1,2,0:T(8,128)(2,1)} %all-to-all-done.1, s32[32]{0:T(128)S(1)} %fusion.22, pred[32]{0:T(512)(128)(4,1)S(1)} %get-tuple-element.28), kind=kOutput, calls=%fused_computation.10 | convolution fusion | flops 17039872 | bytes 2621600 | tf_op jit(solution)/shard_map/ra,rdk->adk/dot_general | solution.py:177
  203.5 1.0 copy.59
  204.5 1.8 fusion.7
  (31 shorter events, 0.7 us)
Async XLA Ops:
  7.2 60.9 %copy-start = (bf16[1024,512]{1,0:T(8,128)(2,1)S(1)}, bf16[1024,512]{1,0:T(8,128)(2,1)}, u32[]{:S(2)}) copy-start(bf16[1024,512]{1,0:T(8,128)(2,1)} %param.7) | copy-start | bytes 3145732
  16.9 54.3 %all-to-all-start = ((bf16[32,576,64]{1,2,0:T(8,128)(2,1)}), bf16[32,576,64]{1,2,0:T(8,128)(2,1)}, u32[]{:S(2)}, u32[]{:S(2)}) async-start(bf16[32,576,64]{1,2,0:T(8,128)(2,1)} %broadcast_select_fusion), calls=%async_computation | async-start | bytes 5242880 | tf_op jit(solution)/shard_map/all_to_all | solution.py:119
  27.0 41.0 %copy-start.5 = (bf16[512,1024]{1,0:T(8,128)(2,1)S(1)}, bf16[512,1024]{1,0:T(8,128)(2,1)}, u32[]{:S(2)}) copy-start(bf16[512,1024]{1,0:T(8,128)(2,1)} %param.8) | copy-start | bytes 3145732
  27.1 177.4 %reduce-scatter.2.cloned.1.call-start = ((), (), s32[]{:S(2)}) async-start(), calls=%async_computation.4 | async-start | bytes 4456448 | tf_op jit(solution)/shard_map/reduce_scatter | solution.py:140
  73.8 43.9 %copy-start.3 = (bf16[8,576,64]{1,2,0:T(8,128)(2,1)}, bf16[8,576,64]{1,2,0:T(8,128)(2,1)S(1)}, u32[]{:S(2)}) copy-start(bf16[8,576,64]{1,2,0:T(8,128)(2,1)S(1)} %broadcast_select_fusion.1) | copy-start | bytes 1769476
  117.7 1.2 slice-start
  119.4 1.0 copy-start.4
  119.4 4.0 %copy-start.1 = (bf16[16,96,1024]{2,1,0:T(8,128)(2,1)S(1)}, bf16[16,96,1024]{2,1,0:T(8,128)(2,1)}, u32[]{:S(2)}) copy-start(bf16[16,96,1024]{2,1,0:T(8,128)(2,1)} %shard_map.103) | copy-start | bytes 9437188
  123.3 1.6 copy-start.2
  128.0 16.9 %all-to-all-start.2 = ((f32[32,4,1024]{2,1,0:T(4,128)}), f32[32,4,1024]{2,1,0:T(4,128)}, u32[]{:S(2)}, u32[]{:S(2)}) async-start(f32[32,4,1024]{2,1,0:T(4,128)} %copy.55), calls=%async_computation.3 | async-start | bytes 1048576 | tf_op jit(solution)/shard_map/all_to_all | solution.py:165
  144.9 55.8 %all-to-all-start.1 = ((bf16[32,512,64]{1,2,0:T(8,128)(2,1)}), bf16[32,512,64]{1,2,0:T(8,128)(2,1)}, u32[]{:S(2)}, u32[]{:S(2)}) async-start(bf16[32,512,64]{1,2,0:T(8,128)(2,1)} %copy.51), calls=%async_computation.2 | async-start | bytes 4194304 | tf_op jit(solution)/shard_map/all_to_all | solution.py:176
  153.8 1.6 copy-start.6
Sparse Core Ops, SparseCore 0:
  117.8 80.8 reduce-scatter.1

commit v15 on v11

--- a/solution.py
+++ b/solution.py
@@ -114,7 +114,7 @@
     both = jnp.concatenate([down_panels, up_rows_mine.reshape(stored, -1, RANK)], axis=1)
     got = lax.all_to_all(jnp.take(both, wanted, axis=0), "dp", split_axis=0, concat_axis=0, tiled=True)
 
-    (cot_all,) = ring_gather([cotangent[None]], n_split, 0)
+    (cot_all,) = ring_gather([cotangent[None]], n_split, 0, pieces=2)
     got, cot_all = lax.optimization_barrier((got, cot_all))
     mine_got = jnp.take(got, my_owner, axis=0)
     panel_a = mine_got[:, :width_dev]
@@ -173,7 +173,7 @@
     grad_down = jnp.einsum(
         "ra,rdk->adk", pick_bf, recv_ga, preferred_element_type=jnp.float32
     ).astype(jnp.bfloat16)
-    (shares,) = ring_gather([grad_share.reshape(1, -1, kv_full)], n_split, 2, pieces=2)
+    (shares,) = ring_gather([grad_share.reshape(1, -1, kv_full)], n_split, 2, pieces=1)
     shares = shares.reshape(n_split, stored, share, kv_full)
     grad_up = shares.transpose(1, 0, 2, 3).reshape(stored, RANK, kv_full)
 

time: 214 us -> 218 us (1.019)
  no operation moved by 1% of the time
where the time goes in v15:
time: 218 us; the launch traced here: 215 us
  Pallas kernels  122 us (56%)
  starting transfers between devices  24.6 us (11%)
  local copies, waits for them, and re-layouts  20.8 us (10%)
  matrix products  19.8 us (9%)
  between operations  14.4 us (7%)
  other arithmetic  7.19 us (3%)
  waiting for transfers between devices  5.89 us (3%)
    pallas_call x3, Pallas kernels, ring_gather(): pl.pallas_call(functools.partial(_ring_kernel, n, k, pieces), out_shape=o...  122 us
    all_to_all x1, starting transfers between devices, per_device(): lax.all_to_all(jnp.take(both, wanted, axis=0), 'dp', split_axis=0, concat...  10.1 us
    all_to_all x1, starting transfers between devices, per_device(): lax.all_to_all(send_gb, 'dp', split_axis=0, concat_axis=0, tiled=True)  7.39 us
    all_to_all x1, starting transfers between devices, per_device(): lax.all_to_all(send_ga, 'dp', split_axis=0, concat_axis=0, tiled=True)  6.99 us
    all_to_all x1, waiting for transfers between devices, per_device(): lax.all_to_all(send_gb, 'dp', split_axis=0, concat_axis=0, tiled=True)  5.87 us
  transfers between devices with their start and end apart: 4, of which 1 were waited for; matrix products, arithmetic and copies ran while one was open for 14% of the time, Pallas kernels for 37%

profile of v15, /device:TPU:24, one launch (start us, length us, event | category | flops | bytes accessed | tf_op | source)
XLA Modules:
  0.0 215.0 jit_solution(4367937418781606140)
XLA Ops:
  7.2 1.0 select_reduce_fusion
  8.2 0.1 fusion.44
  8.5 0.9 constant_dynamic-slice_fusion.1
  9.5 0.1 reshape.109
  9.6 0.1 copy.43
  9.8 1.1 pad_maximum_fusion
  10.9 2.4 %gather_fusion = bf16[32,576,64]{1,2,0:T(8,128)(2,1)} fusion(bf16[8,576,64]{1,2,0:T(8,128)(2,1)S(1)} %pad_maximum_fusion, s32[1024]{0:T(1024)S(1)} %pad_clamp_fusion.1), kind=kCustom, calls=%fused_computation | custom fusion | bytes 4718720 | tf_op jit(solution)/shard_map/jit(_take)/gather | solution.py:115
  13.3 3.6 %broadcast_select_fusion = bf16[32,576,64]{1,2,0:T(8,128)(2,1)} fusion(bf16[32,576,64]{1,2,0:T(8,128)(2,1)} %gather_fusion, pred[32]{0:T(512)(128)(4,1)S(1)} %compare_and_fusion), kind=kLoop, calls=%fused_computation.2 | loop fusion | flops 1179648 | bytes 4718624 | tf_op jit(solution)/shard_map/jit(_take)/select_n | solution.py:115
  16.9 10.1 %all-to-all-start = ((bf16[32,576,64]{1,2,0:T(8,128)(2,1)}), bf16[32,576,64]{1,2,0:T(8,128)(2,1)}, u32[]{:S(2)}, u32[]{:S(2)}) async-start(bf16[32,576,64]{1,2,0:T(8,128)(2,1)} %broadcast_select_fusion), calls=%async_computation | async-start | bytes 5242880 | tf_op jit(solution)/shard_map/all_to_all | solution.py:115
  27.1 41.9 %shard_map.102 = bf16[16,64,1024]{2,1,0:T(8,128)(2,1)} custom-call(bf16[1,64,1024]{2,1,0:T(8,128)(2,1)} %bitcast.56), custom_call_target="tpu_custom_call" | custom-call | bytes 4194304 | tf_op jit(solution)/shard_map/pallas_call | solution.py:74
  69.1 3.2 %fusion.46 = f32[1024,1024]{1,0:T(8,128)} fusion(bf16[1024,512]{1,0:T(8,128)(2,1)S(1)} %copy-done, bf16[512,1024]{1,0:T(8,128)(2,1)S(1)} %copy-done.5), kind=kOutput, calls=%fused_computation.75 | convolution fusion | flops 1073741824 | bytes 6291456 | tf_op jit(solution)/shard_map/dot_general | solution.py:126
  72.3 2.4 %gather_fusion.1 = bf16[8,576,64]{1,2,0:T(8,128)(2,1)S(1)} fusion(bf16[32,576,64]{1,2,0:T(8,128)(2,1)} %all-to-all-done, s32[1024]{0:T(1024)S(1)} %pad_clamp_fusion), kind=kCustom, calls=%fused_computation.1 | custom fusion | bytes 1179680 | tf_op jit(solution)/shard_map/jit(_take)/gather | solution.py:119
  74.7 0.1 broadcast_select_fusion.1
  75.0 0.1 reshape.112
  75.2 0.5 fusion.8
  75.6 0.2 copy.44
  75.8 0.2 reshape.111
  76.0 0.7 maximum_bitcast_fusion.refs_0_
  76.7 41.9 %shard_map.103 = bf16[16,96,1024]{2,1,0:T(8,128)(2,1)} custom-call(bf16[1,96,1024]{2,1,0:T(8,128)(2,1)} %maximum_bitcast_fusion.refs_0_), custom_call_target="tpu_custom_call" | custom-call | bytes 6291456 | tf_op jit(solution)/shard_map/pallas_call | solution.py:74
  118.7 1.2 slice-done
  119.9 0.4 reshape.113
  120.4 1.0 copy-done.4
  121.3 3.0 %convolution_convert_fusion.2 = bf16[8,128,16,4]{1,2,3,0:T(8,128)(2,1)S(1)} fusion(bf16[8,128,1024,1]{2,1,3,0:T(8,128)(2,1)} %bitcast.50, bf16[16,8,4,1024]{3,2,1,0:T(4,128)(2,1)S(1)} %reshape.113), kind=kOutput, calls=%fused_computation.14 | convolution fusion | flops 134283264 | bytes 3276800 | tf_op jit(solution)/shard_map/bnc,jbqc->bnjq/dot_general | solution.py:140
  124.4 0.3 slice_reduce_fusion
  124.7 0.9 reshape.117
  125.6 0.2 copy-done.2
  125.9 1.5 fusion.15
  127.3 0.5 fusion.17
  127.8 1.1 copy.55
  129.0 7.4 %all-to-all-start.2 = ((f32[32,4,1024]{2,1,0:T(4,128)}), f32[32,4,1024]{2,1,0:T(4,128)}, u32[]{:S(2)}, u32[]{:S(2)}) async-start(f32[32,4,1024]{2,1,0:T(4,128)} %copy.55), calls=%async_computation.3 | async-start | bytes 1048576 | tf_op jit(solution)/shard_map/all_to_all | solution.py:161
  136.4 0.3 fusion.6
  136.7 0.8 convolution_convert_fusion
  137.5 2.5 %copy.51 = bf16[32,512,64]{1,2,0:T(8,128)(2,1)} copy(bf16[32,512,64]{1,0,2:T(8,128)(2,1)S(1)} %convolution_convert_fusion) | data formatting | bytes 4194304 | tf_op jit(solution)/shard_map/convert_element_type | solution.py:171
  140.0 5.9 %all-to-all-done.2 = f32[32,4,1024]{2,1,0:T(4,128)} async-done(((f32[32,4,1024]{2,1,0:T(4,128)}), f32[32,4,1024]{2,1,0:T(4,128)}, u32[]{:S(2)}, u32[]{:S(2)}) %all-to-all-start.2) | async-done | bytes 524320 | tf_op jit(solution)/shard_map/all_to_all | solution.py:161
  145.9 7.0 %all-to-all-start.1 = ((bf16[32,512,64]{1,2,0:T(8,128)(2,1)}), bf16[32,512,64]{1,2,0:T(8,128)(2,1)}, u32[]{:S(2)}, u32[]{:S(2)}) async-start(bf16[32,512,64]{1,2,0:T(8,128)(2,1)} %copy.51), calls=%async_computation.2 | async-start | bytes 4194304 | tf_op jit(solution)/shard_map/all_to_all | solution.py:172
  152.9 0.9 reshape_reshape.6
  153.8 1.0 constant_dynamic-slice_fusion
  154.8 1.6 fusion.12
  156.4 2.3 %fusion = bf16[1024,512]{1,0:T(8,128)(2,1)} fusion(f32[8,128,512]{2,1,0:T(8,128)S(1)} %fusion.12, bf16[1024,1024]{1,0:T(8,128)(2,1)S(1)} %bitcast.52, bf16[512,1024]{1,0:T(8,128)(2,1)S(1)} %copy-done.6), kind=kOutput, calls=%fused_computation.4 | convolution fusion | flops 1074790400 | bytes 6291456 | tf_op jit(solution)/shard_map/nc,dc->nd/dot_general | solution.py:180
  158.7 1.6 convolution_convert_fusion.4
  160.4 0.6 reshape.118.refs_0_
  161.0 38.6 %shard_map.104 = bf16[16,32,1024]{2,1,0:T(8,128)(2,1)} custom-call(bf16[1,32,1024]{2,1,0:T(8,128)(2,1)} %reshape.118.refs_0_), custom_call_target="tpu_custom_call" | custom-call | bytes 2097152 | tf_op jit(solution)/shard_map/pallas_call | solution.py:74
  199.6 1.5 reshape.119
  201.1 0.4 copy.58
  201.5 1.1 reshape.120
  202.6 2.8 %fusion.3 = bf16[8,512,64]{1,0,2:T(8,128)(2,1)S(1)} fusion(bf16[32,512,64]{1,2,0:T(8,128)(2,1)} %all-to-all-done.1, s32[32]{0:T(128)S(1)} %fusion.22, pred[32]{0:T(512)(128)(4,1)S(1)} %get-tuple-element.28), kind=kOutput, calls=%fused_computation.10 | convolution fusion | flops 17039872 | bytes 2621600 | tf_op jit(solution)/shard_map/ra,rdk->adk/dot_general | solution.py:173
  205.5 1.0 copy.59
  206.4 1.8 fusion.7
  (31 shorter events, 0.7 us)
Async XLA Ops:
  7.2 61.9 %copy-start = (bf16[1024,512]{1,0:T(8,128)(2,1)S(1)}, bf16[1024,512]{1,0:T(8,128)(2,1)}, u32[]{:S(2)}) copy-start(bf16[1024,512]{1,0:T(8,128)(2,1)} %param.7) | copy-start | bytes 3145732
  16.9 55.4 %all-to-all-start = ((bf16[32,576,64]{1,2,0:T(8,128)(2,1)}), bf16[32,576,64]{1,2,0:T(8,128)(2,1)}, u32[]{:S(2)}, u32[]{:S(2)}) async-start(bf16[32,576,64]{1,2,0:T(8,128)(2,1)} %broadcast_select_fusion), calls=%async_computation | async-start | bytes 5242880 | tf_op jit(solution)/shard_map/all_to_all | solution.py:115
  27.0 42.0 %copy-start.5 = (bf16[512,1024]{1,0:T(8,128)(2,1)S(1)}, bf16[512,1024]{1,0:T(8,128)(2,1)}, u32[]{:S(2)}) copy-start(bf16[512,1024]{1,0:T(8,128)(2,1)} %param.8) | copy-start | bytes 3145732
  27.1 179.3 %reduce-scatter.2.cloned.1.call-start = ((), (), s32[]{:S(2)}) async-start(), calls=%async_computation.4 | async-start | bytes 4456448 | tf_op jit(solution)/shard_map/reduce_scatter | solution.py:136
  74.8 43.8 %copy-start.3 = (bf16[8,576,64]{1,2,0:T(8,128)(2,1)}, bf16[8,576,64]{1,2,0:T(8,128)(2,1)S(1)}, u32[]{:S(2)}) copy-start(bf16[8,576,64]{1,2,0:T(8,128)(2,1)S(1)} %broadcast_select_fusion.1) | copy-start | bytes 1769476
  118.7 1.2 slice-start
  120.3 1.0 copy-start.4
  120.3 4.0 %copy-start.1 = (bf16[16,96,1024]{2,1,0:T(8,128)(2,1)S(1)}, bf16[16,96,1024]{2,1,0:T(8,128)(2,1)}, u32[]{:S(2)}) copy-start(bf16[16,96,1024]{2,1,0:T(8,128)(2,1)} %shard_map.103) | copy-start | bytes 9437188
  124.3 1.6 copy-start.2
  129.0 16.9 %all-to-all-start.2 = ((f32[32,4,1024]{2,1,0:T(4,128)}), f32[32,4,1024]{2,1,0:T(4,128)}, u32[]{:S(2)}, u32[]{:S(2)}) async-start(f32[32,4,1024]{2,1,0:T(4,128)} %copy.55), calls=%async_computation.3 | async-start | bytes 1048576 | tf_op jit(solution)/shard_map/all_to_all | solution.py:161
  145.9 56.8 %all-to-all-start.1 = ((bf16[32,512,64]{1,2,0:T(8,128)(2,1)}), bf16[32,512,64]{1,2,0:T(8,128)(2,1)}, u32[]{:S(2)}, u32[]{:S(2)}) async-start(bf16[32,512,64]{1,2,0:T(8,128)(2,1)} %copy.51), calls=%async_computation.2 | async-start | bytes 4194304 | tf_op jit(solution)/shard_map/all_to_all | solution.py:172
  154.8 1.6 copy-start.6
Sparse Core Ops, SparseCore 0:
  118.8 78.7 reduce-scatter.1

commit v16 on v13

--- a/solution.py
+++ b/solution.py
@@ -131,7 +131,7 @@
     packed = jnp.concatenate(
         [down_part.reshape(down_rows, kv_full), panel_b_cols.reshape(-1, kv_full)], axis=0
     )
-    (parts,) = ring_gather([packed[None]], n_split, 1, pieces=6)
+    (parts,) = ring_gather([packed[None]], n_split, 1, pieces=2)
     partial_value, parts = lax.optimization_barrier((partial_value, parts))
     base = lax.psum_scatter(partial_value, "mp", scatter_dimension=0, tiled=True)
     down = jnp.sum(parts[:, :down_rows].astype(jnp.float32), axis=0)

time: 215 us -> 215 us (level)
  transfers between devices with their start and end apart: 4 -> 4, of which waited for: 1 -> 1; matrix products, arithmetic and copies ran while one was open for 14% -> 14% of each run, Pallas kernels for 37% -> 36%
where the time goes in v16:
time: 215 us; the launch traced here: 213 us
  Pallas kernels  121 us (56%)
  starting transfers between devices  24.5 us (11%)
  local copies, waits for them, and re-layouts  20.8 us (10%)
  matrix products  19.8 us (9%)
  between operations  14.4 us (7%)
  other arithmetic  7.19 us (3%)
  waiting for transfers between devices  5.89 us (3%)
    pallas_call x3, Pallas kernels, ring_gather(): pl.pallas_call(functools.partial(_ring_kernel, n, k, pieces), out_shape=o...  121 us
    all_to_all x1, starting transfers between devices, per_device(): lax.all_to_all(jnp.take(both, wanted, axis=0), 'dp', split_axis=0, concat...  10.1 us
    all_to_all x1, starting transfers between devices, per_device(): lax.all_to_all(send_gb, 'dp', split_axis=0, concat_axis=0, tiled=True)  7.36 us
    all_to_all x1, starting transfers between devices, per_device(): lax.all_to_all(send_ga, 'dp', split_axis=0, concat_axis=0, tiled=True)  6.99 us
    all_to_all x1, waiting for transfers between devices, per_device(): lax.all_to_all(send_gb, 'dp', split_axis=0, concat_axis=0, tiled=True)  5.87 us
  transfers between devices with their start and end apart: 4, of which 1 were waited for; matrix products, arithmetic and copies ran while one was open for 14% of the time, Pallas kernels for 36%

profile of v16, /device:TPU:24, one launch (start us, length us, event | category | flops | bytes accessed | tf_op | source)
XLA Modules:
  0.0 213.4 jit_solution(8278100994344587000)
XLA Ops:
  7.2 1.0 select_reduce_fusion
  8.2 0.1 fusion.44
  8.5 0.9 constant_dynamic-slice_fusion.1
  9.5 0.1 reshape.109
  9.6 0.1 copy.43
  9.8 1.1 pad_maximum_fusion
  10.9 2.4 %gather_fusion = bf16[32,576,64]{1,2,0:T(8,128)(2,1)} fusion(bf16[8,576,64]{1,2,0:T(8,128)(2,1)S(1)} %pad_maximum_fusion, s32[1024]{0:T(1024)S(1)} %pad_clamp_fusion.1), kind=kCustom, calls=%fused_computation | custom fusion | bytes 4718720 | tf_op jit(solution)/shard_map/jit(_take)/gather | solution.py:115
  13.3 3.6 %broadcast_select_fusion = bf16[32,576,64]{1,2,0:T(8,128)(2,1)} fusion(bf16[32,576,64]{1,2,0:T(8,128)(2,1)} %gather_fusion, pred[32]{0:T(512)(128)(4,1)S(1)} %compare_and_fusion), kind=kLoop, calls=%fused_computation.2 | loop fusion | flops 1179648 | bytes 4718624 | tf_op jit(solution)/shard_map/jit(_take)/select_n | solution.py:115
  16.9 10.1 %all-to-all-start = ((bf16[32,576,64]{1,2,0:T(8,128)(2,1)}), bf16[32,576,64]{1,2,0:T(8,128)(2,1)}, u32[]{:S(2)}, u32[]{:S(2)}) async-start(bf16[32,576,64]{1,2,0:T(8,128)(2,1)} %broadcast_select_fusion), calls=%async_computation | async-start | bytes 5242880 | tf_op jit(solution)/shard_map/all_to_all | solution.py:115
  27.1 40.9 %shard_map.102 = bf16[16,64,1024]{2,1,0:T(8,128)(2,1)} custom-call(bf16[1,64,1024]{2,1,0:T(8,128)(2,1)} %bitcast.56), custom_call_target="tpu_custom_call" | custom-call | bytes 4194304 | tf_op jit(solution)/shard_map/pallas_call | solution.py:74
  68.1 3.2 %fusion.46 = f32[1024,1024]{1,0:T(8,128)} fusion(bf16[1024,512]{1,0:T(8,128)(2,1)S(1)} %copy-done, bf16[512,1024]{1,0:T(8,128)(2,1)S(1)} %copy-done.5), kind=kOutput, calls=%fused_computation.75 | convolution fusion | flops 1073741824 | bytes 6291456 | tf_op jit(solution)/shard_map/dot_general | solution.py:126
  71.2 2.4 %gather_fusion.1 = bf16[8,576,64]{1,2,0:T(8,128)(2,1)S(1)} fusion(bf16[32,576,64]{1,2,0:T(8,128)(2,1)} %all-to-all-done, s32[1024]{0:T(1024)S(1)} %pad_clamp_fusion), kind=kCustom, calls=%fused_computation.1 | custom fusion | bytes 1179680 | tf_op jit(solution)/shard_map/jit(_take)/gather | solution.py:119
  73.7 0.1 broadcast_select_fusion.1
  74.0 0.1 reshape.112
  74.1 0.5 fusion.8
  74.6 0.2 copy.44
  74.8 0.2 reshape.111
  75.0 0.7 maximum_bitcast_fusion.refs_0_
  75.7 43.9 %shard_map.103 = bf16[16,96,1024]{2,1,0:T(8,128)(2,1)} custom-call(bf16[1,96,1024]{2,1,0:T(8,128)(2,1)} %maximum_bitcast_fusion.refs_0_), custom_call_target="tpu_custom_call" | custom-call | bytes 6291456 | tf_op jit(solution)/shard_map/pallas_call | solution.py:74
  119.7 1.2 slice-done
  120.9 0.4 reshape.113
  121.3 1.0 copy-done.4
  122.3 3.0 %convolution_convert_fusion.2 = bf16[8,128,16,4]{1,2,3,0:T(8,128)(2,1)S(1)} fusion(bf16[8,128,1024,1]{2,1,3,0:T(8,128)(2,1)} %bitcast.50, bf16[16,8,4,1024]{3,2,1,0:T(4,128)(2,1)S(1)} %reshape.113), kind=kOutput, calls=%fused_computation.14 | convolution fusion | flops 134283264 | bytes 3276800 | tf_op jit(solution)/shard_map/bnc,jbqc->bnjq/dot_general | solution.py:140
  125.3 0.3 slice_reduce_fusion
  125.7 0.9 reshape.117
  126.6 0.2 copy-done.2
  126.8 1.5 fusion.15
  128.3 0.5 fusion.17
  128.8 1.1 copy.55
  129.9 7.4 %all-to-all-start.2 = ((f32[32,4,1024]{2,1,0:T(4,128)}), f32[32,4,1024]{2,1,0:T(4,128)}, u32[]{:S(2)}, u32[]{:S(2)}) async-start(f32[32,4,1024]{2,1,0:T(4,128)} %copy.55), calls=%async_computation.3 | async-start | bytes 1048576 | tf_op jit(solution)/shard_map/all_to_all | solution.py:161
  137.3 0.3 fusion.6
  137.6 0.8 convolution_convert_fusion
  138.4 2.5 %copy.51 = bf16[32,512,64]{1,2,0:T(8,128)(2,1)} copy(bf16[32,512,64]{1,0,2:T(8,128)(2,1)S(1)} %convolution_convert_fusion) | data formatting | bytes 4194304 | tf_op jit(solution)/shard_map/convert_element_type | solution.py:171
  140.9 5.9 %all-to-all-done.2 = f32[32,4,1024]{2,1,0:T(4,128)} async-done(((f32[32,4,1024]{2,1,0:T(4,128)}), f32[32,4,1024]{2,1,0:T(4,128)}, u32[]{:S(2)}, u32[]{:S(2)}) %all-to-all-start.2) | async-done | bytes 524320 | tf_op jit(solution)/shard_map/all_to_all | solution.py:161
  146.8 7.0 %all-to-all-start.1 = ((bf16[32,512,64]{1,2,0:T(8,128)(2,1)}), bf16[32,512,64]{1,2,0:T(8,128)(2,1)}, u32[]{:S(2)}, u32[]{:S(2)}) async-start(bf16[32,512,64]{1,2,0:T(8,128)(2,1)} %copy.51), calls=%async_computation.2 | async-start | bytes 4194304 | tf_op jit(solution)/shard_map/all_to_all | solution.py:172
  153.8 0.9 reshape_reshape.6
  154.7 1.0 constant_dynamic-slice_fusion
  155.7 1.6 fusion.12
  157.3 2.3 %fusion = bf16[1024,512]{1,0:T(8,128)(2,1)} fusion(f32[8,128,512]{2,1,0:T(8,128)S(1)} %fusion.12, bf16[1024,1024]{1,0:T(8,128)(2,1)S(1)} %bitcast.52, bf16[512,1024]{1,0:T(8,128)(2,1)S(1)} %copy-done.6), kind=kOutput, calls=%fused_computation.4 | convolution fusion | flops 1074790400 | bytes 6291456 | tf_op jit(solution)/shard_map/nc,dc->nd/dot_general | solution.py:180
  159.6 1.6 convolution_convert_fusion.4
  161.3 0.6 reshape.118.refs_0_
  161.9 36.1 %shard_map.104 = bf16[16,32,1024]{2,1,0:T(8,128)(2,1)} custom-call(bf16[1,32,1024]{2,1,0:T(8,128)(2,1)} %reshape.118.refs_0_), custom_call_target="tpu_custom_call" | custom-call | bytes 2097152 | tf_op jit(solution)/shard_map/pallas_call | solution.py:74
  198.0 1.5 reshape.119
  199.4 0.4 copy.58
  199.9 1.1 reshape.120
  201.0 2.8 %fusion.3 = bf16[8,512,64]{1,0,2:T(8,128)(2,1)S(1)} fusion(bf16[32,512,64]{1,2,0:T(8,128)(2,1)} %all-to-all-done.1, s32[32]{0:T(128)S(1)} %fusion.22, pred[32]{0:T(512)(128)(4,1)S(1)} %get-tuple-element.28), kind=kOutput, calls=%fused_computation.10 | convolution fusion | flops 17039872 | bytes 2621600 | tf_op jit(solution)/shard_map/ra,rdk->adk/dot_general | solution.py:173
  203.8 1.0 copy.59
  204.8 1.8 fusion.7
  (31 shorter events, 0.7 us)
Async XLA Ops:
  7.2 60.9 %copy-start = (bf16[1024,512]{1,0:T(8,128)(2,1)S(1)}, bf16[1024,512]{1,0:T(8,128)(2,1)}, u32[]{:S(2)}) copy-start(bf16[1024,512]{1,0:T(8,128)(2,1)} %param.7) | copy-start | bytes 3145732
  16.9 54.3 %all-to-all-start = ((bf16[32,576,64]{1,2,0:T(8,128)(2,1)}), bf16[32,576,64]{1,2,0:T(8,128)(2,1)}, u32[]{:S(2)}, u32[]{:S(2)}) async-start(bf16[32,576,64]{1,2,0:T(8,128)(2,1)} %broadcast_select_fusion), calls=%async_computation | async-start | bytes 5242880 | tf_op jit(solution)/shard_map/all_to_all | solution.py:115
  27.0 41.0 %copy-start.5 = (bf16[512,1024]{1,0:T(8,128)(2,1)S(1)}, bf16[512,1024]{1,0:T(8,128)(2,1)}, u32[]{:S(2)}) copy-start(bf16[512,1024]{1,0:T(8,128)(2,1)} %param.8) | copy-start | bytes 3145732
  27.1 177.7 %reduce-scatter.2.cloned.1.call-start = ((), (), s32[]{:S(2)}) async-start(), calls=%async_computation.4 | async-start | bytes 4456448 | tf_op jit(solution)/shard_map/reduce_scatter | solution.py:136
  73.8 45.8 %copy-start.3 = (bf16[8,576,64]{1,2,0:T(8,128)(2,1)}, bf16[8,576,64]{1,2,0:T(8,128)(2,1)S(1)}, u32[]{:S(2)}) copy-start(bf16[8,576,64]{1,2,0:T(8,128)(2,1)S(1)} %broadcast_select_fusion.1) | copy-start | bytes 1769476
  119.6 1.2 slice-start
  121.3 1.0 copy-start.4
  121.3 4.0 %copy-start.1 = (bf16[16,96,1024]{2,1,0:T(8,128)(2,1)S(1)}, bf16[16,96,1024]{2,1,0:T(8,128)(2,1)}, u32[]{:S(2)}) copy-start(bf16[16,96,1024]{2,1,0:T(8,128)(2,1)} %shard_map.103) | copy-start | bytes 9437188
  125.2 1.6 copy-start.2
  129.9 16.9 %all-to-all-start.2 = ((f32[32,4,1024]{2,1,0:T(4,128)}), f32[32,4,1024]{2,1,0:T(4,128)}, u32[]{:S(2)}, u32[]{:S(2)}) async-start(f32[32,4,1024]{2,1,0:T(4,128)} %copy.55), calls=%async_computation.3 | async-start | bytes 1048576 | tf_op jit(solution)/shard_map/all_to_all | solution.py:161
  146.8 54.2 %all-to-all-start.1 = ((bf16[32,512,64]{1,2,0:T(8,128)(2,1)}), bf16[32,512,64]{1,2,0:T(8,128)(2,1)}, u32[]{:S(2)}, u32[]{:S(2)}) async-start(bf16[32,512,64]{1,2,0:T(8,128)(2,1)} %copy.51), calls=%async_computation.2 | async-start | bytes 4194304 | tf_op jit(solution)/shard_map/all_to_all | solution.py:172
  155.7 1.6 copy-start.6
Sparse Core Ops, SparseCore 0:
  119.8 79.9 reduce-scatter.1
